TPU v7x, 32 devices: a whole 2x2x4 slice. The times are simulated.
32 devices in a mesh: fish: 2 (over y), img: 16 (over z, x, core).
Axes of the slice: x: 2, y: 2, z: 4, core: 2. Of those that a mesh axis runs over, the one named last changes fastest.
Arguments:
- img_feat: bfloat16 [64, 16384], P(None, ('fish', 'img')), parts along dimension 1, may hold values from -80 to 80
- mdl_feat: bfloat16 [64, 2048], P(None, ('fish', 'img')), parts along dimension 1, may hold values from -80 to 80
- img_mass: float32 [16384], P(('fish', 'img')), parts along dimension 0, may hold values from 0.5 to 2
- mdl_mass: float32 [2048], P('fish'), parts along dimension 0, may hold values from 0.5 to 2
Outputs:
- grad_img: float32 [64, 16384], P(None, ('fish', 'img')), parts along dimension 1
- grad_mdl: float32 [64, 2048], P(None, ('fish', 'img')), parts along dimension 1
There are 2 independent parts, one for each index of `fish`. A program takes and returns all parts, laid end to end along the dimension named above; each array names one. Nothing has to cross between parts.
All inputs are finite; a program needn't handle non-finite values.
Results may differ from a plain program's by a relative error of at most 0.005.
Values may be sent and summed in bfloat16 or wider, within the bound.
No kernel may reach another device: no remote copies, remote signals or barrier semaphores. Data moves between devices by JAX's collectives and lax.ppermute only.
A program may use at most 64 MiB of HBM per device.

v0:
```python
import jax
import jax.numpy as jnp
from jax import lax
from jax.sharding import PartitionSpec as P

FEAT = 64
ITERS = 4


inv_temp = 20.0


def normalize(features):
    wide = features.astype(jnp.float32)
    guarded = jnp.mean(wide * wide, axis=0, keepdims=True) + 1e-06
    return (wide * lax.rsqrt(guarded)).astype(jnp.bfloat16)


def kernel_tile(imaged_unit, model_slice, factor):
    scores = lax.dot_general(
        imaged_unit, model_slice, (((0,), (0,)), ((), ())), preferred_element_type=jnp.float32
    )
    return jnp.exp(scores * factor).astype(jnp.bfloat16)


def shards(img_feat, mdl_feat, img_mass, mdl_mass):
    factor = inv_temp / FEAT
    imaged_unit = normalize(img_feat)
    model_unit = lax.all_gather(normalize(mdl_feat), "img", axis=1, tiled=True)
    total_model = model_unit.shape[1]
    share = mdl_feat.shape[1]
    local_rows = img_feat.shape[1]
    offset = lax.axis_index("img") * share
    kernel = kernel_tile(imaged_unit, model_unit, factor)
    col_scale = jnp.ones((total_model,), jnp.float32)
    col_low = col_scale.astype(jnp.bfloat16)
    row_scale = jnp.ones((local_rows,), jnp.float32)
    for iteration in range(ITERS):
        row_scale = img_mass / jnp.dot(kernel, col_low, preferred_element_type=jnp.float32)
        partial_cols = jnp.dot(
            row_scale.astype(jnp.bfloat16), kernel, preferred_element_type=jnp.float32
        )
        col_scale = mdl_mass / lax.psum(partial_cols, "img")
        col_low = col_scale.astype(jnp.bfloat16)
    weighted = (model_unit.astype(jnp.float32) * col_scale[None, :]).astype(jnp.bfloat16)
    grad_img = -(
        lax.dot_general(
            weighted, kernel, (((1,), (1,)), ((), ())), preferred_element_type=jnp.float32
        )
        * row_scale[None, :]
    )
    row_feat = (imaged_unit.astype(jnp.float32) * row_scale[None, :]).astype(jnp.bfloat16)
    summed = lax.psum_scatter(
        lax.dot_general(
            kernel, row_feat, (((0,), (1,)), ((), ())), preferred_element_type=jnp.float32
        ),
        "img",
        scatter_dimension=0,
        tiled=True,
    )
    own_scale = lax.dynamic_slice_in_dim(col_scale, offset, share, 0)
    grad_mdl = -(summed * own_scale[:, None]).T
    return (grad_img, grad_mdl)


def solution(mesh):
    placed = (P(None, ("fish", "img")), P(None, ("fish", "img")), P(("fish", "img")), P("fish"))
    return jax.shard_map(
        shards,
        mesh=mesh,
        in_specs=placed,
        out_specs=(P(None, ("fish", "img")), P(None, ("fish", "img"))),
        check_vma=False,
    )
```

profile of v0, /device:TPU:0, one launch (start us, length us, event | category | flops | bytes accessed | tf_op | source)
XLA Modules:
  0.0 188.4 jit_solution(11212692938415362139)
XLA Ops:
  7.2 0.0 reduce-scatter.2.cloned.1.call-start
  7.2 0.8 copy.7
  8.0 0.1 fusion.8
  8.1 0.1 fusion.9
  8.2 23.8 %all_gather.3 = bf16[64,1024]{0,1:T(8,128)(2,1)S(1)} all-gather(bf16[64,64]{0,1:T(8,128)(2,1)S(1)} %fusion.9), channel_id=1, replica_groups=mesh['fish'=2,'img'=16] {'img'}, dimensions={1}, use_global_device_ids=true | all-gather | bytes 139264 | tf_op jit(solution)/shard_map/all_gather | solution.py:29
  32.0 0.9 fusion.2
  32.9 0.0 copy-start.2
  32.9 1.3 exponential_convert_fusion
  34.2 0.0 copy-start.1
  34.2 0.4 fusion.10
  34.6 0.0 copy-done.2
  34.7 0.2 fusion.14
  34.9 29.8 %psum.28 = f32[1024]{0:T(1024)S(1)} all-reduce(f32[1024]{0:T(1024)S(1)} %bitcast.28), channel_id=1, replica_groups=mesh['fish'=2,'img'=16] {'img'}, use_global_device_ids=true, to_apply=%region_2.0 | all-reduce | flops 1024 | bytes 8192 | tf_op jit(solution)/shard_map/psum | solution.py:43
  64.7 0.0 copy-done.1
  64.7 0.4 fusion.15
  65.1 0.3 fusion.16
  65.4 29.5 %psum.29 = f32[1024]{0:T(1024)S(1)} all-reduce(f32[1024]{0:T(1024)S(1)} %bitcast.29), channel_id=1, replica_groups=mesh['fish'=2,'img'=16] {'img'}, use_global_device_ids=true, to_apply=%region_3.0 | all-reduce | flops 1024 | bytes 8192 | tf_op jit(solution)/shard_map/psum | solution.py:43
  94.9 0.4 fusion.17
  95.3 0.0 copy-start
  95.3 0.2 fusion.18
  95.5 29.5 %psum.30 = f32[1024]{0:T(1024)S(1)} all-reduce(f32[1024]{0:T(1024)S(1)} %bitcast.30), channel_id=1, replica_groups=mesh['fish'=2,'img'=16] {'img'}, use_global_device_ids=true, to_apply=%region_4.0 | all-reduce | flops 1024 | bytes 8192 | tf_op jit(solution)/shard_map/psum | solution.py:43
  125.0 0.4 fusion.19
  125.4 0.0 copy-done
  125.4 1.3 fusion.4
  126.7 0.0 reduce-scatter.2.cloned.1.call-update
  126.7 0.2 fusion.20
  127.0 29.5 %psum.31 = f32[1024]{0:T(1024)S(1)} all-reduce(f32[1024]{0:T(1024)S(1)} %bitcast.31), channel_id=1, replica_groups=mesh['fish'=2,'img'=16] {'img'}, use_global_device_ids=true, to_apply=%region_5.0 | all-reduce | flops 1024 | bytes 8192 | tf_op jit(solution)/shard_map/psum | solution.py:43
  156.5 0.1 dynamic_slice.3
  156.6 1.3 fusion
  157.9 22.0 %reduce-scatter.2.cloned.1.call-done = f32[64,64]{1,0:T(8,128)} async-done(((f32[1024,64]{1,0:T(8,128)}), f32[64,64]{1,0:T(8,128)}) %reduce-scatter.2.cloned.1.call-update) | async-done | bytes 16400 | tf_op jit(solution)/shard_map/reduce_scatter | solution.py:53
  180.0 0.8 negate_bitcast_fusion
  180.8 0.7 copy.8
  (17 shorter events, 0.1 us)
Async XLA Ops:
  7.2 172.8 %reduce-scatter.2.cloned.1.call-start = ((), (), s32[]{:S(2)}) async-start(), calls=%async_computation.1 | async-start | bytes 557056 | tf_op jit(solution)/shard_map/reduce_scatter | solution.py:53
  32.9 1.7 copy-start.2
  34.2 30.5 %copy-start.1 = (f32[1024]{0:T(1024)S(1)}, f32[1024]{0:T(1024)}, u32[]{:S(2)}) copy-start(f32[1024]{0:T(1024)} %param.7) | copy-start | bytes 12292
  95.3 30.1 %copy-start = (bf16[64,512]{1,0:T(8,128)(2,1)S(1)}, bf16[64,512]{1,0:T(8,128)(2,1)}, u32[]{:S(2)}) copy-start(bf16[64,512]{1,0:T(8,128)(2,1)} %param.4) | copy-start | bytes 196612
Sparse Core Ops, SparseCore 0:
  126.9 53.0 reduce-scatter.1
where the time goes:
time: 189 us; the launch traced here: 188 us
  blocking collectives  142 us (75%)
  waiting for transfers between devices  22.1 us (12%)
  between operations  14.1 us (7%)
  matrix products  6.44 us (3%)
  other arithmetic  1.98 us (1%)
    psum x4, blocking collectives, shards(): col_scale = mdl_mass / lax.psum(partial_cols, 'img')  118 us
    all_gather x1, blocking collectives, shards(): model_unit = lax.all_gather(normalize(mdl_feat), 'img', axis=1, tiled=True)  23.8 us
    reduce_scatter x1, waiting for transfers between devices, shards(): lax.psum_scatter(lax.dot_general(kernel, row_feat, (((0,), (1,)), ((), ()...  22 us
  transfers between devices with their start and end apart: 1, of which 1 were waited for; matrix products, arithmetic and copies ran while one was open for 1% of the time, Pallas kernels for 0%

commit v1 on v0

v1 whole, which is shorter than its diff:
```python
import jax
import jax.numpy as jnp
from jax import lax
from jax.sharding import PartitionSpec as P

FEAT = 64
ITERS = 4


inv_temp = 20.0


def normalize(features):
    wide = features.astype(jnp.float32)
    guarded = jnp.mean(wide * wide, axis=0, keepdims=True) + 1e-06
    return (wide * lax.rsqrt(guarded)).astype(jnp.bfloat16)


def everyone(block, count):
    copies = jnp.broadcast_to(block, (count,) + block.shape)
    return lax.all_to_all(copies, "img", 0, 0)


def shards(count, img_feat, mdl_feat, img_mass, mdl_mass):
    factor = inv_temp / FEAT
    share = mdl_feat.shape[1]
    local_rows = img_feat.shape[1]
    imaged_unit = normalize(img_feat)
    blocks = everyone(normalize(mdl_feat), count)
    model_unit = blocks.transpose(1, 0, 2).reshape(FEAT, count * share)
    scores = lax.dot_general(
        imaged_unit, model_unit, (((0,), (0,)), ((), ())), preferred_element_type=jnp.float32
    )
    kernel = jnp.exp(scores * factor).astype(jnp.bfloat16)
    col_scale = jnp.ones((count * share,), jnp.float32)
    col_low = col_scale.astype(jnp.bfloat16)
    row_scale = jnp.ones((local_rows,), jnp.float32)
    for iteration in range(ITERS):
        row_scale = img_mass / jnp.dot(kernel, col_low, preferred_element_type=jnp.float32)
        partial_cols = jnp.dot(
            row_scale.astype(jnp.bfloat16), kernel, preferred_element_type=jnp.float32
        )
        col_scale = mdl_mass / jnp.sum(everyone(partial_cols, count), axis=0)
        col_low = col_scale.astype(jnp.bfloat16)
    weighted = (model_unit.astype(jnp.float32) * col_scale[None, :]).astype(jnp.bfloat16)
    grad_img = -(
        lax.dot_general(
            weighted, kernel, (((1,), (1,)), ((), ())), preferred_element_type=jnp.float32
        )
        * row_scale[None, :]
    )
    row_feat = (imaged_unit.astype(jnp.float32) * row_scale[None, :]).astype(jnp.bfloat16)
    terms = lax.dot_general(
        row_feat, kernel, (((1,), (0,)), ((), ())), preferred_element_type=jnp.float32
    )
    terms = terms.reshape(FEAT, count, share).transpose(1, 0, 2)
    summed = jnp.sum(lax.all_to_all(terms, "img", 0, 0), axis=0)
    offset = lax.axis_index("img") * share
    own_scale = lax.dynamic_slice_in_dim(col_scale, offset, share, 0)
    grad_mdl = -(summed * own_scale[None, :])
    return (grad_img, grad_mdl)


def solution(mesh):
    count = mesh.shape["img"]
    placed = (P(None, ("fish", "img")), P(None, ("fish", "img")), P(("fish", "img")), P("fish"))
    return jax.shard_map(
        lambda *args: shards(count, *args),
        mesh=mesh,
        in_specs=placed,
        out_specs=(P(None, ("fish", "img")), P(None, ("fish", "img"))),
        check_vma=False,
    )
```

time: 189 us -> 78.9 us (0.42)
  blocking collectives: 142 us -> 28.4 us
  starting transfers between devices: 0.04 us -> 14.4 us
  between operations: 14.1 us -> 0.89 us
  local copies, waits for them, and re-layouts: 1.66 us -> 4.51 us
  other arithmetic: 1.98 us -> 4.57 us
  matrix products: 6.44 us -> 4.36 us
    psum x4 -> x0, blocking collectives: 118 us -> none  [shards(): col_scale = mdl_mass / lax.psum(partial_cols, 'img')]
    all_to_all x0 -> x3, blocking collectives: none -> 28.4 us  [everyone(): return lax.all_to_all(copies, 'img', 0, 0)]
    all_gather x1 -> x0, blocking collectives: 23.8 us -> none  [shards(): model_unit = lax.all_gather(normalize(mdl_feat), 'img', axis=1, tiled=True)]
    reduce_scatter x1 -> x0, waiting for transfers between devices: 22 us -> none  [shards(): lax.psum_scatter(lax.dot_general(kernel, row_feat, (((0,), (1,)), ((), ()...]
    all_to_all x0 -> x3, waiting for transfers between devices: none -> 21 us  [the longest x2 12.3 us: everyone(): return lax.all_to_all(copies, 'img', 0, 0)]
    all_to_all x0 -> x3, starting transfers between devices: none -> 14.4 us  [the longest x2 10.9 us: everyone(): return lax.all_to_all(copies, 'img', 0, 0)]
  transfers between devices with their start and end apart: 1 -> 3, of which waited for: 1 -> 3; matrix products, arithmetic and copies ran while one was open for 1% -> 5% of each run, Pallas kernels for 0% -> 0%
where the time goes in v1:
time: 78.9 us; the launch traced here: 78.2 us
  blocking collectives  28.4 us (36%)
  waiting for transfers between devices  21 us (27%)
  starting transfers between devices  14.4 us (18%)
  other arithmetic  4.57 us (6%)
  local copies, waits for them, and re-layouts  4.51 us (6%)
  matrix products  4.36 us (6%)
  between operations  0.89 us (1%)
    all_to_all x3, blocking collectives, everyone(): return lax.all_to_all(copies, 'img', 0, 0)  28.4 us
    all_to_all x2, waiting for transfers between devices, everyone(): return lax.all_to_all(copies, 'img', 0, 0)  12.3 us
    all_to_all x2, starting transfers between devices, everyone(): return lax.all_to_all(copies, 'img', 0, 0)  10.9 us
    all_to_all x1, waiting for transfers between devices, shards(): summed = jnp.sum(lax.all_to_all(terms, 'img', 0, 0), axis=0)  8.75 us
    all_to_all x1, starting transfers between devices, shards(): summed = jnp.sum(lax.all_to_all(terms, 'img', 0, 0), axis=0)  3.53 us
    unnamed x10, local copies, waits for them, and re-layouts  2.35 us
    reduce_sum x2, other arithmetic, normalize(): guarded = jnp.mean(wide * wide, axis=0, keepdims=True) + 1e-06  1.62 us
  transfers between devices with their start and end apart: 3, of which 3 were waited for; matrix products, arithmetic and copies ran while one was open for 5% of the time, Pallas kernels for 0%

profile of v1, /device:TPU:0, one launch (start us, length us, event | category | flops | bytes accessed | tf_op | source)
XLA Modules:
  0.0 78.2 jit_solution(4362737281040332837)
XLA Ops:
  0.6 0.7 fusion.8
  1.4 0.7 fusion.9
  2.2 0.0 copy-start
  2.2 0.9 %reshape.63 = bf16[16,2,2048]{2,1,0:T(2,128)(2,1)} reshape(bf16[16,64,64]{2,1,0:T(8,128)(2,1)S(1)} %broadcast_in_dim.10) | data formatting | bytes 262144
  3.1 7.4 %all-to-all-start = ((bf16[16,2,2048]{2,1,0:T(2,128)(2,1)}), bf16[16,2,2048]{2,1,0:T(2,128)(2,1)S(1)}, u32[]{:S(2)}, u32[]{:S(2)}) async-start(bf16[16,2,2048]{2,1,0:T(2,128)(2,1)} %reshape.63), calls=%async_computation | async-start | bytes 262144 | tf_op jit(solution)/shard_map/all_to_all | solution.py:21
  10.4 0.9 %fusion.1 = f32[512]{0:T(512)S(1)} fusion(bf16[64,512]{1,0:T(8,128)(2,1)} %param.4), kind=kLoop, calls=%fused_computation.7 | loop fusion | flops 97792 | bytes 67584 | tf_op jit(solution)/shard_map/reduce_sum | solution.py:15
  11.3 7.1 %all-to-all-done = bf16[16,2,2048]{2,1,0:T(2,128)(2,1)S(1)} async-done(((bf16[16,2,2048]{2,1,0:T(2,128)(2,1)}), bf16[16,2,2048]{2,1,0:T(2,128)(2,1)S(1)}, u32[]{:S(2)}, u32[]{:S(2)}) %all-to-all-start) | async-done | bytes 131104 | tf_op jit(solution)/shard_map/all_to_all | solution.py:21
  18.4 0.2 reshape.64
  18.6 0.2 copy.10
  18.8 0.2 reshape.45
  19.0 0.0 copy-done
  19.0 0.0 copy-start.2
  19.0 0.5 exponential_convert_fusion
  19.5 0.0 copy-start.1
  19.5 0.4 fusion.10
  19.8 0.0 copy-done.2
  19.9 0.2 fusion.14
  20.2 9.5 %all_to_all.34 = f32[16,1,1024]{2,1,0:T(1,128)S(1)} all-to-all(f32[16,1,1024]{2,1,0:T(1,128)S(1)} %broadcast_in_dim.22), channel_id=1, replica_groups=mesh['fish'=2,'img'=16] {'img'}, dimensions={0} | all-to-all | bytes 131072 | tf_op jit(solution)/shard_map/all_to_all | solution.py:21
  29.7 0.1 reduce_sum.65
  29.7 0.0 copy-done.1
  29.7 0.4 fusion.15
  30.1 0.3 fusion.16
  30.4 9.5 %all_to_all.35 = f32[16,1,1024]{2,1,0:T(1,128)S(1)} all-to-all(f32[16,1,1024]{2,1,0:T(1,128)S(1)} %broadcast_in_dim.23), channel_id=1, replica_groups=mesh['fish'=2,'img'=16] {'img'}, dimensions={0} | all-to-all | bytes 131072 | tf_op jit(solution)/shard_map/all_to_all | solution.py:21
  39.9 0.1 reduce_sum.66
  40.0 0.4 fusion.17
  40.4 0.3 fusion.18
  40.7 9.5 %all_to_all.36 = f32[16,1,1024]{2,1,0:T(1,128)S(1)} all-to-all(f32[16,1,1024]{2,1,0:T(1,128)S(1)} %broadcast_in_dim.24), channel_id=1, replica_groups=mesh['fish'=2,'img'=16] {'img'}, dimensions={0} | all-to-all | bytes 131072 | tf_op jit(solution)/shard_map/all_to_all | solution.py:21
  50.2 0.1 reduce_sum.67
  50.3 0.4 fusion.19
  50.7 0.3 fusion.20
  50.9 0.7 broadcast_in_dim.25
  51.6 3.5 %all-to-all-start.4 = ((f32[16,1,1024]{2,1,0:T(1,128)}), f32[16,1,1024]{2,1,0:T(1,128)S(1)}, u32[]{:S(2)}, u32[]{:S(2)}) async-start(f32[16,1,1024]{2,1,0:T(1,128)} %broadcast_in_dim.25), calls=%async_computation.4 | async-start | bytes 131072 | tf_op jit(solution)/shard_map/all_to_all | solution.py:21
  55.1 0.3 fusion.4
  55.4 0.1 reshape.46
  55.5 0.2 copy.21
  55.7 1.0 %reshape.65 = f32[16,1,4096]{2,1,0:T(1,128)} reshape(f32[16,64,64]{2,1,0:T(8,128)S(1)} %bitcast.30) | data formatting | bytes 524288
  56.7 5.2 %all-to-all-done.4 = f32[16,1,1024]{2,1,0:T(1,128)S(1)} async-done(((f32[16,1,1024]{2,1,0:T(1,128)}), f32[16,1,1024]{2,1,0:T(1,128)S(1)}, u32[]{:S(2)}, u32[]{:S(2)}) %all-to-all-start.4) | async-done | bytes 65568 | tf_op jit(solution)/shard_map/all_to_all | solution.py:21
  62.0 3.5 %all-to-all-start.5 = ((f32[16,1,4096]{2,1,0:T(1,128)}), f32[16,1,4096]{2,1,0:T(1,128)S(1)}, u32[]{:S(2)}, u32[]{:S(2)}) async-start(f32[16,1,4096]{2,1,0:T(1,128)} %reshape.65), calls=%async_computation.5 | async-start | bytes 524288 | tf_op jit(solution)/shard_map/all_to_all | solution.py:57
  65.5 0.1 reduce_sum.68
  65.6 0.1 dynamic_slice.3
  65.7 1.1 %fusion = f32[64,512]{1,0:T(8,128)} fusion(bf16[512,1024]{1,0:T(8,128)(2,1)S(1)} %exponential_convert_fusion, bf16[64,1024]{1,0:T(8,128)(2,1)S(1)} %reshape.45, f32[1024]{0:T(1024)S(1)} %div.47, f32[512]{0:T(512)S(1)} %get-tuple-element.3), kind=kOutput, calls=%fused_computation.2 | convolution fusion | flops 67371008 | bytes 1316864 | tf_op jit(solution)/shard_map/dot_general | solution.py:47
  66.8 8.7 %all-to-all-done.5 = f32[16,1,4096]{2,1,0:T(1,128)S(1)} async-done(((f32[16,1,4096]{2,1,0:T(1,128)}), f32[16,1,4096]{2,1,0:T(1,128)S(1)}, u32[]{:S(2)}, u32[]{:S(2)}) %all-to-all-start.5) | async-done | bytes 262176 | tf_op jit(solution)/shard_map/all_to_all | solution.py:57
  75.5 0.5 broadcast.41
  76.0 1.3 %reduce.4 = f32[16,4096]{1,0:T(8,128)S(1)} reduce(f32[16,1,4096]{2,1,0:T(1,128)S(1)} %all-to-all-done.5, f32[]{:T(128)} %broadcast.41), dimensions={1}, to_apply=%all_to_all.27.reduce_sub_computation | reduce | bytes 524292 | tf_op jit(solution)/shard_map/all_to_all | solution.py:57
  77.3 0.2 reshape.66
  77.6 0.6 multiply_negate_fusion
  (22 shorter events, 0.3 us)
Async XLA Ops:
  2.2 16.8 %copy-start = (bf16[64,512]{1,0:T(8,128)(2,1)S(1)}, bf16[64,512]{1,0:T(8,128)(2,1)}, u32[]{:S(2)}) copy-start(bf16[64,512]{1,0:T(8,128)(2,1)} %param.4) | copy-start | bytes 196612
  3.1 15.3 %all-to-all-start = ((bf16[16,2,2048]{2,1,0:T(2,128)(2,1)}), bf16[16,2,2048]{2,1,0:T(2,128)(2,1)S(1)}, u32[]{:S(2)}, u32[]{:S(2)}) async-start(bf16[16,2,2048]{2,1,0:T(2,128)(2,1)} %reshape.63), calls=%async_computation | async-start | bytes 262144 | tf_op jit(solution)/shard_map/all_to_all | solution.py:21
  19.0 0.9 %copy-start.2 = (f32[512]{0:T(512)S(1)}, f32[512]{0:T(512)}, u32[]{:S(2)}) copy-start(f32[512]{0:T(512)} %param.6) | copy-start | bytes 6148
  19.5 10.2 %copy-start.1 = (f32[1024]{0:T(1024)S(1)}, f32[1024]{0:T(1024)}, u32[]{:S(2)}) copy-start(f32[1024]{0:T(1024)} %param.7) | copy-start | bytes 12292
  51.6 10.4 %all-to-all-start.4 = ((f32[16,1,1024]{2,1,0:T(1,128)}), f32[16,1,1024]{2,1,0:T(1,128)S(1)}, u32[]{:S(2)}, u32[]{:S(2)}) async-start(f32[16,1,1024]{2,1,0:T(1,128)} %broadcast_in_dim.25), calls=%async_computation.4 | async-start | bytes 131072 | tf_op jit(solution)/shard_map/all_to_all | solution.py:21
  62.0 13.5 %all-to-all-start.5 = ((f32[16,1,4096]{2,1,0:T(1,128)}), f32[16,1,4096]{2,1,0:T(1,128)S(1)}, u32[]{:S(2)}, u32[]{:S(2)}) async-start(f32[16,1,4096]{2,1,0:T(1,128)} %reshape.65), calls=%async_computation.5 | async-start | bytes 524288 | tf_op jit(solution)/shard_map/all_to_all | solution.py:57

commit v2 on v0

v2 whole, which is shorter than its diff:
```python
import functools
import jax
import jax.numpy as jnp
from jax import lax
from jax.experimental import pallas as pl
from jax.experimental.pallas import tpu as pltpu
from jax.sharding import PartitionSpec as P

FEAT = 64
ITERS = 4
LANES = 128
BF16 = jnp.bfloat16
F32 = jnp.float32

inv_temp = 20.0

RESIDENT = 24 << 20
GRANT = 12 << 20
WHOLE = pl.BlockSpec(memory_space=pltpu.VMEM)


def call(body, outs, *args):
    return pl.pallas_call(
        body,
        out_shape=outs,
        in_specs=[WHOLE] * len(args),
        out_specs=jax.tree.map(lambda _: WHOLE, outs),
        compiler_params=pltpu.CompilerParams(vmem_limit_bytes=GRANT),
    )(*args)


def shape(*dims, dtype=F32):
    return jax.ShapeDtypeStruct(dims, dtype)


def normalize(features):
    wide = features.astype(F32)
    guarded = jnp.mean(wide * wide, axis=0, keepdims=True) + 1e-06
    return (wide * lax.rsqrt(guarded)).astype(BF16)


def matmul(left, right):
    return lax.dot_general(left, right, (((1,), (0,)), ((), ())), preferred_element_type=F32)


def slots_of(groups):
    far = [s for s in range(2, groups, 2)]
    return [0, 1] + far + [s ^ 1 for s in far]


def pack(img_ref, mdl_ref, mass_ref, out_ref):
    rows = img_ref.shape[1]
    chunks = rows // LANES
    out_ref[:, :rows] = normalize(img_ref[...])
    unit = normalize(mdl_ref[...]).astype(F32)
    half = FEAT // 2
    share = unit.shape[1]
    out_ref[:half, rows : rows + share] = unit[:half].astype(BF16)
    out_ref[:half, rows + share :] = unit[half:].astype(BF16)
    mass = mass_ref[...]
    high = mass.astype(BF16)
    rest = mass - high.astype(F32)
    middle = rest.astype(BF16)
    low = (rest - middle.astype(F32)).astype(BF16)
    terms = [t.astype(F32) for t in (high, middle, low)]
    spare = half - 3 * chunks
    terms = jnp.concatenate(terms + [jnp.zeros((spare, LANES), F32)], axis=0)
    out_ref[half:, rows:] = terms.astype(BF16)


def collect(rows, own_ref, near_ref, far_ref, cross_ref, out_ref):
    half = FEAT // 2
    count = far_ref.shape[0] // FEAT
    places = [(own_ref, 0), (near_ref, 0)]
    places += [(far_ref, k) for k in range(count)] + [(cross_ref, k) for k in range(count)]
    for slot, (ref, k) in enumerate(places):
        out_ref[slot * half : (slot + 1) * half, :] = ref[k * FEAT : k * FEAT + half, rows:]


def build(
    groups,
    rows,
    own_ref,
    near_ref,
    far_ref,
    cross_ref,
    mine_ref,
    other_ref,
    mdl_mass_ref,
    kernel_ref,
    turned_ref,
    img_ref,
    mdl_ref,
    mass_ref,
    cols_mass_ref,
    sums_ref,
):
    half = FEAT // 2
    chunks = rows // LANES
    count = far_ref.shape[0] // FEAT
    place = lax.axis_index("img")
    group = place // 2
    first = place % 2 == 0
    places = [(own_ref, 0), (near_ref, 0)]
    places += [(far_ref, k) for k in range(count)] + [(cross_ref, k) for k in range(count)]
    low_lanes = lax.broadcasted_iota(jnp.int32, (FEAT, LANES), 1) < LANES // 2
    for slot, (distance, (ref, k)) in enumerate(zip(slots_of(groups), places)):
        part = ref.at[k * FEAT : (k + 1) * FEAT, :]
        img_ref[:, slot * rows : (slot + 1) * rows] = part[:, :rows]
        terms = part[half:, rows:].astype(F32)
        mass = terms[:chunks] + terms[chunks : 2 * chunks] + terms[2 * chunks : 3 * chunks]
        for j in range(chunks):
            at = slot * rows + j * LANES
            mass_ref[:, at : at + LANES] = mass[j : j + 1]
        sides = []
        for side in (mine_ref, other_ref):
            both = side[slot * half : (slot + 1) * half, :].astype(F32)
            sides.append(jnp.concatenate([both, pltpu.roll(both, LANES // 2, 1)], axis=0))
        left = jnp.where(first, sides[0], sides[1])
        right = jnp.where(first, sides[1], sides[0])
        pair = jnp.where(low_lanes, left, pltpu.roll(right, LANES // 2, 1))
        mdl_ref[:, slot * LANES : (slot + 1) * LANES] = pair.astype(BF16)
        cols_mass_ref[:, slot * LANES : (slot + 1) * LANES] = mdl_mass_ref[
            pl.ds(jnp.bitwise_xor(group, distance), 1), :
        ]

    models = mdl_ref.shape[1]
    sums_ref[...] = jnp.zeros_like(sums_ref)
    ones = jnp.ones((8, models), BF16)

    def block(index, carry):
        at = pl.ds(pl.multiple_of(index * rows, rows), rows)
        scores = lax.dot_general(
            img_ref[:, at], mdl_ref[...], (((0,), (0,)), ((), ())), preferred_element_type=F32
        )
        tile = jnp.exp(scores * (inv_temp / FEAT)).astype(BF16)
        kernel_ref[at, :] = tile
        turned_ref[:, at] = tile.T
        row_sums = matmul(ones, turned_ref[:, at])
        row_scale = mass_ref[:, at] / row_sums
        sums_ref[...] += matmul(row_scale.astype(BF16), kernel_ref[at, :])[:1]
        return carry

    lax.fori_loop(0, groups, block, 0)


def scaled(mine_ref, other_ref, cols_mass_ref):
    return cols_mass_ref[...] / (mine_ref[...] + other_ref[...])


def row_scales(col_scale, mass_ref, turned_ref):
    low = jnp.broadcast_to(col_scale.astype(BF16), (8, col_scale.shape[1]))
    return mass_ref[...] / matmul(low, turned_ref[...])


def iterate(mine_ref, other_ref, cols_mass_ref, mass_ref, kernel_ref, turned_ref, out_ref):
    col_scale = scaled(mine_ref, other_ref, cols_mass_ref)
    row_scale = row_scales(col_scale, mass_ref, turned_ref)
    out_ref[...] = matmul(row_scale.astype(BF16), kernel_ref[...])[:1]


def last(
    rows,
    mine_ref,
    other_ref,
    cols_mass_ref,
    mass_ref,
    kernel_ref,
    turned_ref,
    img_ref,
    out_ref,
    scale_ref,
):
    col_scale = scaled(mine_ref, other_ref, cols_mass_ref)
    row_scale = row_scales(col_scale, mass_ref, turned_ref)
    scale_ref[...] = row_scale[:1, :rows]
    sums = matmul(row_scale.astype(BF16), kernel_ref[...])[:1]
    tiles = sums.shape[1] // LANES
    for slot in range(tiles):
        out_ref[slot : slot + 1, :] = sums[:, slot * LANES : (slot + 1) * LANES]
    row_feat = (img_ref[...].astype(F32) * row_scale[:1]).astype(BF16)
    out_ref[tiles:, :] = matmul(row_feat, kernel_ref[:, :LANES])


def finish(
    mine_ref, other_ref, cols_mass_ref, scale_ref, mdl_ref, turned_ref, grad_img_ref, grad_mdl_ref
):
    rows = scale_ref.shape[1]
    tiles = mdl_ref.shape[1] // LANES
    total = mine_ref[:tiles, :] + other_ref[:tiles, :]
    col_scale = jnp.concatenate([total[k : k + 1] for k in range(tiles)], axis=1)
    col_scale = cols_mass_ref[...] / col_scale
    weighted = (mdl_ref[...].astype(F32) * col_scale).astype(BF16)
    grad_img_ref[...] = -(matmul(weighted, turned_ref[:, :rows]) * scale_ref[...])
    terms = mine_ref[tiles:, :] + other_ref[tiles:, :]
    terms = -(terms * col_scale[:, :LANES])
    first = lax.axis_index("img") % 2 == 0
    terms = jnp.where(first, terms, pltpu.roll(terms, LANES // 2, 1))
    grad_mdl_ref[...] = terms[:, : grad_mdl_ref.shape[1]]


def replicated(count, img_feat, mdl_feat, img_mass, mdl_mass):
    groups = count // 2
    rows, share = img_feat.shape[1], mdl_feat.shape[1]
    held, models = groups * rows, count * share

    def swap(block, distance):
        return lax.ppermute(block, "img", [(i, i ^ distance) for i in range(count)])

    packed = call(
        pack, shape(FEAT, rows + LANES, dtype=BF16), img_feat, mdl_feat, img_mass.reshape(-1, LANES)
    )
    far = jnp.concatenate([swap(packed, 2 * s) for s in range(2, groups, 2)], axis=0)
    near = swap(packed, 2)
    cross = swap(far, 2)
    pieces = (packed, near, far, cross)
    mine = call(
        functools.partial(collect, rows), shape(groups * FEAT // 2, LANES, dtype=BF16), *pieces
    )
    outs = (
        shape(held, models, dtype=BF16),
        shape(models, held, dtype=BF16),
        shape(FEAT, held, dtype=BF16),
        shape(FEAT, models, dtype=BF16),
        shape(1, held),
        shape(1, models),
        shape(1, models),
    )
    kernel, turned, img_unit, mdl_unit, mass, cols_mass, sums = call(
        functools.partial(build, groups, rows),
        outs,
        *pieces,
        mine,
        swap(mine, 1),
        mdl_mass.reshape(-1, LANES),
    )
    for iteration in range(1, ITERS - 1):
        sums = call(
            iterate, shape(1, models), sums, swap(sums, 1), cols_mass, mass, kernel, turned
        )
    both, row_scale = call(
        functools.partial(last, rows),
        (shape(models // LANES + FEAT, LANES), shape(1, rows)),
        sums,
        swap(sums, 1),
        cols_mass,
        mass,
        kernel,
        turned,
        img_unit,
    )
    return call(
        finish,
        (shape(FEAT, rows), shape(FEAT, share)),
        both,
        swap(both, 1),
        cols_mass,
        row_scale,
        mdl_unit,
        turned,
    )


def split(img_feat, mdl_feat, img_mass, mdl_mass):
    factor = inv_temp / FEAT
    share = mdl_feat.shape[1]
    img_unit = normalize(img_feat)
    mdl_unit = lax.all_gather(normalize(mdl_feat), "img", axis=1, tiled=True)
    scores = lax.dot_general(
        img_unit, mdl_unit, (((0,), (0,)), ((), ())), preferred_element_type=F32
    )
    kernel = jnp.exp(scores * factor).astype(BF16)
    col_low = jnp.ones((mdl_unit.shape[1],), BF16)
    for iteration in range(ITERS):
        row_scale = img_mass / jnp.dot(kernel, col_low, preferred_element_type=F32)
        sums = jnp.dot(row_scale.astype(BF16), kernel, preferred_element_type=F32)
        col_scale = mdl_mass / lax.psum(sums, "img")
        col_low = col_scale.astype(BF16)
    weighted = (mdl_unit.astype(F32) * col_scale[None, :]).astype(BF16)
    grad_img = lax.dot_general(
        weighted, kernel, (((1,), (1,)), ((), ())), preferred_element_type=F32
    )
    grad_img = -(grad_img * row_scale[None, :])
    row_feat = (img_unit.astype(F32) * row_scale[None, :]).astype(BF16)
    terms = lax.dot_general(
        kernel, row_feat, (((0,), (1,)), ((), ())), preferred_element_type=F32
    )
    summed = lax.psum_scatter(terms, "img", scatter_dimension=0, tiled=True)
    offset = lax.axis_index("img") * share
    own_scale = lax.dynamic_slice_in_dim(col_scale, offset, share, 0)
    grad_mdl = -(summed * own_scale[:, None]).T
    return (grad_img, grad_mdl)


def shards(count, img_feat, mdl_feat, img_mass, mdl_mass):
    groups = count // 2
    rows, share = img_feat.shape[1], mdl_feat.shape[1]
    resident = 2 * 2 * (groups * rows) * (count * share)
    fits = (
        count == 2 * groups
        and groups >= 4
        and groups & (groups - 1) == 0
        and 2 * share == LANES
        and rows % LANES == 0
        and 3 * (rows // LANES) <= FEAT // 2
        and resident <= RESIDENT
    )
    if fits:
        return replicated(count, img_feat, mdl_feat, img_mass, mdl_mass)
    return split(img_feat, mdl_feat, img_mass, mdl_mass)


def solution(mesh):
    placed = (P(None, ("fish", "img")), P(None, ("fish", "img")), P(("fish", "img")), P("fish"))
    return jax.shard_map(
        functools.partial(shards, mesh.shape["img"]),
        mesh=mesh,
        in_specs=placed,
        out_specs=(P(None, ("fish", "img")), P(None, ("fish", "img"))),
        check_vma=False,
    )
```

time: 189 us -> 48.9 us (0.26)
  blocking collectives: 142 us -> 0 us
  Pallas kernels: 0 us -> 16.2 us
  between operations: 14.1 us -> 0.69 us
  starting transfers between devices: 0.04 us -> 8.53 us
  matrix products: 6.44 us -> 0 us
  other arithmetic: 1.98 us -> 0 us
  waiting for transfers between devices: 22.1 us -> 20.2 us
    psum x4 -> x0, blocking collectives: 118 us -> none  [shards(): col_scale = mdl_mass / lax.psum(partial_cols, 'img')]
    all_gather x1 -> x0, blocking collectives: 23.8 us -> none  [shards(): model_unit = lax.all_gather(normalize(mdl_feat), 'img', axis=1, tiled=True)]
    reduce_scatter x1 -> x0, waiting for transfers between devices: 22 us -> none  [shards(): lax.psum_scatter(lax.dot_general(kernel, row_feat, (((0,), (1,)), ((), ()...]
    ppermute x0 -> x10, waiting for transfers between devices: none -> 20.2 us  [swap(): return lax.ppermute(block, 'img', [(i, i ^ distance) for i in range(count)])]
    pallas_call x0 -> x7, Pallas kernels: none -> 16.2 us  [call(): pl.pallas_call(body, out_shape=outs, in_specs=[WHOLE] * len(args), out_sp...]
    ppermute x0 -> x10, starting transfers between devices: none -> 8.53 us  [swap(): return lax.ppermute(block, 'img', [(i, i ^ distance) for i in range(count)])]
    dot_general x11 -> x0, matrix products: 6.44 us -> none  [the longest x4 1.49 us: shards(): jnp.dot(kernel, col_low, preferred_element_type=jnp.float32)]
  transfers between devices with their start and end apart: 1 -> 10, of which waited for: 1 -> 7; matrix products, arithmetic and copies ran while one was open for 1% -> 0% of each run, Pallas kernels for 0% -> 0%
where the time goes in v2:
time: 48.9 us; the launch traced here: 48.6 us
  waiting for transfers between devices  20.2 us (41%)
  Pallas kernels  16.2 us (33%)
  starting transfers between devices  8.53 us (17%)
  local copies, waits for them, and re-layouts  2.95 us (6%)
  between operations  0.69 us (1%)
    ppermute x10, waiting for transfers between devices, swap(): return lax.ppermute(block, 'img', [(i, i ^ distance) for i in range(count)])  20.2 us
    pallas_call x7, Pallas kernels, call(): pl.pallas_call(body, out_shape=outs, in_specs=[WHOLE] * len(args), out_sp...  16.2 us
    ppermute x10, starting transfers between devices, swap(): return lax.ppermute(block, 'img', [(i, i ^ distance) for i in range(count)])  8.53 us
    unnamed x10, local copies, waits for them, and re-layouts  2.94 us
  transfers between devices with their start and end apart: 10, of which 7 were waited for; matrix products, arithmetic and copies ran while one was open for 0% of the time, Pallas kernels for 0%

profile of v2, /device:TPU:0, one launch (start us, length us, event | category | flops | bytes accessed | tf_op | source)
XLA Modules:
  0.0 48.6 jit_solution(6485267293045467276)
XLA Ops:
  0.6 0.0 copy-start
  0.6 0.8 %copy-done = bf16[64,512]{1,0:T(8,128)(2,1)S(1)} copy-done((bf16[64,512]{1,0:T(8,128)(2,1)S(1)}, bf16[64,512]{1,0:T(8,128)(2,1)}, u32[]{:S(2)}) %copy-start) | copy-done | bytes 65560
  1.5 0.0 copy-start.1
  1.5 0.7 %copy-done.1 = bf16[64,64]{1,0:T(8,128)(2,1)S(1)} copy-done((bf16[64,64]{1,0:T(8,128)(2,1)S(1)}, bf16[64,64]{1,0:T(8,128)(2,1)}, u32[]{:S(2)}) %copy-start.1) | copy-done | bytes 8216
  2.2 0.0 copy-start.3
  2.2 0.7 %copy-done.3 = f32[512]{0:T(512)S(1)} copy-done((f32[512]{0:T(512)S(1)}, f32[512]{0:T(512)}, u32[]{:S(2)}) %copy-start.3) | copy-done | bytes 2072
  2.9 0.1 shard_map.59.own_ref
  3.0 3.0 %collective-permute-start.1 = (bf16[64,640]{1,0:T(8,128)(2,1)S(1)}, bf16[64,640]{1,0:T(8,128)(2,1)S(1)}, u32[]{:S(2)}, u32[]{:S(2)}) collective-permute-start(bf16[64,640]{1,0:T(8,128)(2,1)S(1)} %shard_map.59.own_ref), channel_id=1, source_target_pairs={{0,4},{1,5},{2,6},{3,7},{4,0},{5,1},{6,2},{7,3},{8,12},{9,13},{10,... | collective-permute-start | bytes 245768 | tf_op jit(solution)/shard_map/ppermute | solution.py:208
  6.0 2.5 %collective-permute-start.3 = (bf16[64,640]{1,0:T(8,128)(2,1)S(1)}, bf16[64,640]{1,0:T(8,128)(2,1)S(1)}, u32[]{:S(2)}, u32[]{:S(2)}) collective-permute-start(bf16[64,640]{1,0:T(8,128)(2,1)S(1)} %shard_map.59.own_ref), channel_id=1, source_target_pairs={{0,12},{1,13},{2,14},{3,15},{4,8},{5,9},{6,10},{7,11},{8,4},{9,5},... | collective-permute-start | bytes 245768 | tf_op jit(solution)/shard_map/ppermute | solution.py:208
  8.5 0.1 collective-permute-start.2
  8.6 0.0 collective-permute-done.1
  8.6 7.5 %collective-permute-done.2 = bf16[64,640]{1,0:T(8,128)(2,1)S(1)} collective-permute-done((bf16[64,640]{1,0:T(8,128)(2,1)S(1)}, bf16[64,640]{1,0:T(8,128)(2,1)S(1)}, u32[]{:S(2)}, u32[]{:S(2)}) %collective-permute-start.2) | collective-permute-done | bytes 81952 | tf_op jit(solution)/shard_map/ppermute | solution.py:208
  16.2 0.0 collective-permute-done.3
  16.2 1.6 %collective-permute-start.4 = (bf16[192,640]{1,0:T(8,128)(2,1)S(1)}, bf16[192,640]{1,0:T(8,128)(2,1)S(1)}, u32[]{:S(2)}, u32[]{:S(2)}) collective-permute-start(bf16[192,640]{1,0:T(8,128)(2,1)S(1)} %constant_dynamic-update-slice_fusion.far_ref), channel_id=1, source_target_pairs={{0,2},{1,3},{2,0},{3,1},{4,6},{5,7},{6,4},{7,5},{8,10},{9,11},{10,... | collective-permute-start | bytes 737288 | tf_op jit(solution)/shard_map/ppermute | solution.py:208
  17.8 0.5 %collective-permute-start = (bf16[64,640]{1,0:T(8,128)(2,1)S(1)}, bf16[64,640]{1,0:T(8,128)(2,1)S(1)}, u32[]{:S(2)}, u32[]{:S(2)}) collective-permute-start(bf16[64,640]{1,0:T(8,128)(2,1)S(1)} %shard_map.59.own_ref), channel_id=1, source_target_pairs={{0,2},{1,3},{2,0},{3,1},{4,6},{5,7},{6,4},{7,5},{8,10},{9,11},{10,... | collective-permute-start | bytes 245768 | tf_op jit(solution)/shard_map/ppermute | solution.py:208
  18.3 7.4 %collective-permute-done.near_ref = bf16[64,640]{1,0:T(8,128)(2,1)S(1)} collective-permute-done((bf16[64,640]{1,0:T(8,128)(2,1)S(1)}, bf16[64,640]{1,0:T(8,128)(2,1)S(1)}, u32[]{:S(2)}, u32[]{:S(2)}) %collective-permute-start) | collective-permute-done | bytes 81952 | tf_op jit(solution)/shard_map/ppermute | solution.py:208
  25.7 0.0 collective-permute-done.4.cross_ref
  25.7 0.1 collective-permute-start.5
  25.8 1.2 %collective-permute-done.5.other_ref = bf16[256,128]{1,0:T(8,128)(2,1)S(1)} collective-permute-done((bf16[256,128]{1,0:T(8,128)(2,1)S(1)}, bf16[256,128]{1,0:T(8,128)(2,1)S(1)}, u32[]{:S(2)}, u32[]{:S(2)}) %collective-permute-start.5) | collective-permute-done | bytes 65568 | tf_op jit(solution)/shard_map/ppermute | solution.py:208
  27.0 0.0 copy-start.2
  27.0 0.7 %copy-done.2 = f32[1024]{0:T(1024)S(1)} copy-done((f32[1024]{0:T(1024)S(1)}, f32[1024]{0:T(1024)}, u32[]{:S(2)}) %copy-start.2) | copy-done | bytes 4120
  27.7 7.9 %shard_map.61 = (bf16[4096,1024]{1,0:T(8,128)(2,1)S(1)}, bf16[1024,4096]{1,0:T(8,128)(2,1)S(1)}, bf16[64,4096]{1,0:T(8,128)(2,1)S(1)}, bf16[64,1024]{1,0:T(8,128...) custom-call(bf16[64,640]{1,0:T(8,128)(2,1)S(1)} %shard_map.59.own_ref, ...), custom_call_target="tpu_custom_call" | custom-call | tf_op jit(solution)/shard_map/pallas_call | solution.py:23
  35.6 0.2 collective-permute-start.6
  35.8 1.0 %collective-permute-done.6.other_ref = f32[1,1024]{1,0:T(1,128)S(1)} collective-permute-done((f32[1,1024]{1,0:T(1,128)S(1)}, f32[1,1024]{1,0:T(1,128)S(1)}, u32[]{:S(2)}, u32[]{:S(2)}) %collective-permute-start.6) | collective-permute-done | bytes 4128 | tf_op jit(solution)/shard_map/ppermute | solution.py:208
  36.8 2.3 %shard_map.62.mine_ref = f32[1,1024]{1,0:T(1,128)S(1)} custom-call(f32[1,1024]{1,0:T(1,128)S(1)} %get-tuple-element.11.mine_ref, f32[1,1024]{1,0:T(1,128)S(1)} %collective-permute-done.6.other_ref, f32[1,1024]{1,0:T(1,128)S(1)} %get-tuple-element.12.cols_mass_ref, f32[1,4096]{1,0:T(1,128)S(1)} %get-tuple-element.13.mass_ref, ...), custom_call_target="tpu_custom_call" | custom-call | tf_op jit(solution)/shard_map/pallas_call | solution.py:23
  39.1 0.2 collective-permute-start.7
  39.3 1.0 %collective-permute-done.7.other_ref = f32[1,1024]{1,0:T(1,128)S(1)} collective-permute-done((f32[1,1024]{1,0:T(1,128)S(1)}, f32[1,1024]{1,0:T(1,128)S(1)}, u32[]{:S(2)}, u32[]{:S(2)}) %collective-permute-start.7) | collective-permute-done | bytes 4128 | tf_op jit(solution)/shard_map/ppermute | solution.py:208
  40.3 2.3 %shard_map.63.mine_ref = f32[1,1024]{1,0:T(1,128)S(1)} custom-call(f32[1,1024]{1,0:T(1,128)S(1)} %shard_map.62.mine_ref, f32[1,1024]{1,0:T(1,128)S(1)} %collective-permute-done.7.other_ref, f32[1,1024]{1,0:T(1,128)S(1)} %get-tuple-element.12.cols_mass_ref, f32[1,4096]{1,0:T(1,128)S(1)} %get-tuple-element.13.mass_ref, ...), custom_call_target="tpu_custom_call" | custom-call | tf_op jit(solution)/shard_map/pallas_call | solution.py:23
  42.5 0.2 collective-permute-start.8
  42.7 1.0 %collective-permute-done.8.other_ref = f32[1,1024]{1,0:T(1,128)S(1)} collective-permute-done((f32[1,1024]{1,0:T(1,128)S(1)}, f32[1,1024]{1,0:T(1,128)S(1)}, u32[]{:S(2)}, u32[]{:S(2)}) %collective-permute-start.8) | collective-permute-done | bytes 4128 | tf_op jit(solution)/shard_map/ppermute | solution.py:208
  43.7 2.6 %shard_map.64 = (f32[72,128]{1,0:T(8,128)S(1)}, f32[1,512]{1,0:T(1,128)S(1)}) custom-call(f32[1,1024]{1,0:T(1,128)S(1)} %shard_map.63.mine_ref, f32[1,1024]{1,0:T(1,128)S(1)} %collective-permute-done.8.other_ref, f32[1,1024]{1,0:T(1,128)S(1)} %get-tuple-element.12.cols_mass_ref, f32[1,4096]{1,0:T(1,128)S(1)} %get-tuple-element.13.mass_ref, ...), custom_call_target="tpu_custom_call" | custom-call | tf_op jit(solution)/shard_map/pallas_call | solution.py:23
  46.3 0.2 collective-permute-start.9
  46.6 1.0 %collective-permute-done.9.other_ref = f32[72,128]{1,0:T(8,128)S(1)} collective-permute-done((f32[72,128]{1,0:T(8,128)S(1)}, f32[72,128]{1,0:T(8,128)S(1)}, u32[]{:S(2)}, u32[]{:S(2)}) %collective-permute-start.9) | collective-permute-done | bytes 36896 | tf_op jit(solution)/shard_map/ppermute | solution.py:208
  47.6 1.0 %shard_map.65 = (f32[64,512]{1,0:T(8,128)}, f32[64,64]{1,0:T(8,128)}) custom-call(f32[72,128]{1,0:T(8,128)S(1)} %get-tuple-element.17.mine_ref, f32[72,128]{1,0:T(8,128)S(1)} %collective-permute-done.9.other_ref, f32[1,1024]{1,0:T(1,128)S(1)} %get-tuple-element.12.cols_mass_ref, f32[1,512]{1,0:T(1,128)S(1)} %get-tuple-element.18.scale_ref, ...), custom_call_target="tpu_custom_call" | custom-call | tf_op jit(solution)/shard_map/pallas_call | solution.py:23
  (4 shorter events, 0.0 us)
Async XLA Ops:
  0.6 0.8 %copy-start = (bf16[64,512]{1,0:T(8,128)(2,1)S(1)}, bf16[64,512]{1,0:T(8,128)(2,1)}, u32[]{:S(2)}) copy-start(bf16[64,512]{1,0:T(8,128)(2,1)} %img_ref.1) | copy-start | bytes 196612
  1.5 0.7 %copy-start.1 = (bf16[64,64]{1,0:T(8,128)(2,1)S(1)}, bf16[64,64]{1,0:T(8,128)(2,1)}, u32[]{:S(2)}) copy-start(bf16[64,64]{1,0:T(8,128)(2,1)} %mdl_ref.1) | copy-start | bytes 24580
  2.2 0.7 %copy-start.3 = (f32[512]{0:T(512)S(1)}, f32[512]{0:T(512)}, u32[]{:S(2)}) copy-start(f32[512]{0:T(512)} %param.6) | copy-start | bytes 6148
  3.0 5.6 %collective-permute-start.1 = (bf16[64,640]{1,0:T(8,128)(2,1)S(1)}, bf16[64,640]{1,0:T(8,128)(2,1)S(1)}, u32[]{:S(2)}, u32[]{:S(2)}) collective-permute-start(bf16[64,640]{1,0:T(8,128)(2,1)S(1)} %shard_map.59.own_ref), channel_id=1, source_target_pairs={{0,4},{1,5},{2,6},{3,7},{4,0},{5,1},{6,2},{7,3},{8,12},{9,13},{10,... | collective-permute-start | bytes 245768 | tf_op jit(solution)/shard_map/ppermute | solution.py:208
  6.0 10.2 %collective-permute-start.3 = (bf16[64,640]{1,0:T(8,128)(2,1)S(1)}, bf16[64,640]{1,0:T(8,128)(2,1)S(1)}, u32[]{:S(2)}, u32[]{:S(2)}) collective-permute-start(bf16[64,640]{1,0:T(8,128)(2,1)S(1)} %shard_map.59.own_ref), channel_id=1, source_target_pairs={{0,12},{1,13},{2,14},{3,15},{4,8},{5,9},{6,10},{7,11},{8,4},{9,5},... | collective-permute-start | bytes 245768 | tf_op jit(solution)/shard_map/ppermute | solution.py:208
  8.5 7.7 %collective-permute-start.2 = (bf16[64,640]{1,0:T(8,128)(2,1)S(1)}, bf16[64,640]{1,0:T(8,128)(2,1)S(1)}, u32[]{:S(2)}, u32[]{:S(2)}) collective-permute-start(bf16[64,640]{1,0:T(8,128)(2,1)S(1)} %shard_map.59.own_ref), channel_id=1, source_target_pairs={{0,8},{1,9},{2,10},{3,11},{4,12},{5,13},{6,14},{7,15},{8,0},{9,1},... | collective-permute-start | bytes 245768 | tf_op jit(solution)/shard_map/ppermute | solution.py:208
  16.2 9.5 %collective-permute-start.4 = (bf16[192,640]{1,0:T(8,128)(2,1)S(1)}, bf16[192,640]{1,0:T(8,128)(2,1)S(1)}, u32[]{:S(2)}, u32[]{:S(2)}) collective-permute-start(bf16[192,640]{1,0:T(8,128)(2,1)S(1)} %constant_dynamic-update-slice_fusion.far_ref), channel_id=1, source_target_pairs={{0,2},{1,3},{2,0},{3,1},{4,6},{5,7},{6,4},{7,5},{8,10},{9,11},{10,... | collective-permute-start | bytes 737288 | tf_op jit(solution)/shard_map/ppermute | solution.py:208
  17.8 7.9 %collective-permute-start = (bf16[64,640]{1,0:T(8,128)(2,1)S(1)}, bf16[64,640]{1,0:T(8,128)(2,1)S(1)}, u32[]{:S(2)}, u32[]{:S(2)}) collective-permute-start(bf16[64,640]{1,0:T(8,128)(2,1)S(1)} %shard_map.59.own_ref), channel_id=1, source_target_pairs={{0,2},{1,3},{2,0},{3,1},{4,6},{5,7},{6,4},{7,5},{8,10},{9,11},{10,... | collective-permute-start | bytes 245768 | tf_op jit(solution)/shard_map/ppermute | solution.py:208
  25.7 1.3 %collective-permute-start.5 = (bf16[256,128]{1,0:T(8,128)(2,1)S(1)}, bf16[256,128]{1,0:T(8,128)(2,1)S(1)}, u32[]{:S(2)}, u32[]{:S(2)}) collective-permute-start(bf16[256,128]{1,0:T(8,128)(2,1)S(1)} %shard_map.60.mine_ref), channel_id=1, source_target_pairs={{0,1},{1,0},{2,3},{3,2},{4,5},{5,4},{6,7},{7,6},{8,9},{9,8},{10,11... | collective-permute-start | bytes 196616 | tf_op jit(solution)/shard_map/ppermute | solution.py:208
  27.0 0.7 %copy-start.2 = (f32[1024]{0:T(1024)S(1)}, f32[1024]{0:T(1024)}, u32[]{:S(2)}) copy-start(f32[1024]{0:T(1024)} %param.7) | copy-start | bytes 12292
  35.6 1.2 %collective-permute-start.6 = (f32[1,1024]{1,0:T(1,128)S(1)}, f32[1,1024]{1,0:T(1,128)S(1)}, u32[]{:S(2)}, u32[]{:S(2)}) collective-permute-start(f32[1,1024]{1,0:T(1,128)S(1)} %get-tuple-element.11.mine_ref), channel_id=1, source_target_pairs={{0,1},{1,0},{2,3},{3,2},{4,5},{5,4},{6,7},{7,6},{8,9},{9,8},{10,11... | collective-permute-start | bytes 12296 | tf_op jit(solution)/shard_map/ppermute | solution.py:208
  39.1 1.2 %collective-permute-start.7 = (f32[1,1024]{1,0:T(1,128)S(1)}, f32[1,1024]{1,0:T(1,128)S(1)}, u32[]{:S(2)}, u32[]{:S(2)}) collective-permute-start(f32[1,1024]{1,0:T(1,128)S(1)} %shard_map.62.mine_ref), channel_id=1, source_target_pairs={{0,1},{1,0},{2,3},{3,2},{4,5},{5,4},{6,7},{7,6},{8,9},{9,8},{10,11... | collective-permute-start | bytes 12296 | tf_op jit(solution)/shard_map/ppermute | solution.py:208
  42.5 1.2 %collective-permute-start.8 = (f32[1,1024]{1,0:T(1,128)S(1)}, f32[1,1024]{1,0:T(1,128)S(1)}, u32[]{:S(2)}, u32[]{:S(2)}) collective-permute-start(f32[1,1024]{1,0:T(1,128)S(1)} %shard_map.63.mine_ref), channel_id=1, source_target_pairs={{0,1},{1,0},{2,3},{3,2},{4,5},{5,4},{6,7},{7,6},{8,9},{9,8},{10,11... | collective-permute-start | bytes 12296 | tf_op jit(solution)/shard_map/ppermute | solution.py:208
  46.3 1.3 %collective-permute-start.9 = (f32[72,128]{1,0:T(8,128)S(1)}, f32[72,128]{1,0:T(8,128)S(1)}, u32[]{:S(2)}, u32[]{:S(2)}) collective-permute-start(f32[72,128]{1,0:T(8,128)S(1)} %get-tuple-element.17.mine_ref), channel_id=1, source_target_pairs={{0,1},{1,0},{2,3},{3,2},{4,5},{5,4},{6,7},{7,6},{8,9},{9,8},{10,11... | collective-permute-start | bytes 110600 | tf_op jit(solution)/shard_map/ppermute | solution.py:208

commit v3 on v2

v3 whole, which is shorter than its diff:
```python
import functools
import jax
import jax.numpy as jnp
from jax import lax
from jax.experimental import pallas as pl
from jax.experimental.pallas import tpu as pltpu
from jax.sharding import PartitionSpec as P

FEAT = 64
ITERS = 4
LANES = 128
BF16 = jnp.bfloat16
F32 = jnp.float32

inv_temp = 20.0

RESIDENT = 24 << 20
GRANT = 12 << 20
SIZE = 512
COST = 400
WHOLE = pl.BlockSpec(memory_space=pltpu.VMEM)


def call(body, outs, *args, alias=None, specs=None, scratch=(), flops=0):
    return pl.pallas_call(
        body,
        out_shape=outs,
        in_specs=specs or [WHOLE] * len(args),
        out_specs=jax.tree.map(lambda _: WHOLE, outs),
        scratch_shapes=scratch,
        input_output_aliases=alias or {},
        compiler_params=pltpu.CompilerParams(vmem_limit_bytes=GRANT),
        cost_estimate=pl.CostEstimate(flops=flops, bytes_accessed=flops // 512, transcendentals=0),
    )(*args)


def shape(*dims, dtype=F32):
    return jax.ShapeDtypeStruct(dims, dtype)


def normalize(features):
    wide = features.astype(F32)
    guarded = jnp.mean(wide * wide, axis=0, keepdims=True) + 1e-06
    return (wide * lax.rsqrt(guarded)).astype(BF16)


def matmul(left, right):
    return lax.dot_general(left, right, (((1,), (0,)), ((), ())), preferred_element_type=F32)


def fetch(img_hbm, mdl_hbm, mass_hbm, cols_hbm, out_ref, cols_ref, img_ref, mdl_ref, mass_ref, sems):
    pairs = ((img_hbm, img_ref), (mdl_hbm, mdl_ref), (mass_hbm, mass_ref), (cols_hbm, cols_ref))
    copies = [pltpu.make_async_copy(a, b, sems.at[k]) for k, (a, b) in enumerate(pairs)]
    for copy in copies:
        copy.start()
    for copy in copies:
        copy.wait()
    rows = img_ref.shape[1]
    chunks = rows // LANES
    out_ref[:, :rows] = normalize(img_ref[...])
    unit = normalize(mdl_ref[...]).astype(F32)
    half = FEAT // 2
    share = unit.shape[1]
    out_ref[:half, rows : rows + share] = unit[:half].astype(BF16)
    out_ref[:half, rows + share :] = unit[half:].astype(BF16)
    mass = mass_ref[...]
    high = mass.astype(BF16)
    rest = mass - high.astype(F32)
    middle = rest.astype(BF16)
    low = (rest - middle.astype(F32)).astype(BF16)
    terms = [t.astype(F32) for t in (high, middle, low)]
    spare = half - 3 * chunks
    terms = jnp.concatenate(terms + [jnp.zeros((spare, LANES), F32)], axis=0)
    out_ref[half:, rows:] = terms.astype(BF16)


def collect(rows, *refs):
    half = FEAT // 2
    out_ref = refs[-1]
    for slot, ref in enumerate(refs[:-1]):
        out_ref[slot * half : (slot + 1) * half, :] = ref[:half, rows:]


def gather_rows(refs, img_ref, mass_ref):
    half = FEAT // 2
    rows = img_ref.shape[1] // len(refs)
    chunks = rows // LANES
    for slot, ref in enumerate(refs):
        img_ref[:, slot * rows : (slot + 1) * rows] = ref[:, :rows]
        terms = ref[half:, rows:].astype(F32)
        mass = terms[:chunks] + terms[chunks : 2 * chunks] + terms[2 * chunks : 3 * chunks]
        for j in range(chunks):
            at = slot * rows + j * LANES
            mass_ref[:, at : at + LANES] = mass[j : j + 1]


def gather_models(distances, mine_ref, other_ref, mdl_mass_ref, mdl_ref, cols_mass_ref):
    half = FEAT // 2
    place = lax.axis_index("img")
    first = place % 2 == 0
    low_lanes = lax.broadcasted_iota(jnp.int32, (FEAT, LANES), 1) < LANES // 2
    for slot, distance in enumerate(distances):
        sides = []
        for side in (mine_ref, other_ref):
            both = side[slot * half : (slot + 1) * half, :].astype(F32)
            sides.append(jnp.concatenate([both, pltpu.roll(both, LANES // 2, 1)], axis=0))
        left = jnp.where(first, sides[0], sides[1])
        right = jnp.where(first, sides[1], sides[0])
        pair = jnp.where(low_lanes, left, pltpu.roll(right, LANES // 2, 1))
        mdl_ref[:, slot * LANES : (slot + 1) * LANES] = pair.astype(BF16)
        cols_mass_ref[:, slot * LANES : (slot + 1) * LANES] = mdl_mass_ref[
            pl.ds(jnp.bitwise_xor(place // 2, distance), 1), :
        ]


def fill(img_ref, row_at, mdl_ref, cols, kernel_ref, turned_ref, size, also=None):
    def block(index, carry):
        start = pl.multiple_of(index * size, size)
        scores = lax.dot_general(
            img_ref[:, pl.ds(start, size)],
            mdl_ref[...],
            (((0,), (0,)), ((), ())),
            preferred_element_type=F32,
        )
        tile = jnp.exp(scores * (inv_temp / FEAT)).astype(BF16)
        at = pl.ds(pl.multiple_of(row_at + start, size), size)
        kernel_ref[at, cols] = tile
        turned_ref[cols, at] = tile.T
        if also is not None:
            also(at)
        return carry

    lax.fori_loop(0, img_ref.shape[1] // size, block, 0)


def build_first(distances, *refs):
    pieces, refs = refs[: len(distances)], refs[len(distances) :]
    mine_ref, other_ref, mdl_mass_ref, kernel_ref, turned_ref = refs[:5]
    img_ref, mass_ref, mdl_ref, cols_mass_ref = refs[5:]
    gather_rows(pieces, img_ref, mass_ref)
    gather_models(distances, mine_ref, other_ref, mdl_mass_ref, mdl_ref, cols_mass_ref)
    cols = slice(0, mdl_ref.shape[1])
    fill(img_ref, 0, mdl_ref, cols, kernel_ref, turned_ref, SIZE)


def build_rows(count, *refs):
    pieces, refs = refs[:count], refs[count:]
    mdl_ref, _, _, kernel_ref, turned_ref, img_ref, mass_ref = refs
    gather_rows(pieces, img_ref, mass_ref)
    cols = slice(0, mdl_ref.shape[1])
    fill(img_ref, img_ref.shape[1], mdl_ref, cols, kernel_ref, turned_ref, SIZE)


def build_cols(
    distances,
    mine_ref,
    other_ref,
    mdl_mass_ref,
    img_even_ref,
    img_odd_ref,
    mass_even_ref,
    mass_odd_ref,
    _kernel,
    _turned,
    kernel_ref,
    turned_ref,
    mdl_ref,
    cols_mass_ref,
    sums_ref,
):
    gather_models(distances, mine_ref, other_ref, mdl_mass_ref, mdl_ref, cols_mass_ref)
    half = mdl_ref.shape[1]
    cols = slice(half, 2 * half)
    ones = jnp.ones((8, 2 * half), BF16)
    sums_ref[...] = jnp.zeros_like(sums_ref)

    for part, (img_ref, mass_ref) in enumerate(
        ((img_even_ref, mass_even_ref), (img_odd_ref, mass_odd_ref))
    ):
        base = part * img_ref.shape[1]

        def first_iteration(at, base=base, mass_ref=mass_ref):
            row_sums = matmul(ones, turned_ref[:, at])
            start = pl.multiple_of(at.start - base, at.size)
            row_scale = mass_ref[:, pl.ds(start, at.size)] / row_sums
            sums_ref[...] += matmul(row_scale.astype(BF16), kernel_ref[at, :])[:1]

        fill(img_ref, base, mdl_ref, cols, kernel_ref, turned_ref, SIZE, first_iteration)


def joined(refs):
    return jnp.concatenate([ref[...] for ref in refs], axis=1)


def scaled(mine_ref, other_ref, cols_mass):
    return joined(cols_mass) / (mine_ref[...] + other_ref[...])


def row_scales(col_scale, mass, turned_ref):
    low = jnp.broadcast_to(col_scale.astype(BF16), (8, col_scale.shape[1]))
    return joined(mass) / matmul(low, turned_ref[...])


def iterate(mine_ref, other_ref, ce_ref, co_ref, me_ref, mo_ref, kernel_ref, turned_ref, out_ref):
    col_scale = scaled(mine_ref, other_ref, (ce_ref, co_ref))
    row_scale = row_scales(col_scale, (me_ref, mo_ref), turned_ref)
    out_ref[...] = matmul(row_scale.astype(BF16), kernel_ref[...])[:1]


def last(
    rows,
    mine_ref,
    other_ref,
    ce_ref,
    co_ref,
    me_ref,
    mo_ref,
    kernel_ref,
    turned_ref,
    ie_ref,
    io_ref,
    out_ref,
    scale_ref,
):
    col_scale = scaled(mine_ref, other_ref, (ce_ref, co_ref))
    row_scale = row_scales(col_scale, (me_ref, mo_ref), turned_ref)
    scale_ref[...] = row_scale[:1, :rows]
    sums = matmul(row_scale.astype(BF16), kernel_ref[...])[:1]
    tiles = sums.shape[1] // LANES
    for slot in range(tiles):
        out_ref[slot : slot + 1, :] = sums[:, slot * LANES : (slot + 1) * LANES]
    row_feat = (joined((ie_ref, io_ref)).astype(F32) * row_scale[:1]).astype(BF16)
    out_ref[tiles:, :] = matmul(row_feat, kernel_ref[:, :LANES])


def finish(
    mine_ref,
    other_ref,
    ce_ref,
    co_ref,
    scale_ref,
    ue_ref,
    uo_ref,
    turned_ref,
    grad_img_ref,
    grad_mdl_ref,
):
    rows = scale_ref.shape[1]
    tiles = turned_ref.shape[0] // LANES
    total = mine_ref[:tiles, :] + other_ref[:tiles, :]
    col_sums = jnp.concatenate([total[k : k + 1] for k in range(tiles)], axis=1)
    col_scale = joined((ce_ref, co_ref)) / col_sums
    weighted = (joined((ue_ref, uo_ref)).astype(F32) * col_scale).astype(BF16)
    grad_img_ref[...] = -(matmul(weighted, turned_ref[:, :rows]) * scale_ref[...])
    terms = mine_ref[tiles:, :] + other_ref[tiles:, :]
    terms = -(terms * col_scale[:, :LANES])
    first = lax.axis_index("img") % 2 == 0
    terms = jnp.where(first, terms, pltpu.roll(terms, LANES // 2, 1))
    grad_mdl_ref[...] = terms[:, : grad_mdl_ref.shape[1]]


def replicated(count, img_feat, mdl_feat, img_mass, mdl_mass):
    groups = count // 2
    rows, share = img_feat.shape[1], mdl_feat.shape[1]
    held, models = groups * rows, count * share
    even = list(range(0, groups, 2))
    odd = [s + 1 for s in even]

    def swap(block, distance):
        return lax.ppermute(block, "img", [(i, i ^ distance) for i in range(count)])

    arguments = (img_feat, mdl_feat, img_mass.reshape(-1, LANES), mdl_mass.reshape(-1, LANES))
    packed, cols = call(
        fetch,
        (shape(FEAT, rows + LANES, dtype=BF16), shape(models // LANES, LANES)),
        *[pltpu.with_memory_space_constraint(x, pltpu.HBM) for x in arguments],
        specs=[pl.BlockSpec(memory_space=pltpu.HBM)] * 4,
        scratch=[
            pltpu.VMEM((FEAT, rows), BF16),
            pltpu.VMEM((FEAT, share), BF16),
            pltpu.VMEM((rows // LANES, LANES), F32),
            pltpu.SemaphoreType.DMA((4,)),
        ],
    )
    far = [swap(packed, 2 * s) for s in even[1:]]
    near = swap(packed, 2)
    along = [packed] + far
    across = [near] + [swap(block, 2) for block in far]

    def models_of(blocks):
        out = shape(len(blocks) * FEAT // 2, LANES, dtype=BF16)
        mine = call(functools.partial(collect, rows), out, *blocks)
        return mine, swap(mine, 1)

    halves = (shape(FEAT, held // 2, dtype=BF16), shape(1, held // 2))
    sides = (shape(FEAT, models // 2, dtype=BF16), shape(1, models // 2))
    whole = (shape(held, models, dtype=BF16), shape(models, held, dtype=BF16))
    kernel, turned, img_even, mass_even, mdl_even, cols_even = call(
        functools.partial(build_first, even), whole + halves + sides, *along, *models_of(along), cols,
        flops=held * models // 4 * COST,
    )
    kernel, turned, img_odd, mass_odd = call(
        functools.partial(build_rows, len(across)),
        whole + halves,
        *across,
        mdl_even,
        kernel,
        turned,
        alias={len(across) + 1: 0, len(across) + 2: 1},
        flops=held * models // 4 * COST,
    )
    kernel, turned, mdl_odd, cols_odd, sums = call(
        functools.partial(build_cols, odd),
        whole + sides + (shape(1, models),),
        *models_of(across),
        cols,
        img_even,
        img_odd,
        mass_even,
        mass_odd,
        kernel,
        turned,
        alias={7: 0, 8: 1},
        flops=held * models * COST,
    )
    fixed = (cols_even, cols_odd, mass_even, mass_odd, kernel, turned)
    for iteration in range(1, ITERS - 1):
        sums = call(iterate, shape(1, models), sums, swap(sums, 1), *fixed)
    both, row_scale = call(
        functools.partial(last, rows),
        (shape(models // LANES + FEAT, LANES), shape(1, rows)),
        sums,
        swap(sums, 1),
        *fixed,
        img_even,
        img_odd,
    )
    return call(
        finish,
        (shape(FEAT, rows), shape(FEAT, share)),
        both,
        swap(both, 1),
        cols_even,
        cols_odd,
        row_scale,
        mdl_even,
        mdl_odd,
        turned,
    )


def split(img_feat, mdl_feat, img_mass, mdl_mass):
    factor = inv_temp / FEAT
    share = mdl_feat.shape[1]
    img_unit = normalize(img_feat)
    mdl_unit = lax.all_gather(normalize(mdl_feat), "img", axis=1, tiled=True)
    scores = lax.dot_general(
        img_unit, mdl_unit, (((0,), (0,)), ((), ())), preferred_element_type=F32
    )
    kernel = jnp.exp(scores * factor).astype(BF16)
    col_low = jnp.ones((mdl_unit.shape[1],), BF16)
    for iteration in range(ITERS):
        row_scale = img_mass / jnp.dot(kernel, col_low, preferred_element_type=F32)
        sums = jnp.dot(row_scale.astype(BF16), kernel, preferred_element_type=F32)
        col_scale = mdl_mass / lax.psum(sums, "img")
        col_low = col_scale.astype(BF16)
    weighted = (mdl_unit.astype(F32) * col_scale[None, :]).astype(BF16)
    grad_img = lax.dot_general(
        weighted, kernel, (((1,), (1,)), ((), ())), preferred_element_type=F32
    )
    grad_img = -(grad_img * row_scale[None, :])
    row_feat = (img_unit.astype(F32) * row_scale[None, :]).astype(BF16)
    terms = lax.dot_general(
        kernel, row_feat, (((0,), (1,)), ((), ())), preferred_element_type=F32
    )
    summed = lax.psum_scatter(terms, "img", scatter_dimension=0, tiled=True)
    offset = lax.axis_index("img") * share
    own_scale = lax.dynamic_slice_in_dim(col_scale, offset, share, 0)
    grad_mdl = -(summed * own_scale[:, None]).T
    return (grad_img, grad_mdl)


def shards(count, img_feat, mdl_feat, img_mass, mdl_mass):
    groups = count // 2
    rows, share = img_feat.shape[1], mdl_feat.shape[1]
    resident = 2 * 2 * (groups * rows) * (count * share)
    fits = (
        count == 2 * groups
        and groups >= 4
        and groups & (groups - 1) == 0
        and 2 * share == LANES
        and rows % LANES == 0
        and 3 * (rows // LANES) <= FEAT // 2
        and resident <= RESIDENT
    )
    if fits:
        return replicated(count, img_feat, mdl_feat, img_mass, mdl_mass)
    return split(img_feat, mdl_feat, img_mass, mdl_mass)


def solution(mesh):
    placed = (P(None, ("fish", "img")), P(None, ("fish", "img")), P(("fish", "img")), P("fish"))
    return jax.shard_map(
        functools.partial(shards, mesh.shape["img"]),
        mesh=mesh,
        in_specs=placed,
        out_specs=(P(None, ("fish", "img")), P(None, ("fish", "img"))),
        check_vma=False,
    )
```

time: 48.9 us -> 41.2 us (0.84)
  waiting for transfers between devices: 20.2 us -> 9.92 us
  local copies, waits for them, and re-layouts: 2.95 us -> 0 us
  starting transfers between devices: 8.53 us -> 11.4 us
  Pallas kernels: 16.2 us -> 19 us
    ppermute x10 -> x13, waiting for transfers between devices: 20.2 us -> 9.92 us  [swap(): return lax.ppermute(block, 'img', [(i, i ^ distance) for i in range(count)])]
    unnamed x10 -> x0, local copies, waits for them, and re-layouts: 2.94 us -> none
    pallas_call x7 -> x10, Pallas kernels: 16.2 us -> 19 us  [call(): pl.pallas_call(body, out_shape=outs, in_specs=specs or [WHOLE] * len(args...]
    ppermute x10 -> x13, starting transfers between devices: 8.53 us -> 11.4 us  [swap(): return lax.ppermute(block, 'img', [(i, i ^ distance) for i in range(count)])]
  transfers between devices with their start and end apart: 10 -> 13, of which waited for: 7 -> 7; matrix products, arithmetic and copies ran while one was open for 0% -> 0% of each run, Pallas kernels for 0% -> 9%
where the time goes in v3:
time: 41.2 us; the launch traced here: 41 us
  Pallas kernels  19 us (46%)
  starting transfers between devices  11.4 us (28%)
  waiting for transfers between devices  9.92 us (24%)
  between operations  0.72 us (2%)
    pallas_call x10, Pallas kernels, call(): pl.pallas_call(body, out_shape=outs, in_specs=specs or [WHOLE] * len(args...  19 us
    ppermute x13, starting transfers between devices, swap(): return lax.ppermute(block, 'img', [(i, i ^ distance) for i in range(count)])  11.4 us
    ppermute x13, waiting for transfers between devices, swap(): return lax.ppermute(block, 'img', [(i, i ^ distance) for i in range(count)])  9.92 us
  transfers between devices with their start and end apart: 13, of which 7 were waited for; matrix products, arithmetic and copies ran while one was open for 0% of the time, Pallas kernels for 9%

profile of v3, /device:TPU:0, one launch (start us, length us, event | category | flops | bytes accessed | tf_op | source)
XLA Modules:
  0.0 41.0 jit_solution(16876990073405970751)
XLA Ops:
  0.6 1.0 %shard_map.59 = (bf16[64,640]{1,0:T(8,128)(2,1)S(1)}, f32[8,128]{1,0:T(8,128)S(1)}) custom-call(bf16[64,512]{1,0:T(8,128)(2,1)} %img_hbm.1, bf16[64,64]{1,0:T(8,128)(2,1)} %mdl_hbm.1, f32[4,128]{1,0:T(4,128)} %bitcast.3, f32[8,128]{1,0:T(8,128)} %bitcast.2), custom_call_target="tpu_custom_call" | custom-call | tf_op jit(solution)/shard_map/pallas_call | solution.py:25
  1.6 3.1 %collective-permute-start.1 = (bf16[64,640]{1,0:T(8,128)(2,1)S(1)}, bf16[64,640]{1,0:T(8,128)(2,1)S(1)}, u32[]{:S(2)}, u32[]{:S(2)}) collective-permute-start(bf16[64,640]{1,0:T(8,128)(2,1)S(1)} %get-tuple-element.21.refs_0_), channel_id=1, source_target_pairs={{0,4},{1,5},{2,6},{3,7},{4,0},{5,1},{6,2},{7,3},{8,12},{9,13},{10,... | collective-permute-start | bytes 245768 | tf_op jit(solution)/shard_map/ppermute | solution.py:270
  4.7 2.6 %collective-permute-start.3 = (bf16[64,640]{1,0:T(8,128)(2,1)S(1)}, bf16[64,640]{1,0:T(8,128)(2,1)S(1)}, u32[]{:S(2)}, u32[]{:S(2)}) collective-permute-start(bf16[64,640]{1,0:T(8,128)(2,1)S(1)} %get-tuple-element.21.refs_0_), channel_id=1, source_target_pairs={{0,8},{1,9},{2,10},{3,11},{4,12},{5,13},{6,14},{7,15},{8,0},{9,1},... | collective-permute-start | bytes 245768 | tf_op jit(solution)/shard_map/ppermute | solution.py:270
  7.3 0.0 collective-permute-start.5
  7.3 1.7 %collective-permute-start = (bf16[64,640]{1,0:T(8,128)(2,1)S(1)}, bf16[64,640]{1,0:T(8,128)(2,1)S(1)}, u32[]{:S(2)}, u32[]{:S(2)}) collective-permute-start(bf16[64,640]{1,0:T(8,128)(2,1)S(1)} %get-tuple-element.21.refs_0_), channel_id=1, source_target_pairs={{0,2},{1,3},{2,0},{3,1},{4,6},{5,7},{6,4},{7,5},{8,10},{9,11},{10,... | collective-permute-start | bytes 245768 | tf_op jit(solution)/shard_map/ppermute | solution.py:270
  9.0 0.0 collective-permute-done.1.refs_1_
  9.0 0.3 collective-permute-start.2
  9.3 4.6 %collective-permute-done.3.refs_2_ = bf16[64,640]{1,0:T(8,128)(2,1)S(1)} collective-permute-done((bf16[64,640]{1,0:T(8,128)(2,1)S(1)}, bf16[64,640]{1,0:T(8,128)(2,1)S(1)}, u32[]{:S(2)}, u32[]{:S(2)}) %collective-permute-start.3) | collective-permute-done | bytes 81952 | tf_op jit(solution)/shard_map/ppermute | solution.py:270
  13.9 1.5 %collective-permute-start.4 = (bf16[64,640]{1,0:T(8,128)(2,1)S(1)}, bf16[64,640]{1,0:T(8,128)(2,1)S(1)}, u32[]{:S(2)}, u32[]{:S(2)}) collective-permute-start(bf16[64,640]{1,0:T(8,128)(2,1)S(1)} %collective-permute-done.3.refs_2_), channel_id=1, source_target_pairs={{0,2},{1,3},{2,0},{3,1},{4,6},{5,7},{6,4},{7,5},{8,10},{9,11},{10,... | collective-permute-start | bytes 245768 | tf_op jit(solution)/shard_map/ppermute | solution.py:270
  15.4 0.0 collective-permute-done.5.refs_3_
  15.4 0.5 %collective-permute-start.6 = (bf16[64,640]{1,0:T(8,128)(2,1)S(1)}, bf16[64,640]{1,0:T(8,128)(2,1)S(1)}, u32[]{:S(2)}, u32[]{:S(2)}) collective-permute-start(bf16[64,640]{1,0:T(8,128)(2,1)S(1)} %collective-permute-done.5.refs_3_), channel_id=1, source_target_pairs={{0,2},{1,3},{2,0},{3,1},{4,6},{5,7},{6,4},{7,5},{8,10},{9,11},{10,... | collective-permute-start | bytes 245768 | tf_op jit(solution)/shard_map/ppermute | solution.py:270
  15.9 0.0 collective-permute-start.8
  15.9 1.2 %collective-permute-done.8.refs_5_ = bf16[128,128]{1,0:T(8,128)(2,1)S(1)} collective-permute-done((bf16[128,128]{1,0:T(8,128)(2,1)S(1)}, bf16[128,128]{1,0:T(8,128)(2,1)S(1)}, u32[]{:S(2)}, u32[]{:S(2)}) %collective-permute-start.8) | collective-permute-done | bytes 32800 | tf_op jit(solution)/shard_map/ppermute | solution.py:270
  17.1 1.9 %shard_map.62 = (bf16[4096,1024]{1,0:T(8,128)(2,1)S(1)}, bf16[1024,4096]{1,0:T(8,128)(2,1)S(1)}, bf16[64,2048]{1,0:T(8,128)(2,1)S(1)}, f32[1,2048]{1,0:T(1,128)S...) custom-call(bf16[64,640]{1,0:T(8,128)(2,1)S(1)} %get-tuple-element.21.refs_0_, ...), custom_call_target="tpu_custom_call" | custom-call | flops 419430400 | bytes 819200 | tf_op jit(solution)/shard_map/pallas_call | solution.py:25
  19.0 0.0 collective-permute-done.refs_0_
  19.0 0.0 collective-permute-done.2.refs_1_
  19.0 0.0 collective-permute-done.4.refs_2_
  19.0 0.8 %collective-permute-done.6.refs_3_ = bf16[64,640]{1,0:T(8,128)(2,1)S(1)} collective-permute-done((bf16[64,640]{1,0:T(8,128)(2,1)S(1)}, bf16[64,640]{1,0:T(8,128)(2,1)S(1)}, u32[]{:S(2)}, u32[]{:S(2)}) %collective-permute-start.6) | collective-permute-done | bytes 81952 | tf_op jit(solution)/shard_map/ppermute | solution.py:270
  19.8 0.0 collective-permute-start.7
  19.9 1.7 %shard_map.63 = (bf16[4096,1024]{1,0:T(8,128)(2,1)S(1)}, bf16[1024,4096]{1,0:T(8,128)(2,1)S(1)}, bf16[64,2048]{1,0:T(8,128)(2,1)S(1)}, f32[1,2048]{1,0:T(1,128)S(1)}) custom-call(bf16[64,640]{1,0:T(8,128)(2,1)S(1)} %collective-permute-done.refs_0_, bf16[64,640]{1,0:T(8,128)(2,1)S(1)} %collective-permute-done.2.refs_1_, ...), custom_call_target="tpu_custom_call", output_to_operand_aliasing={{0}: (5, {}), {1}: (6, {})} | custom-call | flops 419430400 | bytes 819200 | tf_op jit(solution)/shard_map/pallas_call | solution.py:25
  21.6 0.0 collective-permute-done.7.other_ref
  21.6 6.3 %shard_map.64 = (bf16[4096,1024]{1,0:T(8,128)(2,1)S(1)}, bf16[1024,4096]{1,0:T(8,128)(2,1)S(1)}, bf16[64,512]{1,0:T(8,128)(2,1)S(1)}, f32[1,512]{1,0:T(1,128)S(1)}, f32[1,1024]{1,0:T(1,128)S(1)}) custom-call(bf16[128,128]{1,0:T(8,128)(2,1)S(1)} %shard_map.60.mine_ref, ...), custom_call_target="tpu_custom_call", output_to_operand_aliasing={{0}: (7, {}), {1}: (8, {})} | custom-call | flops 1677721600 | bytes 3276800 | tf_op jit(solution)/shard_map/pallas_call | solution.py:25
  27.9 0.5 %collective-permute-start.9 = (f32[1,1024]{1,0:T(1,128)S(1)}, f32[1,1024]{1,0:T(1,128)S(1)}, u32[]{:S(2)}, u32[]{:S(2)}) collective-permute-start(f32[1,1024]{1,0:T(1,128)S(1)} %get-tuple-element.32.mine_ref), channel_id=1, source_target_pairs={{0,1},{1,0},{2,3},{3,2},{4,5},{5,4},{6,7},{7,6},{8,9},{9,8},{10,11... | collective-permute-start | bytes 12296 | tf_op jit(solution)/shard_map/ppermute | solution.py:270
  28.4 0.8 %collective-permute-done.9.other_ref = f32[1,1024]{1,0:T(1,128)S(1)} collective-permute-done((f32[1,1024]{1,0:T(1,128)S(1)}, f32[1,1024]{1,0:T(1,128)S(1)}, u32[]{:S(2)}, u32[]{:S(2)}) %collective-permute-start.9) | collective-permute-done | bytes 4128 | tf_op jit(solution)/shard_map/ppermute | solution.py:270
  29.2 2.3 %shard_map.65.mine_ref = f32[1,1024]{1,0:T(1,128)S(1)} custom-call(f32[1,1024]{1,0:T(1,128)S(1)} %get-tuple-element.32.mine_ref, f32[1,1024]{1,0:T(1,128)S(1)} %collective-permute-done.9.other_ref, f32[1,512]{1,0:T(1,128)S(1)} %get-tuple-element.33.ce_ref, f32[1,512]{1,0:T(1,128)S(1)} %get-tuple-element.34.co_ref, ...), custom_call_target="tpu_custom_call" | custom-call | tf_op jit(solution)/shard_map/pallas_call | solution.py:25
  31.5 0.4 collective-permute-start.10
  31.8 0.8 %collective-permute-done.10.other_ref = f32[1,1024]{1,0:T(1,128)S(1)} collective-permute-done((f32[1,1024]{1,0:T(1,128)S(1)}, f32[1,1024]{1,0:T(1,128)S(1)}, u32[]{:S(2)}, u32[]{:S(2)}) %collective-permute-start.10) | collective-permute-done | bytes 4128 | tf_op jit(solution)/shard_map/ppermute | solution.py:270
  32.6 2.3 %shard_map.66.mine_ref = f32[1,1024]{1,0:T(1,128)S(1)} custom-call(f32[1,1024]{1,0:T(1,128)S(1)} %shard_map.65.mine_ref, f32[1,1024]{1,0:T(1,128)S(1)} %collective-permute-done.10.other_ref, f32[1,512]{1,0:T(1,128)S(1)} %get-tuple-element.33.ce_ref, f32[1,512]{1,0:T(1,128)S(1)} %get-tuple-element.34.co_ref, ...), custom_call_target="tpu_custom_call" | custom-call | tf_op jit(solution)/shard_map/pallas_call | solution.py:25
  34.9 0.4 collective-permute-start.11
  35.3 0.8 %collective-permute-done.11.other_ref = f32[1,1024]{1,0:T(1,128)S(1)} collective-permute-done((f32[1,1024]{1,0:T(1,128)S(1)}, f32[1,1024]{1,0:T(1,128)S(1)}, u32[]{:S(2)}, u32[]{:S(2)}) %collective-permute-start.11) | collective-permute-done | bytes 4128 | tf_op jit(solution)/shard_map/ppermute | solution.py:270
  36.1 2.7 %shard_map.67 = (f32[72,128]{1,0:T(8,128)S(1)}, f32[1,512]{1,0:T(1,128)S(1)}) custom-call(f32[1,1024]{1,0:T(1,128)S(1)} %shard_map.66.mine_ref, f32[1,1024]{1,0:T(1,128)S(1)} %collective-permute-done.11.other_ref, f32[1,512]{1,0:T(1,128)S(1)} %get-tuple-element.33.ce_ref, f32[1,512]{1,0:T(1,128)S(1)} %get-tuple-element.34.co_ref, ...), custom_call_target="tpu_custom_call" | custom-call | tf_op jit(solution)/shard_map/pallas_call | solution.py:25
  38.8 0.4 collective-permute-start.12
  39.2 0.9 %collective-permute-done.12.other_ref = f32[72,128]{1,0:T(8,128)S(1)} collective-permute-done((f32[72,128]{1,0:T(8,128)S(1)}, f32[72,128]{1,0:T(8,128)S(1)}, u32[]{:S(2)}, u32[]{:S(2)}) %collective-permute-start.12) | collective-permute-done | bytes 36896 | tf_op jit(solution)/shard_map/ppermute | solution.py:270
  40.1 1.0 %shard_map.68 = (f32[64,512]{1,0:T(8,128)}, f32[64,64]{1,0:T(8,128)}) custom-call(f32[72,128]{1,0:T(8,128)S(1)} %get-tuple-element.37.mine_ref, f32[72,128]{1,0:T(8,128)S(1)} %collective-permute-done.12.other_ref, f32[1,512]{1,0:T(1,128)S(1)} %get-tuple-element.33.ce_ref, f32[1,512]{1,0:T(1,128)S(1)} %get-tuple-element.34.co_ref, ...), custom_call_target="tpu_custom_call" | custom-call | tf_op jit(solution)/shard_map/pallas_call | solution.py:25
  (2 shorter events, 0.0 us)
Async XLA Ops:
  1.6 7.4 %collective-permute-start.1 = (bf16[64,640]{1,0:T(8,128)(2,1)S(1)}, bf16[64,640]{1,0:T(8,128)(2,1)S(1)}, u32[]{:S(2)}, u32[]{:S(2)}) collective-permute-start(bf16[64,640]{1,0:T(8,128)(2,1)S(1)} %get-tuple-element.21.refs_0_), channel_id=1, source_target_pairs={{0,4},{1,5},{2,6},{3,7},{4,0},{5,1},{6,2},{7,3},{8,12},{9,13},{10,... | collective-permute-start | bytes 245768 | tf_op jit(solution)/shard_map/ppermute | solution.py:270
  4.7 9.2 %collective-permute-start.3 = (bf16[64,640]{1,0:T(8,128)(2,1)S(1)}, bf16[64,640]{1,0:T(8,128)(2,1)S(1)}, u32[]{:S(2)}, u32[]{:S(2)}) collective-permute-start(bf16[64,640]{1,0:T(8,128)(2,1)S(1)} %get-tuple-element.21.refs_0_), channel_id=1, source_target_pairs={{0,8},{1,9},{2,10},{3,11},{4,12},{5,13},{6,14},{7,15},{8,0},{9,1},... | collective-permute-start | bytes 245768 | tf_op jit(solution)/shard_map/ppermute | solution.py:270
  7.3 8.1 %collective-permute-start.5 = (bf16[64,640]{1,0:T(8,128)(2,1)S(1)}, bf16[64,640]{1,0:T(8,128)(2,1)S(1)}, u32[]{:S(2)}, u32[]{:S(2)}) collective-permute-start(bf16[64,640]{1,0:T(8,128)(2,1)S(1)} %get-tuple-element.21.refs_0_), channel_id=1, source_target_pairs={{0,12},{1,13},{2,14},{3,15},{4,8},{5,9},{6,10},{7,11},{8,4},{9,5},... | collective-permute-start | bytes 245768 | tf_op jit(solution)/shard_map/ppermute | solution.py:270
  7.3 11.7 %collective-permute-start = (bf16[64,640]{1,0:T(8,128)(2,1)S(1)}, bf16[64,640]{1,0:T(8,128)(2,1)S(1)}, u32[]{:S(2)}, u32[]{:S(2)}) collective-permute-start(bf16[64,640]{1,0:T(8,128)(2,1)S(1)} %get-tuple-element.21.refs_0_), channel_id=1, source_target_pairs={{0,2},{1,3},{2,0},{3,1},{4,6},{5,7},{6,4},{7,5},{8,10},{9,11},{10,... | collective-permute-start | bytes 245768 | tf_op jit(solution)/shard_map/ppermute | solution.py:270
  9.0 10.0 %collective-permute-start.2 = (bf16[64,640]{1,0:T(8,128)(2,1)S(1)}, bf16[64,640]{1,0:T(8,128)(2,1)S(1)}, u32[]{:S(2)}, u32[]{:S(2)}) collective-permute-start(bf16[64,640]{1,0:T(8,128)(2,1)S(1)} %collective-permute-done.1.refs_1_), channel_id=1, source_target_pairs={{0,2},{1,3},{2,0},{3,1},{4,6},{5,7},{6,4},{7,5},{8,10},{9,11},{10,... | collective-permute-start | bytes 245768 | tf_op jit(solution)/shard_map/ppermute | solution.py:270
  13.9 5.1 %collective-permute-start.4 = (bf16[64,640]{1,0:T(8,128)(2,1)S(1)}, bf16[64,640]{1,0:T(8,128)(2,1)S(1)}, u32[]{:S(2)}, u32[]{:S(2)}) collective-permute-start(bf16[64,640]{1,0:T(8,128)(2,1)S(1)} %collective-permute-done.3.refs_2_), channel_id=1, source_target_pairs={{0,2},{1,3},{2,0},{3,1},{4,6},{5,7},{6,4},{7,5},{8,10},{9,11},{10,... | collective-permute-start | bytes 245768 | tf_op jit(solution)/shard_map/ppermute | solution.py:270
  15.4 4.4 %collective-permute-start.6 = (bf16[64,640]{1,0:T(8,128)(2,1)S(1)}, bf16[64,640]{1,0:T(8,128)(2,1)S(1)}, u32[]{:S(2)}, u32[]{:S(2)}) collective-permute-start(bf16[64,640]{1,0:T(8,128)(2,1)S(1)} %collective-permute-done.5.refs_3_), channel_id=1, source_target_pairs={{0,2},{1,3},{2,0},{3,1},{4,6},{5,7},{6,4},{7,5},{8,10},{9,11},{10,... | collective-permute-start | bytes 245768 | tf_op jit(solution)/shard_map/ppermute | solution.py:270
  15.9 1.2 %collective-permute-start.8 = (bf16[128,128]{1,0:T(8,128)(2,1)S(1)}, bf16[128,128]{1,0:T(8,128)(2,1)S(1)}, u32[]{:S(2)}, u32[]{:S(2)}) collective-permute-start(bf16[128,128]{1,0:T(8,128)(2,1)S(1)} %shard_map.61.refs_4_), channel_id=1, source_target_pairs={{0,1},{1,0},{2,3},{3,2},{4,5},{5,4},{6,7},{7,6},{8,9},{9,8},{10,11... | collective-permute-start | bytes 98312 | tf_op jit(solution)/shard_map/ppermute | solution.py:270
  19.8 1.7 %collective-permute-start.7 = (bf16[128,128]{1,0:T(8,128)(2,1)S(1)}, bf16[128,128]{1,0:T(8,128)(2,1)S(1)}, u32[]{:S(2)}, u32[]{:S(2)}) collective-permute-start(bf16[128,128]{1,0:T(8,128)(2,1)S(1)} %shard_map.60.mine_ref), channel_id=1, source_target_pairs={{0,1},{1,0},{2,3},{3,2},{4,5},{5,4},{6,7},{7,6},{8,9},{9,8},{10,11... | collective-permute-start | bytes 98312 | tf_op jit(solution)/shard_map/ppermute | solution.py:270
  27.9 1.3 %collective-permute-start.9 = (f32[1,1024]{1,0:T(1,128)S(1)}, f32[1,1024]{1,0:T(1,128)S(1)}, u32[]{:S(2)}, u32[]{:S(2)}) collective-permute-start(f32[1,1024]{1,0:T(1,128)S(1)} %get-tuple-element.32.mine_ref), channel_id=1, source_target_pairs={{0,1},{1,0},{2,3},{3,2},{4,5},{5,4},{6,7},{7,6},{8,9},{9,8},{10,11... | collective-permute-start | bytes 12296 | tf_op jit(solution)/shard_map/ppermute | solution.py:270
  31.5 1.2 %collective-permute-start.10 = (f32[1,1024]{1,0:T(1,128)S(1)}, f32[1,1024]{1,0:T(1,128)S(1)}, u32[]{:S(2)}, u32[]{:S(2)}) collective-permute-start(f32[1,1024]{1,0:T(1,128)S(1)} %shard_map.65.mine_ref), channel_id=1, source_target_pairs={{0,1},{1,0},{2,3},{3,2},{4,5},{5,4},{6,7},{7,6},{8,9},{9,8},{10,11... | collective-permute-start | bytes 12296 | tf_op jit(solution)/shard_map/ppermute | solution.py:270
  34.9 1.2 %collective-permute-start.11 = (f32[1,1024]{1,0:T(1,128)S(1)}, f32[1,1024]{1,0:T(1,128)S(1)}, u32[]{:S(2)}, u32[]{:S(2)}) collective-permute-start(f32[1,1024]{1,0:T(1,128)S(1)} %shard_map.66.mine_ref), channel_id=1, source_target_pairs={{0,1},{1,0},{2,3},{3,2},{4,5},{5,4},{6,7},{7,6},{8,9},{9,8},{10,11... | collective-permute-start | bytes 12296 | tf_op jit(solution)/shard_map/ppermute | solution.py:270
  38.8 1.3 %collective-permute-start.12 = (f32[72,128]{1,0:T(8,128)S(1)}, f32[72,128]{1,0:T(8,128)S(1)}, u32[]{:S(2)}, u32[]{:S(2)}) collective-permute-start(f32[72,128]{1,0:T(8,128)S(1)} %get-tuple-element.37.mine_ref), channel_id=1, source_target_pairs={{0,1},{1,0},{2,3},{3,2},{4,5},{5,4},{6,7},{7,6},{8,9},{9,8},{10,11... | collective-permute-start | bytes 110600 | tf_op jit(solution)/shard_map/ppermute | solution.py:270

commit v4 on v3

--- a/solution.py
+++ b/solution.py
@@ -16,7 +16,6 @@
 
 RESIDENT = 24 << 20
 GRANT = 12 << 20
-SIZE = 512
 COST = 400
 WHOLE = pl.BlockSpec(memory_space=pltpu.VMEM)
 
@@ -113,24 +112,17 @@
         ]
 
 
-def fill(img_ref, row_at, mdl_ref, cols, kernel_ref, turned_ref, size, also=None):
-    def block(index, carry):
-        start = pl.multiple_of(index * size, size)
-        scores = lax.dot_general(
-            img_ref[:, pl.ds(start, size)],
-            mdl_ref[...],
-            (((0,), (0,)), ((), ())),
-            preferred_element_type=F32,
-        )
-        tile = jnp.exp(scores * (inv_temp / FEAT)).astype(BF16)
-        at = pl.ds(pl.multiple_of(row_at + start, size), size)
-        kernel_ref[at, cols] = tile
-        turned_ref[cols, at] = tile.T
-        if also is not None:
-            also(at)
-        return carry
-
-    lax.fori_loop(0, img_ref.shape[1] // size, block, 0)
+def fill(img_ref, rows, mdl_ref, cols, kernel_ref, turned_ref):
+    scores = lax.dot_general(
+        img_ref[...], mdl_ref[...], (((0,), (0,)), ((), ())), preferred_element_type=F32
+    )
+    tile = jnp.exp(scores * (inv_temp / FEAT)).astype(BF16)
+    kernel_ref[rows, cols] = tile
+    turned_ref[cols, rows] = tile.T
+
+
+def halves_of(extent):
+    return slice(0, extent // 2), slice(extent // 2, extent)
 
 
 def build_first(distances, *refs):
@@ -139,16 +131,16 @@
     img_ref, mass_ref, mdl_ref, cols_mass_ref = refs[5:]
     gather_rows(pieces, img_ref, mass_ref)
     gather_models(distances, mine_ref, other_ref, mdl_mass_ref, mdl_ref, cols_mass_ref)
-    cols = slice(0, mdl_ref.shape[1])
-    fill(img_ref, 0, mdl_ref, cols, kernel_ref, turned_ref, SIZE)
+    rows, cols = (halves_of(extent)[0] for extent in kernel_ref.shape)
+    fill(img_ref, rows, mdl_ref, cols, kernel_ref, turned_ref)
 
 
 def build_rows(count, *refs):
     pieces, refs = refs[:count], refs[count:]
     mdl_ref, _, _, kernel_ref, turned_ref, img_ref, mass_ref = refs
     gather_rows(pieces, img_ref, mass_ref)
-    cols = slice(0, mdl_ref.shape[1])
-    fill(img_ref, img_ref.shape[1], mdl_ref, cols, kernel_ref, turned_ref, SIZE)
+    rows, cols = halves_of(kernel_ref.shape[0])[1], halves_of(kernel_ref.shape[1])[0]
+    fill(img_ref, rows, mdl_ref, cols, kernel_ref, turned_ref)
 
 
 def build_cols(
@@ -169,23 +161,12 @@
     sums_ref,
 ):
     gather_models(distances, mine_ref, other_ref, mdl_mass_ref, mdl_ref, cols_mass_ref)
-    half = mdl_ref.shape[1]
-    cols = slice(half, 2 * half)
-    ones = jnp.ones((8, 2 * half), BF16)
-    sums_ref[...] = jnp.zeros_like(sums_ref)
-
-    for part, (img_ref, mass_ref) in enumerate(
-        ((img_even_ref, mass_even_ref), (img_odd_ref, mass_odd_ref))
-    ):
-        base = part * img_ref.shape[1]
-
-        def first_iteration(at, base=base, mass_ref=mass_ref):
-            row_sums = matmul(ones, turned_ref[:, at])
-            start = pl.multiple_of(at.start - base, at.size)
-            row_scale = mass_ref[:, pl.ds(start, at.size)] / row_sums
-            sums_ref[...] += matmul(row_scale.astype(BF16), kernel_ref[at, :])[:1]
-
-        fill(img_ref, base, mdl_ref, cols, kernel_ref, turned_ref, SIZE, first_iteration)
+    cols = halves_of(kernel_ref.shape[1])[1]
+    for rows, img_ref in zip(halves_of(kernel_ref.shape[0]), (img_even_ref, img_odd_ref)):
+        fill(img_ref, rows, mdl_ref, cols, kernel_ref, turned_ref)
+    ones = jnp.ones((1, kernel_ref.shape[1]), F32)
+    row_scale = row_scales(ones, (mass_even_ref, mass_odd_ref), turned_ref)
+    sums_ref[...] = matmul(row_scale.astype(BF16), kernel_ref[...])[:1]
 
 
 def joined(refs):

time: 41.2 us -> 38.4 us (0.932)
  Pallas kernels: 19 us -> 15.5 us
  waiting for transfers between devices: 9.92 us -> 10.8 us
    pallas_call x10, Pallas kernels: 19 us -> 15.5 us  [call(): pl.pallas_call(body, out_shape=outs, in_specs=specs or [WHOLE] * len(args...]
    ppermute x13, waiting for transfers between devices: 9.92 us -> 10.8 us  [swap(): return lax.ppermute(block, 'img', [(i, i ^ distance) for i in range(count)])]
  transfers between devices with their start and end apart: 13 -> 13, of which waited for: 7 -> 8; matrix products, arithmetic and copies ran while one was open for 0% -> 0% of each run, Pallas kernels for 9% -> 6%
where the time goes in v4:
time: 38.4 us; the launch traced here: 38.2 us
  Pallas kernels  15.5 us (40%)
  starting transfers between devices  11.2 us (29%)
  waiting for transfers between devices  10.8 us (28%)
  between operations  0.7 us (2%)
    pallas_call x10, Pallas kernels, call(): pl.pallas_call(body, out_shape=outs, in_specs=specs or [WHOLE] * len(args...  15.5 us
    ppermute x13, starting transfers between devices, swap(): return lax.ppermute(block, 'img', [(i, i ^ distance) for i in range(count)])  11.2 us
    ppermute x13, waiting for transfers between devices, swap(): return lax.ppermute(block, 'img', [(i, i ^ distance) for i in range(count)])  10.8 us
  transfers between devices with their start and end apart: 13, of which 8 were waited for; matrix products, arithmetic and copies ran while one was open for 0% of the time, Pallas kernels for 6%

profile of v4, /device:TPU:0, one launch (start us, length us, event | category | flops | bytes accessed | tf_op | source)
XLA Modules:
  0.0 38.2 jit_solution(658121384609097242)
XLA Ops:
  0.6 1.0 %shard_map.59 = (bf16[64,640]{1,0:T(8,128)(2,1)S(1)}, f32[8,128]{1,0:T(8,128)S(1)}) custom-call(bf16[64,512]{1,0:T(8,128)(2,1)} %img_hbm.1, bf16[64,64]{1,0:T(8,128)(2,1)} %mdl_hbm.1, f32[4,128]{1,0:T(4,128)} %bitcast.3, f32[8,128]{1,0:T(8,128)} %bitcast.2), custom_call_target="tpu_custom_call" | custom-call | tf_op jit(solution)/shard_map/pallas_call | solution.py:24
  1.6 3.1 %collective-permute-start.1 = (bf16[64,640]{1,0:T(8,128)(2,1)S(1)}, bf16[64,640]{1,0:T(8,128)(2,1)S(1)}, u32[]{:S(2)}, u32[]{:S(2)}) collective-permute-start(bf16[64,640]{1,0:T(8,128)(2,1)S(1)} %get-tuple-element.21.refs_0_), channel_id=1, source_target_pairs={{0,4},{1,5},{2,6},{3,7},{4,0},{5,1},{6,2},{7,3},{8,12},{9,13},{10,... | collective-permute-start | bytes 245768 | tf_op jit(solution)/shard_map/ppermute | solution.py:251
  4.7 2.6 %collective-permute-start.3 = (bf16[64,640]{1,0:T(8,128)(2,1)S(1)}, bf16[64,640]{1,0:T(8,128)(2,1)S(1)}, u32[]{:S(2)}, u32[]{:S(2)}) collective-permute-start(bf16[64,640]{1,0:T(8,128)(2,1)S(1)} %get-tuple-element.21.refs_0_), channel_id=1, source_target_pairs={{0,8},{1,9},{2,10},{3,11},{4,12},{5,13},{6,14},{7,15},{8,0},{9,1},... | collective-permute-start | bytes 245768 | tf_op jit(solution)/shard_map/ppermute | solution.py:251
  7.3 0.0 collective-permute-start.5
  7.3 1.7 %collective-permute-start = (bf16[64,640]{1,0:T(8,128)(2,1)S(1)}, bf16[64,640]{1,0:T(8,128)(2,1)S(1)}, u32[]{:S(2)}, u32[]{:S(2)}) collective-permute-start(bf16[64,640]{1,0:T(8,128)(2,1)S(1)} %get-tuple-element.21.refs_0_), channel_id=1, source_target_pairs={{0,2},{1,3},{2,0},{3,1},{4,6},{5,7},{6,4},{7,5},{8,10},{9,11},{10,... | collective-permute-start | bytes 245768 | tf_op jit(solution)/shard_map/ppermute | solution.py:251
  9.0 0.0 collective-permute-done.1.refs_1_
  9.0 0.3 collective-permute-start.2
  9.3 4.6 %collective-permute-done.3.refs_2_ = bf16[64,640]{1,0:T(8,128)(2,1)S(1)} collective-permute-done((bf16[64,640]{1,0:T(8,128)(2,1)S(1)}, bf16[64,640]{1,0:T(8,128)(2,1)S(1)}, u32[]{:S(2)}, u32[]{:S(2)}) %collective-permute-start.3) | collective-permute-done | bytes 81952 | tf_op jit(solution)/shard_map/ppermute | solution.py:251
  13.9 1.5 %collective-permute-start.4 = (bf16[64,640]{1,0:T(8,128)(2,1)S(1)}, bf16[64,640]{1,0:T(8,128)(2,1)S(1)}, u32[]{:S(2)}, u32[]{:S(2)}) collective-permute-start(bf16[64,640]{1,0:T(8,128)(2,1)S(1)} %collective-permute-done.3.refs_2_), channel_id=1, source_target_pairs={{0,2},{1,3},{2,0},{3,1},{4,6},{5,7},{6,4},{7,5},{8,10},{9,11},{10,... | collective-permute-start | bytes 245768 | tf_op jit(solution)/shard_map/ppermute | solution.py:251
  15.4 0.0 collective-permute-done.5.refs_3_
  15.4 0.5 %collective-permute-start.6 = (bf16[64,640]{1,0:T(8,128)(2,1)S(1)}, bf16[64,640]{1,0:T(8,128)(2,1)S(1)}, u32[]{:S(2)}, u32[]{:S(2)}) collective-permute-start(bf16[64,640]{1,0:T(8,128)(2,1)S(1)} %collective-permute-done.5.refs_3_), channel_id=1, source_target_pairs={{0,2},{1,3},{2,0},{3,1},{4,6},{5,7},{6,4},{7,5},{8,10},{9,11},{10,... | collective-permute-start | bytes 245768 | tf_op jit(solution)/shard_map/ppermute | solution.py:251
  15.9 0.0 collective-permute-start.8
  15.9 1.2 %collective-permute-done.8.refs_5_ = bf16[128,128]{1,0:T(8,128)(2,1)S(1)} collective-permute-done((bf16[128,128]{1,0:T(8,128)(2,1)S(1)}, bf16[128,128]{1,0:T(8,128)(2,1)S(1)}, u32[]{:S(2)}, u32[]{:S(2)}) %collective-permute-start.8) | collective-permute-done | bytes 32800 | tf_op jit(solution)/shard_map/ppermute | solution.py:251
  17.1 1.1 %shard_map.62 = (bf16[4096,1024]{1,0:T(8,128)(2,1)S(1)}, bf16[1024,4096]{1,0:T(8,128)(2,1)S(1)}, bf16[64,2048]{1,0:T(8,128)(2,1)S(1)}, f32[1,2048]{1,0:T(1,128)S...) custom-call(bf16[64,640]{1,0:T(8,128)(2,1)S(1)} %get-tuple-element.21.refs_0_, ...), custom_call_target="tpu_custom_call" | custom-call | flops 419430400 | bytes 819200 | tf_op jit(solution)/shard_map/pallas_call | solution.py:24
  18.3 0.0 collective-permute-done.refs_0_
  18.3 0.0 collective-permute-done.2.refs_1_
  18.3 0.0 collective-permute-done.4.refs_2_
  18.3 1.5 %collective-permute-done.6.refs_3_ = bf16[64,640]{1,0:T(8,128)(2,1)S(1)} collective-permute-done((bf16[64,640]{1,0:T(8,128)(2,1)S(1)}, bf16[64,640]{1,0:T(8,128)(2,1)S(1)}, u32[]{:S(2)}, u32[]{:S(2)}) %collective-permute-start.6) | collective-permute-done | bytes 81952 | tf_op jit(solution)/shard_map/ppermute | solution.py:251
  19.8 0.0 collective-permute-start.7
  19.9 1.1 %shard_map.63 = (bf16[4096,1024]{1,0:T(8,128)(2,1)S(1)}, bf16[1024,4096]{1,0:T(8,128)(2,1)S(1)}, bf16[64,2048]{1,0:T(8,128)(2,1)S(1)}, f32[1,2048]{1,0:T(1,128)S(1)}) custom-call(bf16[64,640]{1,0:T(8,128)(2,1)S(1)} %collective-permute-done.refs_0_, bf16[64,640]{1,0:T(8,128)(2,1)S(1)} %collective-permute-done.2.refs_1_, ...), custom_call_target="tpu_custom_call", output_to_operand_aliasing={{0}: (5, {}), {1}: (6, {})} | custom-call | flops 419430400 | bytes 819200 | tf_op jit(solution)/shard_map/pallas_call | solution.py:24
  20.9 0.1 collective-permute-done.7.other_ref
  21.0 4.1 %shard_map.64 = (bf16[4096,1024]{1,0:T(8,128)(2,1)S(1)}, bf16[1024,4096]{1,0:T(8,128)(2,1)S(1)}, bf16[64,512]{1,0:T(8,128)(2,1)S(1)}, f32[1,512]{1,0:T(1,128)S(1)}, f32[1,1024]{1,0:T(1,128)S(1)}) custom-call(bf16[128,128]{1,0:T(8,128)(2,1)S(1)} %shard_map.60.mine_ref, ...), custom_call_target="tpu_custom_call", output_to_operand_aliasing={{0}: (7, {}), {1}: (8, {})} | custom-call | flops 1677721600 | bytes 3276800 | tf_op jit(solution)/shard_map/pallas_call | solution.py:24
  25.2 0.4 %collective-permute-start.9 = (f32[1,1024]{1,0:T(1,128)S(1)}, f32[1,1024]{1,0:T(1,128)S(1)}, u32[]{:S(2)}, u32[]{:S(2)}) collective-permute-start(f32[1,1024]{1,0:T(1,128)S(1)} %get-tuple-element.32.mine_ref), channel_id=1, source_target_pairs={{0,1},{1,0},{2,3},{3,2},{4,5},{5,4},{6,7},{7,6},{8,9},{9,8},{10,11... | collective-permute-start | bytes 12296 | tf_op jit(solution)/shard_map/ppermute | solution.py:251
  25.6 0.8 %collective-permute-done.9.other_ref = f32[1,1024]{1,0:T(1,128)S(1)} collective-permute-done((f32[1,1024]{1,0:T(1,128)S(1)}, f32[1,1024]{1,0:T(1,128)S(1)}, u32[]{:S(2)}, u32[]{:S(2)}) %collective-permute-start.9) | collective-permute-done | bytes 4128 | tf_op jit(solution)/shard_map/ppermute | solution.py:251
  26.4 2.3 %shard_map.65.mine_ref = f32[1,1024]{1,0:T(1,128)S(1)} custom-call(f32[1,1024]{1,0:T(1,128)S(1)} %get-tuple-element.32.mine_ref, f32[1,1024]{1,0:T(1,128)S(1)} %collective-permute-done.9.other_ref, f32[1,512]{1,0:T(1,128)S(1)} %get-tuple-element.33.ce_ref, f32[1,512]{1,0:T(1,128)S(1)} %get-tuple-element.34.co_ref, ...), custom_call_target="tpu_custom_call" | custom-call | tf_op jit(solution)/shard_map/pallas_call | solution.py:24
  28.7 0.4 collective-permute-start.10
  29.0 0.8 %collective-permute-done.10.other_ref = f32[1,1024]{1,0:T(1,128)S(1)} collective-permute-done((f32[1,1024]{1,0:T(1,128)S(1)}, f32[1,1024]{1,0:T(1,128)S(1)}, u32[]{:S(2)}, u32[]{:S(2)}) %collective-permute-start.10) | collective-permute-done | bytes 4128 | tf_op jit(solution)/shard_map/ppermute | solution.py:251
  29.8 2.3 %shard_map.66.mine_ref = f32[1,1024]{1,0:T(1,128)S(1)} custom-call(f32[1,1024]{1,0:T(1,128)S(1)} %shard_map.65.mine_ref, f32[1,1024]{1,0:T(1,128)S(1)} %collective-permute-done.10.other_ref, f32[1,512]{1,0:T(1,128)S(1)} %get-tuple-element.33.ce_ref, f32[1,512]{1,0:T(1,128)S(1)} %get-tuple-element.34.co_ref, ...), custom_call_target="tpu_custom_call" | custom-call | tf_op jit(solution)/shard_map/pallas_call | solution.py:24
  32.1 0.4 collective-permute-start.11
  32.5 0.8 %collective-permute-done.11.other_ref = f32[1,1024]{1,0:T(1,128)S(1)} collective-permute-done((f32[1,1024]{1,0:T(1,128)S(1)}, f32[1,1024]{1,0:T(1,128)S(1)}, u32[]{:S(2)}, u32[]{:S(2)}) %collective-permute-start.11) | collective-permute-done | bytes 4128 | tf_op jit(solution)/shard_map/ppermute | solution.py:251
  33.3 2.7 %shard_map.67 = (f32[72,128]{1,0:T(8,128)S(1)}, f32[1,512]{1,0:T(1,128)S(1)}) custom-call(f32[1,1024]{1,0:T(1,128)S(1)} %shard_map.66.mine_ref, f32[1,1024]{1,0:T(1,128)S(1)} %collective-permute-done.11.other_ref, f32[1,512]{1,0:T(1,128)S(1)} %get-tuple-element.33.ce_ref, f32[1,512]{1,0:T(1,128)S(1)} %get-tuple-element.34.co_ref, ...), custom_call_target="tpu_custom_call" | custom-call | tf_op jit(solution)/shard_map/pallas_call | solution.py:24
  36.0 0.4 %collective-permute-start.12 = (f32[72,128]{1,0:T(8,128)S(1)}, f32[72,128]{1,0:T(8,128)S(1)}, u32[]{:S(2)}, u32[]{:S(2)}) collective-permute-start(f32[72,128]{1,0:T(8,128)S(1)} %get-tuple-element.37.mine_ref), channel_id=1, source_target_pairs={{0,1},{1,0},{2,3},{3,2},{4,5},{5,4},{6,7},{7,6},{8,9},{9,8},{10,11... | collective-permute-start | bytes 110600 | tf_op jit(solution)/shard_map/ppermute | solution.py:251
  36.4 0.9 %collective-permute-done.12.other_ref = f32[72,128]{1,0:T(8,128)S(1)} collective-permute-done((f32[72,128]{1,0:T(8,128)S(1)}, f32[72,128]{1,0:T(8,128)S(1)}, u32[]{:S(2)}, u32[]{:S(2)}) %collective-permute-start.12) | collective-permute-done | bytes 36896 | tf_op jit(solution)/shard_map/ppermute | solution.py:251
  37.3 1.0 %shard_map.68 = (f32[64,512]{1,0:T(8,128)}, f32[64,64]{1,0:T(8,128)}) custom-call(f32[72,128]{1,0:T(8,128)S(1)} %get-tuple-element.37.mine_ref, f32[72,128]{1,0:T(8,128)S(1)} %collective-permute-done.12.other_ref, f32[1,512]{1,0:T(1,128)S(1)} %get-tuple-element.33.ce_ref, f32[1,512]{1,0:T(1,128)S(1)} %get-tuple-element.34.co_ref, ...), custom_call_target="tpu_custom_call" | custom-call | tf_op jit(solution)/shard_map/pallas_call | solution.py:24
  (2 shorter events, 0.0 us)
Async XLA Ops:
  1.6 7.4 %collective-permute-start.1 = (bf16[64,640]{1,0:T(8,128)(2,1)S(1)}, bf16[64,640]{1,0:T(8,128)(2,1)S(1)}, u32[]{:S(2)}, u32[]{:S(2)}) collective-permute-start(bf16[64,640]{1,0:T(8,128)(2,1)S(1)} %get-tuple-element.21.refs_0_), channel_id=1, source_target_pairs={{0,4},{1,5},{2,6},{3,7},{4,0},{5,1},{6,2},{7,3},{8,12},{9,13},{10,... | collective-permute-start | bytes 245768 | tf_op jit(solution)/shard_map/ppermute | solution.py:251
  4.7 9.2 %collective-permute-start.3 = (bf16[64,640]{1,0:T(8,128)(2,1)S(1)}, bf16[64,640]{1,0:T(8,128)(2,1)S(1)}, u32[]{:S(2)}, u32[]{:S(2)}) collective-permute-start(bf16[64,640]{1,0:T(8,128)(2,1)S(1)} %get-tuple-element.21.refs_0_), channel_id=1, source_target_pairs={{0,8},{1,9},{2,10},{3,11},{4,12},{5,13},{6,14},{7,15},{8,0},{9,1},... | collective-permute-start | bytes 245768 | tf_op jit(solution)/shard_map/ppermute | solution.py:251
  7.3 8.1 %collective-permute-start.5 = (bf16[64,640]{1,0:T(8,128)(2,1)S(1)}, bf16[64,640]{1,0:T(8,128)(2,1)S(1)}, u32[]{:S(2)}, u32[]{:S(2)}) collective-permute-start(bf16[64,640]{1,0:T(8,128)(2,1)S(1)} %get-tuple-element.21.refs_0_), channel_id=1, source_target_pairs={{0,12},{1,13},{2,14},{3,15},{4,8},{5,9},{6,10},{7,11},{8,4},{9,5},... | collective-permute-start | bytes 245768 | tf_op jit(solution)/shard_map/ppermute | solution.py:251
  7.3 11.0 %collective-permute-start = (bf16[64,640]{1,0:T(8,128)(2,1)S(1)}, bf16[64,640]{1,0:T(8,128)(2,1)S(1)}, u32[]{:S(2)}, u32[]{:S(2)}) collective-permute-start(bf16[64,640]{1,0:T(8,128)(2,1)S(1)} %get-tuple-element.21.refs_0_), channel_id=1, source_target_pairs={{0,2},{1,3},{2,0},{3,1},{4,6},{5,7},{6,4},{7,5},{8,10},{9,11},{10,... | collective-permute-start | bytes 245768 | tf_op jit(solution)/shard_map/ppermute | solution.py:251
  9.0 9.3 %collective-permute-start.2 = (bf16[64,640]{1,0:T(8,128)(2,1)S(1)}, bf16[64,640]{1,0:T(8,128)(2,1)S(1)}, u32[]{:S(2)}, u32[]{:S(2)}) collective-permute-start(bf16[64,640]{1,0:T(8,128)(2,1)S(1)} %collective-permute-done.1.refs_1_), channel_id=1, source_target_pairs={{0,2},{1,3},{2,0},{3,1},{4,6},{5,7},{6,4},{7,5},{8,10},{9,11},{10,... | collective-permute-start | bytes 245768 | tf_op jit(solution)/shard_map/ppermute | solution.py:251
  13.9 4.4 %collective-permute-start.4 = (bf16[64,640]{1,0:T(8,128)(2,1)S(1)}, bf16[64,640]{1,0:T(8,128)(2,1)S(1)}, u32[]{:S(2)}, u32[]{:S(2)}) collective-permute-start(bf16[64,640]{1,0:T(8,128)(2,1)S(1)} %collective-permute-done.3.refs_2_), channel_id=1, source_target_pairs={{0,2},{1,3},{2,0},{3,1},{4,6},{5,7},{6,4},{7,5},{8,10},{9,11},{10,... | collective-permute-start | bytes 245768 | tf_op jit(solution)/shard_map/ppermute | solution.py:251
  15.4 4.4 %collective-permute-start.6 = (bf16[64,640]{1,0:T(8,128)(2,1)S(1)}, bf16[64,640]{1,0:T(8,128)(2,1)S(1)}, u32[]{:S(2)}, u32[]{:S(2)}) collective-permute-start(bf16[64,640]{1,0:T(8,128)(2,1)S(1)} %collective-permute-done.5.refs_3_), channel_id=1, source_target_pairs={{0,2},{1,3},{2,0},{3,1},{4,6},{5,7},{6,4},{7,5},{8,10},{9,11},{10,... | collective-permute-start | bytes 245768 | tf_op jit(solution)/shard_map/ppermute | solution.py:251
  15.9 1.2 %collective-permute-start.8 = (bf16[128,128]{1,0:T(8,128)(2,1)S(1)}, bf16[128,128]{1,0:T(8,128)(2,1)S(1)}, u32[]{:S(2)}, u32[]{:S(2)}) collective-permute-start(bf16[128,128]{1,0:T(8,128)(2,1)S(1)} %shard_map.61.refs_4_), channel_id=1, source_target_pairs={{0,1},{1,0},{2,3},{3,2},{4,5},{5,4},{6,7},{7,6},{8,9},{9,8},{10,11... | collective-permute-start | bytes 98312 | tf_op jit(solution)/shard_map/ppermute | solution.py:251
  19.8 1.2 %collective-permute-start.7 = (bf16[128,128]{1,0:T(8,128)(2,1)S(1)}, bf16[128,128]{1,0:T(8,128)(2,1)S(1)}, u32[]{:S(2)}, u32[]{:S(2)}) collective-permute-start(bf16[128,128]{1,0:T(8,128)(2,1)S(1)} %shard_map.60.mine_ref), channel_id=1, source_target_pairs={{0,1},{1,0},{2,3},{3,2},{4,5},{5,4},{6,7},{7,6},{8,9},{9,8},{10,11... | collective-permute-start | bytes 98312 | tf_op jit(solution)/shard_map/ppermute | solution.py:251
  25.2 1.2 %collective-permute-start.9 = (f32[1,1024]{1,0:T(1,128)S(1)}, f32[1,1024]{1,0:T(1,128)S(1)}, u32[]{:S(2)}, u32[]{:S(2)}) collective-permute-start(f32[1,1024]{1,0:T(1,128)S(1)} %get-tuple-element.32.mine_ref), channel_id=1, source_target_pairs={{0,1},{1,0},{2,3},{3,2},{4,5},{5,4},{6,7},{7,6},{8,9},{9,8},{10,11... | collective-permute-start | bytes 12296 | tf_op jit(solution)/shard_map/ppermute | solution.py:251
  28.7 1.2 %collective-permute-start.10 = (f32[1,1024]{1,0:T(1,128)S(1)}, f32[1,1024]{1,0:T(1,128)S(1)}, u32[]{:S(2)}, u32[]{:S(2)}) collective-permute-start(f32[1,1024]{1,0:T(1,128)S(1)} %shard_map.65.mine_ref), channel_id=1, source_target_pairs={{0,1},{1,0},{2,3},{3,2},{4,5},{5,4},{6,7},{7,6},{8,9},{9,8},{10,11... | collective-permute-start | bytes 12296 | tf_op jit(solution)/shard_map/ppermute | solution.py:251
  32.1 1.2 %collective-permute-start.11 = (f32[1,1024]{1,0:T(1,128)S(1)}, f32[1,1024]{1,0:T(1,128)S(1)}, u32[]{:S(2)}, u32[]{:S(2)}) collective-permute-start(f32[1,1024]{1,0:T(1,128)S(1)} %shard_map.66.mine_ref), channel_id=1, source_target_pairs={{0,1},{1,0},{2,3},{3,2},{4,5},{5,4},{6,7},{7,6},{8,9},{9,8},{10,11... | collective-permute-start | bytes 12296 | tf_op jit(solution)/shard_map/ppermute | solution.py:251
  36.0 1.3 %collective-permute-start.12 = (f32[72,128]{1,0:T(8,128)S(1)}, f32[72,128]{1,0:T(8,128)S(1)}, u32[]{:S(2)}, u32[]{:S(2)}) collective-permute-start(f32[72,128]{1,0:T(8,128)S(1)} %get-tuple-element.37.mine_ref), channel_id=1, source_target_pairs={{0,1},{1,0},{2,3},{3,2},{4,5},{5,4},{6,7},{7,6},{8,9},{9,8},{10,11... | collective-permute-start | bytes 110600 | tf_op jit(solution)/shard_map/ppermute | solution.py:251

commit v5 on v4

--- a/solution.py
+++ b/solution.py
@@ -244,7 +244,8 @@
     groups = count // 2
     rows, share = img_feat.shape[1], mdl_feat.shape[1]
     held, models = groups * rows, count * share
-    even = list(range(0, groups, 2))
+    middle = groups // 2
+    even = [0, middle] + [s for s in range(2, groups, 2) if s != middle]
     odd = [s + 1 for s in even]
 
     def swap(block, distance):

time: 38.4 us -> 36.5 us (0.951)
  waiting for transfers between devices: 10.8 us -> 7.43 us
  starting transfers between devices: 11.2 us -> 12.7 us
    ppermute x13, waiting for transfers between devices: 10.8 us -> 7.43 us  [swap(): return lax.ppermute(block, 'img', [(i, i ^ distance) for i in range(count)])]
    ppermute x13, starting transfers between devices: 11.2 us -> 12.7 us  [swap(): return lax.ppermute(block, 'img', [(i, i ^ distance) for i in range(count)])]
  transfers between devices with their start and end apart: 13 -> 13, of which waited for: 8 -> 9; matrix products, arithmetic and copies ran while one was open for 0% -> 0% of each run, Pallas kernels for 6% -> 6%
where the time goes in v5:
time: 36.5 us; the launch traced here: 36.4 us
  Pallas kernels  15.5 us (42%)
  starting transfers between devices  12.7 us (35%)
  waiting for transfers between devices  7.43 us (20%)
  between operations  0.71 us (2%)
    pallas_call x10, Pallas kernels, call(): pl.pallas_call(body, out_shape=outs, in_specs=specs or [WHOLE] * len(args...  15.5 us
    ppermute x13, starting transfers between devices, swap(): return lax.ppermute(block, 'img', [(i, i ^ distance) for i in range(count)])  12.7 us
    ppermute x13, waiting for transfers between devices, swap(): return lax.ppermute(block, 'img', [(i, i ^ distance) for i in range(count)])  7.43 us
  transfers between devices with their start and end apart: 13, of which 9 were waited for; matrix products, arithmetic and copies ran while one was open for 0% of the time, Pallas kernels for 6%

profile of v5, /device:TPU:0, one launch (start us, length us, event | category | flops | bytes accessed | tf_op | source)
XLA Modules:
  0.0 36.4 jit_solution(2256823426629159362)
XLA Ops:
  0.6 1.0 %shard_map.59 = (bf16[64,640]{1,0:T(8,128)(2,1)S(1)}, f32[8,128]{1,0:T(8,128)S(1)}) custom-call(bf16[64,512]{1,0:T(8,128)(2,1)} %img_hbm.1, bf16[64,64]{1,0:T(8,128)(2,1)} %mdl_hbm.1, f32[4,128]{1,0:T(4,128)} %bitcast.3, f32[8,128]{1,0:T(8,128)} %bitcast.2), custom_call_target="tpu_custom_call" | custom-call | tf_op jit(solution)/shard_map/pallas_call | solution.py:24
  1.6 4.1 %collective-permute-start.1 = (bf16[64,640]{1,0:T(8,128)(2,1)S(1)}, bf16[64,640]{1,0:T(8,128)(2,1)S(1)}, u32[]{:S(2)}, u32[]{:S(2)}) collective-permute-start(bf16[64,640]{1,0:T(8,128)(2,1)S(1)} %get-tuple-element.21.refs_0_), channel_id=1, source_target_pairs={{0,8},{1,9},{2,10},{3,11},{4,12},{5,13},{6,14},{7,15},{8,0},{9,1},... | collective-permute-start | bytes 245768 | tf_op jit(solution)/shard_map/ppermute | solution.py:252
  5.7 1.6 %collective-permute-start.3 = (bf16[64,640]{1,0:T(8,128)(2,1)S(1)}, bf16[64,640]{1,0:T(8,128)(2,1)S(1)}, u32[]{:S(2)}, u32[]{:S(2)}) collective-permute-start(bf16[64,640]{1,0:T(8,128)(2,1)S(1)} %get-tuple-element.21.refs_0_), channel_id=1, source_target_pairs={{0,4},{1,5},{2,6},{3,7},{4,0},{5,1},{6,2},{7,3},{8,12},{9,13},{10,... | collective-permute-start | bytes 245768 | tf_op jit(solution)/shard_map/ppermute | solution.py:252
  7.3 0.0 collective-permute-start.5
  7.3 1.7 %collective-permute-start = (bf16[64,640]{1,0:T(8,128)(2,1)S(1)}, bf16[64,640]{1,0:T(8,128)(2,1)S(1)}, u32[]{:S(2)}, u32[]{:S(2)}) collective-permute-start(bf16[64,640]{1,0:T(8,128)(2,1)S(1)} %get-tuple-element.21.refs_0_), channel_id=1, source_target_pairs={{0,2},{1,3},{2,0},{3,1},{4,6},{5,7},{6,4},{7,5},{8,10},{9,11},{10,... | collective-permute-start | bytes 245768 | tf_op jit(solution)/shard_map/ppermute | solution.py:252
  9.0 0.7 %collective-permute-done.1.refs_1_ = bf16[64,640]{1,0:T(8,128)(2,1)S(1)} collective-permute-done((bf16[64,640]{1,0:T(8,128)(2,1)S(1)}, bf16[64,640]{1,0:T(8,128)(2,1)S(1)}, u32[]{:S(2)}, u32[]{:S(2)}) %collective-permute-start.1) | collective-permute-done | bytes 81952 | tf_op jit(solution)/shard_map/ppermute | solution.py:252
  9.7 2.2 %collective-permute-start.2 = (bf16[64,640]{1,0:T(8,128)(2,1)S(1)}, bf16[64,640]{1,0:T(8,128)(2,1)S(1)}, u32[]{:S(2)}, u32[]{:S(2)}) collective-permute-start(bf16[64,640]{1,0:T(8,128)(2,1)S(1)} %collective-permute-done.1.refs_1_), channel_id=1, source_target_pairs={{0,2},{1,3},{2,0},{3,1},{4,6},{5,7},{6,4},{7,5},{8,10},{9,11},{10,... | collective-permute-start | bytes 245768 | tf_op jit(solution)/shard_map/ppermute | solution.py:252
  11.9 0.0 collective-permute-done.3.refs_2_
  11.9 0.0 collective-permute-start.4
  12.0 1.6 %collective-permute-done.5.refs_3_ = bf16[64,640]{1,0:T(8,128)(2,1)S(1)} collective-permute-done((bf16[64,640]{1,0:T(8,128)(2,1)S(1)}, bf16[64,640]{1,0:T(8,128)(2,1)S(1)}, u32[]{:S(2)}, u32[]{:S(2)}) %collective-permute-start.5) | collective-permute-done | bytes 81952 | tf_op jit(solution)/shard_map/ppermute | solution.py:252
  13.5 1.6 %collective-permute-start.6 = (bf16[64,640]{1,0:T(8,128)(2,1)S(1)}, bf16[64,640]{1,0:T(8,128)(2,1)S(1)}, u32[]{:S(2)}, u32[]{:S(2)}) collective-permute-start(bf16[64,640]{1,0:T(8,128)(2,1)S(1)} %collective-permute-done.5.refs_3_), channel_id=1, source_target_pairs={{0,2},{1,3},{2,0},{3,1},{4,6},{5,7},{6,4},{7,5},{8,10},{9,11},{10,... | collective-permute-start | bytes 245768 | tf_op jit(solution)/shard_map/ppermute | solution.py:252
  15.1 0.0 collective-permute-start.8
  15.1 1.2 %collective-permute-done.8.refs_5_ = bf16[128,128]{1,0:T(8,128)(2,1)S(1)} collective-permute-done((bf16[128,128]{1,0:T(8,128)(2,1)S(1)}, bf16[128,128]{1,0:T(8,128)(2,1)S(1)}, u32[]{:S(2)}, u32[]{:S(2)}) %collective-permute-start.8) | collective-permute-done | bytes 32800 | tf_op jit(solution)/shard_map/ppermute | solution.py:252
  16.3 1.1 %shard_map.62 = (bf16[4096,1024]{1,0:T(8,128)(2,1)S(1)}, bf16[1024,4096]{1,0:T(8,128)(2,1)S(1)}, bf16[64,2048]{1,0:T(8,128)(2,1)S(1)}, f32[1,2048]{1,0:T(1,128)S...) custom-call(bf16[64,640]{1,0:T(8,128)(2,1)S(1)} %get-tuple-element.21.refs_0_, ...), custom_call_target="tpu_custom_call" | custom-call | flops 419430400 | bytes 819200 | tf_op jit(solution)/shard_map/pallas_call | solution.py:24
  17.5 0.0 collective-permute-done.refs_0_
  17.5 0.0 collective-permute-done.2.refs_1_
  17.5 0.0 collective-permute-done.4.refs_2_
  17.5 0.5 %collective-permute-done.6.refs_3_ = bf16[64,640]{1,0:T(8,128)(2,1)S(1)} collective-permute-done((bf16[64,640]{1,0:T(8,128)(2,1)S(1)}, bf16[64,640]{1,0:T(8,128)(2,1)S(1)}, u32[]{:S(2)}, u32[]{:S(2)}) %collective-permute-start.6) | collective-permute-done | bytes 81952 | tf_op jit(solution)/shard_map/ppermute | solution.py:252
  18.0 0.0 collective-permute-start.7
  18.0 1.1 %shard_map.63 = (bf16[4096,1024]{1,0:T(8,128)(2,1)S(1)}, bf16[1024,4096]{1,0:T(8,128)(2,1)S(1)}, bf16[64,2048]{1,0:T(8,128)(2,1)S(1)}, f32[1,2048]{1,0:T(1,128)S(1)}) custom-call(bf16[64,640]{1,0:T(8,128)(2,1)S(1)} %collective-permute-done.refs_0_, bf16[64,640]{1,0:T(8,128)(2,1)S(1)} %collective-permute-done.2.refs_1_, ...), custom_call_target="tpu_custom_call", output_to_operand_aliasing={{0}: (5, {}), {1}: (6, {})} | custom-call | flops 419430400 | bytes 819200 | tf_op jit(solution)/shard_map/pallas_call | solution.py:24
  19.1 0.1 collective-permute-done.7.other_ref
  19.2 4.1 %shard_map.64 = (bf16[4096,1024]{1,0:T(8,128)(2,1)S(1)}, bf16[1024,4096]{1,0:T(8,128)(2,1)S(1)}, bf16[64,512]{1,0:T(8,128)(2,1)S(1)}, f32[1,512]{1,0:T(1,128)S(1)}, f32[1,1024]{1,0:T(1,128)S(1)}) custom-call(bf16[128,128]{1,0:T(8,128)(2,1)S(1)} %shard_map.60.mine_ref, ...), custom_call_target="tpu_custom_call", output_to_operand_aliasing={{0}: (7, {}), {1}: (8, {})} | custom-call | flops 1677721600 | bytes 3276800 | tf_op jit(solution)/shard_map/pallas_call | solution.py:24
  23.3 0.4 %collective-permute-start.9 = (f32[1,1024]{1,0:T(1,128)S(1)}, f32[1,1024]{1,0:T(1,128)S(1)}, u32[]{:S(2)}, u32[]{:S(2)}) collective-permute-start(f32[1,1024]{1,0:T(1,128)S(1)} %get-tuple-element.32.mine_ref), channel_id=1, source_target_pairs={{0,1},{1,0},{2,3},{3,2},{4,5},{5,4},{6,7},{7,6},{8,9},{9,8},{10,11... | collective-permute-start | bytes 12296 | tf_op jit(solution)/shard_map/ppermute | solution.py:252
  23.7 0.8 %collective-permute-done.9.other_ref = f32[1,1024]{1,0:T(1,128)S(1)} collective-permute-done((f32[1,1024]{1,0:T(1,128)S(1)}, f32[1,1024]{1,0:T(1,128)S(1)}, u32[]{:S(2)}, u32[]{:S(2)}) %collective-permute-start.9) | collective-permute-done | bytes 4128 | tf_op jit(solution)/shard_map/ppermute | solution.py:252
  24.5 2.3 %shard_map.65.mine_ref = f32[1,1024]{1,0:T(1,128)S(1)} custom-call(f32[1,1024]{1,0:T(1,128)S(1)} %get-tuple-element.32.mine_ref, f32[1,1024]{1,0:T(1,128)S(1)} %collective-permute-done.9.other_ref, f32[1,512]{1,0:T(1,128)S(1)} %get-tuple-element.33.ce_ref, f32[1,512]{1,0:T(1,128)S(1)} %get-tuple-element.34.co_ref, ...), custom_call_target="tpu_custom_call" | custom-call | tf_op jit(solution)/shard_map/pallas_call | solution.py:24
  26.8 0.4 collective-permute-start.10
  27.2 0.8 %collective-permute-done.10.other_ref = f32[1,1024]{1,0:T(1,128)S(1)} collective-permute-done((f32[1,1024]{1,0:T(1,128)S(1)}, f32[1,1024]{1,0:T(1,128)S(1)}, u32[]{:S(2)}, u32[]{:S(2)}) %collective-permute-start.10) | collective-permute-done | bytes 4128 | tf_op jit(solution)/shard_map/ppermute | solution.py:252
  28.0 2.3 %shard_map.66.mine_ref = f32[1,1024]{1,0:T(1,128)S(1)} custom-call(f32[1,1024]{1,0:T(1,128)S(1)} %shard_map.65.mine_ref, f32[1,1024]{1,0:T(1,128)S(1)} %collective-permute-done.10.other_ref, f32[1,512]{1,0:T(1,128)S(1)} %get-tuple-element.33.ce_ref, f32[1,512]{1,0:T(1,128)S(1)} %get-tuple-element.34.co_ref, ...), custom_call_target="tpu_custom_call" | custom-call | tf_op jit(solution)/shard_map/pallas_call | solution.py:24
  30.3 0.4 collective-permute-start.11
  30.6 0.8 %collective-permute-done.11.other_ref = f32[1,1024]{1,0:T(1,128)S(1)} collective-permute-done((f32[1,1024]{1,0:T(1,128)S(1)}, f32[1,1024]{1,0:T(1,128)S(1)}, u32[]{:S(2)}, u32[]{:S(2)}) %collective-permute-start.11) | collective-permute-done | bytes 4128 | tf_op jit(solution)/shard_map/ppermute | solution.py:252
  31.4 2.7 %shard_map.67 = (f32[72,128]{1,0:T(8,128)S(1)}, f32[1,512]{1,0:T(1,128)S(1)}) custom-call(f32[1,1024]{1,0:T(1,128)S(1)} %shard_map.66.mine_ref, f32[1,1024]{1,0:T(1,128)S(1)} %collective-permute-done.11.other_ref, f32[1,512]{1,0:T(1,128)S(1)} %get-tuple-element.33.ce_ref, f32[1,512]{1,0:T(1,128)S(1)} %get-tuple-element.34.co_ref, ...), custom_call_target="tpu_custom_call" | custom-call | tf_op jit(solution)/shard_map/pallas_call | solution.py:24
  34.1 0.4 %collective-permute-start.12 = (f32[72,128]{1,0:T(8,128)S(1)}, f32[72,128]{1,0:T(8,128)S(1)}, u32[]{:S(2)}, u32[]{:S(2)}) collective-permute-start(f32[72,128]{1,0:T(8,128)S(1)} %get-tuple-element.37.mine_ref), channel_id=1, source_target_pairs={{0,1},{1,0},{2,3},{3,2},{4,5},{5,4},{6,7},{7,6},{8,9},{9,8},{10,11... | collective-permute-start | bytes 110600 | tf_op jit(solution)/shard_map/ppermute | solution.py:252
  34.5 0.9 %collective-permute-done.12.other_ref = f32[72,128]{1,0:T(8,128)S(1)} collective-permute-done((f32[72,128]{1,0:T(8,128)S(1)}, f32[72,128]{1,0:T(8,128)S(1)}, u32[]{:S(2)}, u32[]{:S(2)}) %collective-permute-start.12) | collective-permute-done | bytes 36896 | tf_op jit(solution)/shard_map/ppermute | solution.py:252
  35.4 1.0 %shard_map.68 = (f32[64,512]{1,0:T(8,128)}, f32[64,64]{1,0:T(8,128)}) custom-call(f32[72,128]{1,0:T(8,128)S(1)} %get-tuple-element.37.mine_ref, f32[72,128]{1,0:T(8,128)S(1)} %collective-permute-done.12.other_ref, f32[1,512]{1,0:T(1,128)S(1)} %get-tuple-element.33.ce_ref, f32[1,512]{1,0:T(1,128)S(1)} %get-tuple-element.34.co_ref, ...), custom_call_target="tpu_custom_call" | custom-call | tf_op jit(solution)/shard_map/pallas_call | solution.py:24
  (2 shorter events, 0.0 us)
Async XLA Ops:
  1.6 8.1 %collective-permute-start.1 = (bf16[64,640]{1,0:T(8,128)(2,1)S(1)}, bf16[64,640]{1,0:T(8,128)(2,1)S(1)}, u32[]{:S(2)}, u32[]{:S(2)}) collective-permute-start(bf16[64,640]{1,0:T(8,128)(2,1)S(1)} %get-tuple-element.21.refs_0_), channel_id=1, source_target_pairs={{0,8},{1,9},{2,10},{3,11},{4,12},{5,13},{6,14},{7,15},{8,0},{9,1},... | collective-permute-start | bytes 245768 | tf_op jit(solution)/shard_map/ppermute | solution.py:252
  5.7 6.2 %collective-permute-start.3 = (bf16[64,640]{1,0:T(8,128)(2,1)S(1)}, bf16[64,640]{1,0:T(8,128)(2,1)S(1)}, u32[]{:S(2)}, u32[]{:S(2)}) collective-permute-start(bf16[64,640]{1,0:T(8,128)(2,1)S(1)} %get-tuple-element.21.refs_0_), channel_id=1, source_target_pairs={{0,4},{1,5},{2,6},{3,7},{4,0},{5,1},{6,2},{7,3},{8,12},{9,13},{10,... | collective-permute-start | bytes 245768 | tf_op jit(solution)/shard_map/ppermute | solution.py:252
  7.3 6.2 %collective-permute-start.5 = (bf16[64,640]{1,0:T(8,128)(2,1)S(1)}, bf16[64,640]{1,0:T(8,128)(2,1)S(1)}, u32[]{:S(2)}, u32[]{:S(2)}) collective-permute-start(bf16[64,640]{1,0:T(8,128)(2,1)S(1)} %get-tuple-element.21.refs_0_), channel_id=1, source_target_pairs={{0,12},{1,13},{2,14},{3,15},{4,8},{5,9},{6,10},{7,11},{8,4},{9,5},... | collective-permute-start | bytes 245768 | tf_op jit(solution)/shard_map/ppermute | solution.py:252
  7.3 10.2 %collective-permute-start = (bf16[64,640]{1,0:T(8,128)(2,1)S(1)}, bf16[64,640]{1,0:T(8,128)(2,1)S(1)}, u32[]{:S(2)}, u32[]{:S(2)}) collective-permute-start(bf16[64,640]{1,0:T(8,128)(2,1)S(1)} %get-tuple-element.21.refs_0_), channel_id=1, source_target_pairs={{0,2},{1,3},{2,0},{3,1},{4,6},{5,7},{6,4},{7,5},{8,10},{9,11},{10,... | collective-permute-start | bytes 245768 | tf_op jit(solution)/shard_map/ppermute | solution.py:252
  9.7 7.8 %collective-permute-start.2 = (bf16[64,640]{1,0:T(8,128)(2,1)S(1)}, bf16[64,640]{1,0:T(8,128)(2,1)S(1)}, u32[]{:S(2)}, u32[]{:S(2)}) collective-permute-start(bf16[64,640]{1,0:T(8,128)(2,1)S(1)} %collective-permute-done.1.refs_1_), channel_id=1, source_target_pairs={{0,2},{1,3},{2,0},{3,1},{4,6},{5,7},{6,4},{7,5},{8,10},{9,11},{10,... | collective-permute-start | bytes 245768 | tf_op jit(solution)/shard_map/ppermute | solution.py:252
  11.9 5.6 %collective-permute-start.4 = (bf16[64,640]{1,0:T(8,128)(2,1)S(1)}, bf16[64,640]{1,0:T(8,128)(2,1)S(1)}, u32[]{:S(2)}, u32[]{:S(2)}) collective-permute-start(bf16[64,640]{1,0:T(8,128)(2,1)S(1)} %collective-permute-done.3.refs_2_), channel_id=1, source_target_pairs={{0,2},{1,3},{2,0},{3,1},{4,6},{5,7},{6,4},{7,5},{8,10},{9,11},{10,... | collective-permute-start | bytes 245768 | tf_op jit(solution)/shard_map/ppermute | solution.py:252
  13.5 4.4 %collective-permute-start.6 = (bf16[64,640]{1,0:T(8,128)(2,1)S(1)}, bf16[64,640]{1,0:T(8,128)(2,1)S(1)}, u32[]{:S(2)}, u32[]{:S(2)}) collective-permute-start(bf16[64,640]{1,0:T(8,128)(2,1)S(1)} %collective-permute-done.5.refs_3_), channel_id=1, source_target_pairs={{0,2},{1,3},{2,0},{3,1},{4,6},{5,7},{6,4},{7,5},{8,10},{9,11},{10,... | collective-permute-start | bytes 245768 | tf_op jit(solution)/shard_map/ppermute | solution.py:252
  15.1 1.2 %collective-permute-start.8 = (bf16[128,128]{1,0:T(8,128)(2,1)S(1)}, bf16[128,128]{1,0:T(8,128)(2,1)S(1)}, u32[]{:S(2)}, u32[]{:S(2)}) collective-permute-start(bf16[128,128]{1,0:T(8,128)(2,1)S(1)} %shard_map.61.refs_4_), channel_id=1, source_target_pairs={{0,1},{1,0},{2,3},{3,2},{4,5},{5,4},{6,7},{7,6},{8,9},{9,8},{10,11... | collective-permute-start | bytes 98312 | tf_op jit(solution)/shard_map/ppermute | solution.py:252
  18.0 1.2 %collective-permute-start.7 = (bf16[128,128]{1,0:T(8,128)(2,1)S(1)}, bf16[128,128]{1,0:T(8,128)(2,1)S(1)}, u32[]{:S(2)}, u32[]{:S(2)}) collective-permute-start(bf16[128,128]{1,0:T(8,128)(2,1)S(1)} %shard_map.60.mine_ref), channel_id=1, source_target_pairs={{0,1},{1,0},{2,3},{3,2},{4,5},{5,4},{6,7},{7,6},{8,9},{9,8},{10,11... | collective-permute-start | bytes 98312 | tf_op jit(solution)/shard_map/ppermute | solution.py:252
  23.3 1.2 %collective-permute-start.9 = (f32[1,1024]{1,0:T(1,128)S(1)}, f32[1,1024]{1,0:T(1,128)S(1)}, u32[]{:S(2)}, u32[]{:S(2)}) collective-permute-start(f32[1,1024]{1,0:T(1,128)S(1)} %get-tuple-element.32.mine_ref), channel_id=1, source_target_pairs={{0,1},{1,0},{2,3},{3,2},{4,5},{5,4},{6,7},{7,6},{8,9},{9,8},{10,11... | collective-permute-start | bytes 12296 | tf_op jit(solution)/shard_map/ppermute | solution.py:252
  26.8 1.2 %collective-permute-start.10 = (f32[1,1024]{1,0:T(1,128)S(1)}, f32[1,1024]{1,0:T(1,128)S(1)}, u32[]{:S(2)}, u32[]{:S(2)}) collective-permute-start(f32[1,1024]{1,0:T(1,128)S(1)} %shard_map.65.mine_ref), channel_id=1, source_target_pairs={{0,1},{1,0},{2,3},{3,2},{4,5},{5,4},{6,7},{7,6},{8,9},{9,8},{10,11... | collective-permute-start | bytes 12296 | tf_op jit(solution)/shard_map/ppermute | solution.py:252
  30.3 1.2 %collective-permute-start.11 = (f32[1,1024]{1,0:T(1,128)S(1)}, f32[1,1024]{1,0:T(1,128)S(1)}, u32[]{:S(2)}, u32[]{:S(2)}) collective-permute-start(f32[1,1024]{1,0:T(1,128)S(1)} %shard_map.66.mine_ref), channel_id=1, source_target_pairs={{0,1},{1,0},{2,3},{3,2},{4,5},{5,4},{6,7},{7,6},{8,9},{9,8},{10,11... | collective-permute-start | bytes 12296 | tf_op jit(solution)/shard_map/ppermute | solution.py:252
  34.1 1.3 %collective-permute-start.12 = (f32[72,128]{1,0:T(8,128)S(1)}, f32[72,128]{1,0:T(8,128)S(1)}, u32[]{:S(2)}, u32[]{:S(2)}) collective-permute-start(f32[72,128]{1,0:T(8,128)S(1)} %get-tuple-element.37.mine_ref), channel_id=1, source_target_pairs={{0,1},{1,0},{2,3},{3,2},{4,5},{5,4},{6,7},{7,6},{8,9},{9,8},{10,11... | collective-permute-start | bytes 110600 | tf_op jit(solution)/shard_map/ppermute | solution.py:252

commit v6 on v5

--- a/solution.py
+++ b/solution.py
@@ -90,7 +90,7 @@
         mass = terms[:chunks] + terms[chunks : 2 * chunks] + terms[2 * chunks : 3 * chunks]
         for j in range(chunks):
             at = slot * rows + j * LANES
-            mass_ref[:, at : at + LANES] = mass[j : j + 1]
+            mass_ref[:, at : at + LANES] = jnp.broadcast_to(mass[j : j + 1], (8, LANES))
 
 
 def gather_models(distances, mine_ref, other_ref, mdl_mass_ref, mdl_ref, cols_mass_ref):
@@ -121,18 +121,30 @@
     turned_ref[cols, rows] = tile.T
 
 
+def fill_wide(img_ref, rows, mdl_ref, cols, kernel_ref, turned_ref, wide_ref):
+    scores = lax.dot_general(
+        mdl_ref[...], img_ref[...], (((0,), (0,)), ((), ())), preferred_element_type=F32
+    )
+    tile = jnp.exp(scores * (inv_temp / FEAT)).astype(BF16)
+    turned_ref[cols, rows] = tile
+    kernel_ref[rows, cols] = tile.T
+    wide = tile.astype(F32)
+    wide_ref[cols, :] = wide
+    return jnp.sum(wide, axis=0, keepdims=True)
+
+
 def halves_of(extent):
     return slice(0, extent // 2), slice(extent // 2, extent)
 
 
 def build_first(distances, *refs):
     pieces, refs = refs[: len(distances)], refs[len(distances) :]
-    mine_ref, other_ref, mdl_mass_ref, kernel_ref, turned_ref = refs[:5]
-    img_ref, mass_ref, mdl_ref, cols_mass_ref = refs[5:]
+    mine_ref, other_ref, mdl_mass_ref, kernel_ref, turned_ref, wide_ref, known_ref = refs[:7]
+    img_ref, mass_ref, mdl_ref, cols_mass_ref = refs[7:]
     gather_rows(pieces, img_ref, mass_ref)
     gather_models(distances, mine_ref, other_ref, mdl_mass_ref, mdl_ref, cols_mass_ref)
     rows, cols = (halves_of(extent)[0] for extent in kernel_ref.shape)
-    fill(img_ref, rows, mdl_ref, cols, kernel_ref, turned_ref)
+    known_ref[...] = fill_wide(img_ref, rows, mdl_ref, cols, kernel_ref, turned_ref, wide_ref)
 
 
 def build_rows(count, *refs):
@@ -152,21 +164,30 @@
     img_odd_ref,
     mass_even_ref,
     mass_odd_ref,
+    known_ref,
     _kernel,
     _turned,
+    _wide,
     kernel_ref,
     turned_ref,
+    wide_ref,
     mdl_ref,
     cols_mass_ref,
     sums_ref,
+    lanes_ref,
 ):
     gather_models(distances, mine_ref, other_ref, mdl_mass_ref, mdl_ref, cols_mass_ref)
+    even, odd = halves_of(kernel_ref.shape[0])
     cols = halves_of(kernel_ref.shape[1])[1]
-    for rows, img_ref in zip(halves_of(kernel_ref.shape[0]), (img_even_ref, img_odd_ref)):
-        fill(img_ref, rows, mdl_ref, cols, kernel_ref, turned_ref)
-    ones = jnp.ones((1, kernel_ref.shape[1]), F32)
-    row_scale = row_scales(ones, (mass_even_ref, mass_odd_ref), turned_ref)
-    sums_ref[...] = matmul(row_scale.astype(BF16), kernel_ref[...])[:1]
+    fill(img_odd_ref, odd, mdl_ref, cols, kernel_ref, turned_ref)
+    rest = fill_wide(img_even_ref, even, mdl_ref, cols, kernel_ref, turned_ref, wide_ref)
+    row_scale = mass_even_ref[...] / (known_ref[...] + rest)
+    ones = jnp.ones((8, kernel_ref.shape[1]), BF16)
+    scales = (
+        lambda: row_scale,
+        lambda: mass_odd_ref[...] / matmul(ones, turned_ref[:, odd]),
+    )
+    sums_ref[...] = column_sums(scales, kernel_ref, wide_ref, lanes_ref)
 
 
 def joined(refs):
@@ -179,13 +200,51 @@
 
 def row_scales(col_scale, mass, turned_ref):
     low = jnp.broadcast_to(col_scale.astype(BF16), (8, col_scale.shape[1]))
-    return joined(mass) / matmul(low, turned_ref[...])
-
-
-def iterate(mine_ref, other_ref, ce_ref, co_ref, me_ref, mo_ref, kernel_ref, turned_ref, out_ref):
+
+    def of(mass_ref, rows):
+        return lambda: mass_ref[...] / matmul(low, turned_ref[:, rows])
+
+    return [of(*pair) for pair in zip(mass, halves_of(turned_ref.shape[1]))]
+
+
+def column_sums(scales, kernel_ref, wide_ref, lanes_ref):
+    even, odd = scales
+    scale = even().astype(BF16).astype(F32)
+    for at in range(0, wide_ref.shape[0], 8):
+        part = None
+        for lane in range(0, wide_ref.shape[1], LANES):
+            lanes = slice(lane, lane + LANES)
+            term = wide_ref[at : at + 8, lanes] * scale[:, lanes]
+            part = term if part is None else part + term
+        lanes_ref[at : at + 8, :] = part
+    sums = matmul(odd().astype(BF16), kernel_ref[halves_of(kernel_ref.shape[0])[1], :])
+    lanes = lanes_ref[...]
+    high = lanes.astype(BF16)
+    rest = (lanes - high.astype(F32)).astype(BF16)
+    ones = jnp.ones((8, LANES), BF16)
+    for part in (high, rest):
+        sums += lax.dot_general(
+            ones, part, (((1,), (1,)), ((), ())), preferred_element_type=F32
+        )
+    return sums[:1]
+
+
+def iterate(
+    mine_ref,
+    other_ref,
+    ce_ref,
+    co_ref,
+    me_ref,
+    mo_ref,
+    kernel_ref,
+    turned_ref,
+    wide_ref,
+    out_ref,
+    lanes_ref,
+):
     col_scale = scaled(mine_ref, other_ref, (ce_ref, co_ref))
-    row_scale = row_scales(col_scale, (me_ref, mo_ref), turned_ref)
-    out_ref[...] = matmul(row_scale.astype(BF16), kernel_ref[...])[:1]
+    scales = row_scales(col_scale, (me_ref, mo_ref), turned_ref)
+    out_ref[...] = column_sums(scales, kernel_ref, wide_ref, lanes_ref)
 
 
 def last(
@@ -198,20 +257,35 @@
     mo_ref,
     kernel_ref,
     turned_ref,
+    wide_ref,
     ie_ref,
     io_ref,
     out_ref,
     scale_ref,
+    lanes_ref,
 ):
     col_scale = scaled(mine_ref, other_ref, (ce_ref, co_ref))
-    row_scale = row_scales(col_scale, (me_ref, mo_ref), turned_ref)
-    scale_ref[...] = row_scale[:1, :rows]
-    sums = matmul(row_scale.astype(BF16), kernel_ref[...])[:1]
+    found = []
+
+    def kept(scale):
+        def of():
+            found.append(scale())
+            return found[-1]
+
+        return of
+
+    scales = [kept(scale) for scale in row_scales(col_scale, (me_ref, mo_ref), turned_ref)]
+    sums = column_sums(scales, kernel_ref, wide_ref, lanes_ref)
+    scale_ref[...] = found[0][:1, :rows]
     tiles = sums.shape[1] // LANES
     for slot in range(tiles):
         out_ref[slot : slot + 1, :] = sums[:, slot * LANES : (slot + 1) * LANES]
-    row_feat = (joined((ie_ref, io_ref)).astype(F32) * row_scale[:1]).astype(BF16)
-    out_ref[tiles:, :] = matmul(row_feat, kernel_ref[:, :LANES])
+    terms = None
+    for img_ref, scale, at in zip((ie_ref, io_ref), found, halves_of(kernel_ref.shape[0])):
+        row_feat = (img_ref[...].astype(F32) * scale[:1]).astype(BF16)
+        term = matmul(row_feat, kernel_ref[at, :LANES])
+        terms = term if terms is None else terms + term
+    out_ref[tiles:, :] = terms
 
 
 def finish(
@@ -245,7 +319,7 @@
     rows, share = img_feat.shape[1], mdl_feat.shape[1]
     held, models = groups * rows, count * share
     middle = groups // 2
-    even = [0, middle] + [s for s in range(2, groups, 2) if s != middle]
+    even = [0] + [s for s in range(groups - 2, 0, -2) if s != middle] + [middle]
     odd = [s + 1 for s in even]
 
     def swap(block, distance):
@@ -274,11 +348,15 @@
         mine = call(functools.partial(collect, rows), out, *blocks)
         return mine, swap(mine, 1)
 
-    halves = (shape(FEAT, held // 2, dtype=BF16), shape(1, held // 2))
+    halves = (shape(FEAT, held // 2, dtype=BF16), shape(8, held // 2))
     sides = (shape(FEAT, models // 2, dtype=BF16), shape(1, models // 2))
     whole = (shape(held, models, dtype=BF16), shape(models, held, dtype=BF16))
-    kernel, turned, img_even, mass_even, mdl_even, cols_even = call(
-        functools.partial(build_first, even), whole + halves + sides, *along, *models_of(along), cols,
+    extra = (shape(models, held // 2),)
+    lanes = [pltpu.VMEM((models, LANES), F32)]
+    kernel, turned, wide, known, img_even, mass_even, mdl_even, cols_even = call(
+        functools.partial(build_first, even),
+        whole + extra + (shape(1, held // 2),) + halves + sides,
+        *along, *models_of(along), cols,
         flops=held * models // 4 * COST,
     )
     kernel, turned, img_odd, mass_odd = call(
@@ -291,23 +369,26 @@
         alias={len(across) + 1: 0, len(across) + 2: 1},
         flops=held * models // 4 * COST,
     )
-    kernel, turned, mdl_odd, cols_odd, sums = call(
+    kernel, turned, wide, mdl_odd, cols_odd, sums = call(
         functools.partial(build_cols, odd),
-        whole + sides + (shape(1, models),),
+        whole + extra + sides + (shape(1, models),),
         *models_of(across),
         cols,
         img_even,
         img_odd,
         mass_even,
         mass_odd,
+        known,
         kernel,
         turned,
-        alias={7: 0, 8: 1},
+        wide,
+        alias={8: 0, 9: 1, 10: 2},
+        scratch=lanes,
         flops=held * models * COST,
     )
-    fixed = (cols_even, cols_odd, mass_even, mass_odd, kernel, turned)
+    fixed = (cols_even, cols_odd, mass_even, mass_odd, kernel, turned, wide)
     for iteration in range(1, ITERS - 1):
-        sums = call(iterate, shape(1, models), sums, swap(sums, 1), *fixed)
+        sums = call(iterate, shape(1, models), sums, swap(sums, 1), *fixed, scratch=lanes)
     both, row_scale = call(
         functools.partial(last, rows),
         (shape(models // LANES + FEAT, LANES), shape(1, rows)),
@@ -316,6 +397,7 @@
         *fixed,
         img_even,
         img_odd,
+        scratch=lanes,
     )
     return call(
         finish,
@@ -365,7 +447,7 @@
 def shards(count, img_feat, mdl_feat, img_mass, mdl_mass):
     groups = count // 2
     rows, share = img_feat.shape[1], mdl_feat.shape[1]
-    resident = 2 * 2 * (groups * rows) * (count * share)
+    resident = (2 + 2 + 4 // 2) * (groups * rows) * (count * share)
     fits = (
         count == 2 * groups
         and groups >= 4

time: 36.5 us -> 35.5 us (0.973)
  Pallas kernels: 15.5 us -> 14.7 us
    pallas_call x10, Pallas kernels: 15.5 us -> 14.7 us  [call(): pl.pallas_call(body, out_shape=outs, in_specs=specs or [WHOLE] * len(args...]
  transfers between devices with their start and end apart: 13 -> 13, of which waited for: 9 -> 9; matrix products, arithmetic and copies ran while one was open for 0% -> 0% of each run, Pallas kernels for 6% -> 7%
where the time goes in v6:
time: 35.5 us; the launch traced here: 35.4 us
  Pallas kernels  14.7 us (41%)
  starting transfers between devices  12.9 us (36%)
  waiting for transfers between devices  7.14 us (20%)
  between operations  0.7 us (2%)
    pallas_call x10, Pallas kernels, call(): pl.pallas_call(body, out_shape=outs, in_specs=specs or [WHOLE] * len(args...  14.7 us
    ppermute x13, starting transfers between devices, swap(): return lax.ppermute(block, 'img', [(i, i ^ distance) for i in range(count)])  12.9 us
    ppermute x13, waiting for transfers between devices, swap(): return lax.ppermute(block, 'img', [(i, i ^ distance) for i in range(count)])  7.14 us
  transfers between devices with their start and end apart: 13, of which 9 were waited for; matrix products, arithmetic and copies ran while one was open for 0% of the time, Pallas kernels for 7%

profile of v6, /device:TPU:0, one launch (start us, length us, event | category | flops | bytes accessed | tf_op | source)
XLA Modules:
  0.0 35.4 jit_solution(17745926677336465543)
XLA Ops:
  0.6 1.0 %shard_map.59 = (bf16[64,640]{1,0:T(8,128)(2,1)S(1)}, f32[8,128]{1,0:T(8,128)S(1)}) custom-call(bf16[64,512]{1,0:T(8,128)(2,1)} %img_hbm.1, bf16[64,64]{1,0:T(8,128)(2,1)} %mdl_hbm.1, f32[4,128]{1,0:T(4,128)} %bitcast.3, f32[8,128]{1,0:T(8,128)} %bitcast.2), custom_call_target="tpu_custom_call" | custom-call | tf_op jit(solution)/shard_map/pallas_call | solution.py:24
  1.6 4.1 %collective-permute-start.5 = (bf16[64,640]{1,0:T(8,128)(2,1)S(1)}, bf16[64,640]{1,0:T(8,128)(2,1)S(1)}, u32[]{:S(2)}, u32[]{:S(2)}) collective-permute-start(bf16[64,640]{1,0:T(8,128)(2,1)S(1)} %get-tuple-element.24.refs_0_), channel_id=1, source_target_pairs={{0,8},{1,9},{2,10},{3,11},{4,12},{5,13},{6,14},{7,15},{8,0},{9,1},... | collective-permute-start | bytes 245768 | tf_op jit(solution)/shard_map/ppermute | solution.py:326
  5.7 1.6 %collective-permute-start.3 = (bf16[64,640]{1,0:T(8,128)(2,1)S(1)}, bf16[64,640]{1,0:T(8,128)(2,1)S(1)}, u32[]{:S(2)}, u32[]{:S(2)}) collective-permute-start(bf16[64,640]{1,0:T(8,128)(2,1)S(1)} %get-tuple-element.24.refs_0_), channel_id=1, source_target_pairs={{0,4},{1,5},{2,6},{3,7},{4,0},{5,1},{6,2},{7,3},{8,12},{9,13},{10,... | collective-permute-start | bytes 245768 | tf_op jit(solution)/shard_map/ppermute | solution.py:326
  7.3 0.0 collective-permute-start.1
  7.3 1.7 %collective-permute-start = (bf16[64,640]{1,0:T(8,128)(2,1)S(1)}, bf16[64,640]{1,0:T(8,128)(2,1)S(1)}, u32[]{:S(2)}, u32[]{:S(2)}) collective-permute-start(bf16[64,640]{1,0:T(8,128)(2,1)S(1)} %get-tuple-element.24.refs_0_), channel_id=1, source_target_pairs={{0,2},{1,3},{2,0},{3,1},{4,6},{5,7},{6,4},{7,5},{8,10},{9,11},{10,... | collective-permute-start | bytes 245768 | tf_op jit(solution)/shard_map/ppermute | solution.py:326
  9.0 0.7 %collective-permute-done.5.refs_3_ = bf16[64,640]{1,0:T(8,128)(2,1)S(1)} collective-permute-done((bf16[64,640]{1,0:T(8,128)(2,1)S(1)}, bf16[64,640]{1,0:T(8,128)(2,1)S(1)}, u32[]{:S(2)}, u32[]{:S(2)}) %collective-permute-start.5) | collective-permute-done | bytes 81952 | tf_op jit(solution)/shard_map/ppermute | solution.py:326
  9.7 2.2 %collective-permute-start.6 = (bf16[64,640]{1,0:T(8,128)(2,1)S(1)}, bf16[64,640]{1,0:T(8,128)(2,1)S(1)}, u32[]{:S(2)}, u32[]{:S(2)}) collective-permute-start(bf16[64,640]{1,0:T(8,128)(2,1)S(1)} %collective-permute-done.5.refs_3_), channel_id=1, source_target_pairs={{0,2},{1,3},{2,0},{3,1},{4,6},{5,7},{6,4},{7,5},{8,10},{9,11},{10,... | collective-permute-start | bytes 245768 | tf_op jit(solution)/shard_map/ppermute | solution.py:326
  11.9 0.0 collective-permute-done.3.refs_2_
  11.9 0.0 collective-permute-start.4
  12.0 1.6 %collective-permute-done.1.refs_1_ = bf16[64,640]{1,0:T(8,128)(2,1)S(1)} collective-permute-done((bf16[64,640]{1,0:T(8,128)(2,1)S(1)}, bf16[64,640]{1,0:T(8,128)(2,1)S(1)}, u32[]{:S(2)}, u32[]{:S(2)}) %collective-permute-start.1) | collective-permute-done | bytes 81952 | tf_op jit(solution)/shard_map/ppermute | solution.py:326
  13.5 1.6 %collective-permute-start.2 = (bf16[64,640]{1,0:T(8,128)(2,1)S(1)}, bf16[64,640]{1,0:T(8,128)(2,1)S(1)}, u32[]{:S(2)}, u32[]{:S(2)}) collective-permute-start(bf16[64,640]{1,0:T(8,128)(2,1)S(1)} %collective-permute-done.1.refs_1_), channel_id=1, source_target_pairs={{0,2},{1,3},{2,0},{3,1},{4,6},{5,7},{6,4},{7,5},{8,10},{9,11},{10,... | collective-permute-start | bytes 245768 | tf_op jit(solution)/shard_map/ppermute | solution.py:326
  15.1 0.0 collective-permute-start.8
  15.1 1.2 %collective-permute-done.8.refs_5_ = bf16[128,128]{1,0:T(8,128)(2,1)S(1)} collective-permute-done((bf16[128,128]{1,0:T(8,128)(2,1)S(1)}, bf16[128,128]{1,0:T(8,128)(2,1)S(1)}, u32[]{:S(2)}, u32[]{:S(2)}) %collective-permute-start.8) | collective-permute-done | bytes 32800 | tf_op jit(solution)/shard_map/ppermute | solution.py:326
  16.3 1.4 %shard_map.62 = (bf16[4096,1024]{1,0:T(8,128)(2,1)S(1)}, bf16[1024,4096]{1,0:T(8,128)(2,1)S(1)}, f32[1024,2048]{1,0:T(8,128)S(1)}, f32[1,2048]{1,0:T(1,128)S(1)}...) custom-call(bf16[64,640]{1,0:T(8,128)(2,1)S(1)} %get-tuple-element.2, ...), custom_call_target="tpu_custom_call" | custom-call | flops 419430400 | bytes 819200 | tf_op jit(solution)/shard_map/pallas_call | solution.py:24
  17.7 0.0 collective-permute-done.refs_0_
  17.8 0.0 collective-permute-done.6.refs_3_
  17.8 0.0 collective-permute-done.4.refs_2_
  17.8 0.2 collective-permute-done.2.refs_1_
  18.0 0.0 collective-permute-start.7
  18.0 1.1 %shard_map.63 = (bf16[4096,1024]{1,0:T(8,128)(2,1)S(1)}, bf16[1024,4096]{1,0:T(8,128)(2,1)S(1)}, bf16[64,2048]{1,0:T(8,128)(2,1)S(1)}, f32[8,2048]{1,0:T(8,128)S(1)}) custom-call(bf16[64,640]{1,0:T(8,128)(2,1)S(1)} %collective-permute-done.refs_0_, bf16[64,640]{1,0:T(8,128)(2,1)S(1)} %collective-permute-done.2.refs_1_, ...), custom_call_target="tpu_custom_call", output_to_operand_aliasing={{0}: (5, {}), {1}: (6, {})} | custom-call | flops 419430400 | bytes 819200 | tf_op jit(solution)/shard_map/pallas_call | solution.py:24
  19.1 0.1 collective-permute-done.7.other_ref
  19.2 3.9 %shard_map.64 = (bf16[4096,1024]{1,0:T(8,128)(2,1)S(1)}, bf16[1024,4096]{1,0:T(8,128)(2,1)S(1)}, f32[1024,2048]{1,0:T(8,128)S(1)}, bf16[64,512]{1,0:T(8,128)(2,1...) custom-call(bf16[128,128]{1,0:T(8,128)(2,1)S(1)} %shard_map.60.mine_, ...), custom_call_target="tpu_custom_call", output_to_operand_aliasing={{0}: (8, {}), {1}: (9, {}), {2}: (10, {})} | custom-call | flops 1677721600 | bytes 3276800 | tf_op jit(solution)/shard_map/pallas_call | solution.py:24
  23.1 0.4 %collective-permute-start.9 = (f32[1,1024]{1,0:T(1,128)S(1)}, f32[1,1024]{1,0:T(1,128)S(1)}, u32[]{:S(2)}, u32[]{:S(2)}) collective-permute-start(f32[1,1024]{1,0:T(1,128)S(1)} %get-tuple-element.37.mine_ref), channel_id=1, source_target_pairs={{0,1},{1,0},{2,3},{3,2},{4,5},{5,4},{6,7},{7,6},{8,9},{9,8},{10,11... | collective-permute-start | bytes 12296 | tf_op jit(solution)/shard_map/ppermute | solution.py:326
  23.6 0.8 %collective-permute-done.9.other_ref = f32[1,1024]{1,0:T(1,128)S(1)} collective-permute-done((f32[1,1024]{1,0:T(1,128)S(1)}, f32[1,1024]{1,0:T(1,128)S(1)}, u32[]{:S(2)}, u32[]{:S(2)}) %collective-permute-start.9) | collective-permute-done | bytes 4128 | tf_op jit(solution)/shard_map/ppermute | solution.py:326
  24.4 2.0 %shard_map.65.mine_ref = f32[1,1024]{1,0:T(1,128)S(1)} custom-call(f32[1,1024]{1,0:T(1,128)S(1)} %get-tuple-element.37.mine_ref, f32[1,1024]{1,0:T(1,128)S(1)} %collective-permute-done.9.other_ref, f32[1,512]{1,0:T(1,128)S(1)} %get-tuple-element.38.ce_ref, f32[1,512]{1,0:T(1,128)S(1)} %get-tuple-element.39.co_ref, ...), custom_call_target="tpu_custom_call" | custom-call | tf_op jit(solution)/shard_map/pallas_call | solution.py:24
  26.4 0.4 %collective-permute-start.10 = (f32[1,1024]{1,0:T(1,128)S(1)}, f32[1,1024]{1,0:T(1,128)S(1)}, u32[]{:S(2)}, u32[]{:S(2)}) collective-permute-start(f32[1,1024]{1,0:T(1,128)S(1)} %shard_map.65.mine_ref), channel_id=1, source_target_pairs={{0,1},{1,0},{2,3},{3,2},{4,5},{5,4},{6,7},{7,6},{8,9},{9,8},{10,11... | collective-permute-start | bytes 12296 | tf_op jit(solution)/shard_map/ppermute | solution.py:326
  26.8 0.8 %collective-permute-done.10.other_ref = f32[1,1024]{1,0:T(1,128)S(1)} collective-permute-done((f32[1,1024]{1,0:T(1,128)S(1)}, f32[1,1024]{1,0:T(1,128)S(1)}, u32[]{:S(2)}, u32[]{:S(2)}) %collective-permute-start.10) | collective-permute-done | bytes 4128 | tf_op jit(solution)/shard_map/ppermute | solution.py:326
  27.6 2.0 %shard_map.66.mine_ref = f32[1,1024]{1,0:T(1,128)S(1)} custom-call(f32[1,1024]{1,0:T(1,128)S(1)} %shard_map.65.mine_ref, f32[1,1024]{1,0:T(1,128)S(1)} %collective-permute-done.10.other_ref, f32[1,512]{1,0:T(1,128)S(1)} %get-tuple-element.38.ce_ref, f32[1,512]{1,0:T(1,128)S(1)} %get-tuple-element.39.co_ref, ...), custom_call_target="tpu_custom_call" | custom-call | tf_op jit(solution)/shard_map/pallas_call | solution.py:24
  29.6 0.4 %collective-permute-start.11 = (f32[1,1024]{1,0:T(1,128)S(1)}, f32[1,1024]{1,0:T(1,128)S(1)}, u32[]{:S(2)}, u32[]{:S(2)}) collective-permute-start(f32[1,1024]{1,0:T(1,128)S(1)} %shard_map.66.mine_ref), channel_id=1, source_target_pairs={{0,1},{1,0},{2,3},{3,2},{4,5},{5,4},{6,7},{7,6},{8,9},{9,8},{10,11... | collective-permute-start | bytes 12296 | tf_op jit(solution)/shard_map/ppermute | solution.py:326
  30.0 0.8 %collective-permute-done.11.other_ref = f32[1,1024]{1,0:T(1,128)S(1)} collective-permute-done((f32[1,1024]{1,0:T(1,128)S(1)}, f32[1,1024]{1,0:T(1,128)S(1)}, u32[]{:S(2)}, u32[]{:S(2)}) %collective-permute-start.11) | collective-permute-done | bytes 4128 | tf_op jit(solution)/shard_map/ppermute | solution.py:326
  30.8 2.3 %shard_map.67 = (f32[72,128]{1,0:T(8,128)S(1)}, f32[1,512]{1,0:T(1,128)S(1)}) custom-call(f32[1,1024]{1,0:T(1,128)S(1)} %shard_map.66.mine_ref, f32[1,1024]{1,0:T(1,128)S(1)} %collective-permute-done.11.other_ref, f32[1,512]{1,0:T(1,128)S(1)} %get-tuple-element.38.ce_ref, f32[1,512]{1,0:T(1,128)S(1)} %get-tuple-element.39.co_ref, ...), custom_call_target="tpu_custom_call" | custom-call | tf_op jit(solution)/shard_map/pallas_call | solution.py:24
  33.1 0.4 %collective-permute-start.12 = (f32[72,128]{1,0:T(8,128)S(1)}, f32[72,128]{1,0:T(8,128)S(1)}, u32[]{:S(2)}, u32[]{:S(2)}) collective-permute-start(f32[72,128]{1,0:T(8,128)S(1)} %get-tuple-element.43.mine_ref), channel_id=1, source_target_pairs={{0,1},{1,0},{2,3},{3,2},{4,5},{5,4},{6,7},{7,6},{8,9},{9,8},{10,11... | collective-permute-start | bytes 110600 | tf_op jit(solution)/shard_map/ppermute | solution.py:326
  33.5 0.9 %collective-permute-done.12.other_ref = f32[72,128]{1,0:T(8,128)S(1)} collective-permute-done((f32[72,128]{1,0:T(8,128)S(1)}, f32[72,128]{1,0:T(8,128)S(1)}, u32[]{:S(2)}, u32[]{:S(2)}) %collective-permute-start.12) | collective-permute-done | bytes 36896 | tf_op jit(solution)/shard_map/ppermute | solution.py:326
  34.4 1.0 %shard_map.68 = (f32[64,512]{1,0:T(8,128)}, f32[64,64]{1,0:T(8,128)}) custom-call(f32[72,128]{1,0:T(8,128)S(1)} %get-tuple-element.43.mine_ref, f32[72,128]{1,0:T(8,128)S(1)} %collective-permute-done.12.other_ref, f32[1,512]{1,0:T(1,128)S(1)} %get-tuple-element.38.ce_ref, f32[1,512]{1,0:T(1,128)S(1)} %get-tuple-element.39.co_ref, ...), custom_call_target="tpu_custom_call" | custom-call | tf_op jit(solution)/shard_map/pallas_call | solution.py:24
  (2 shorter events, 0.0 us)
Async XLA Ops:
  1.6 8.1 %collective-permute-start.5 = (bf16[64,640]{1,0:T(8,128)(2,1)S(1)}, bf16[64,640]{1,0:T(8,128)(2,1)S(1)}, u32[]{:S(2)}, u32[]{:S(2)}) collective-permute-start(bf16[64,640]{1,0:T(8,128)(2,1)S(1)} %get-tuple-element.24.refs_0_), channel_id=1, source_target_pairs={{0,8},{1,9},{2,10},{3,11},{4,12},{5,13},{6,14},{7,15},{8,0},{9,1},... | collective-permute-start | bytes 245768 | tf_op jit(solution)/shard_map/ppermute | solution.py:326
  5.7 6.2 %collective-permute-start.3 = (bf16[64,640]{1,0:T(8,128)(2,1)S(1)}, bf16[64,640]{1,0:T(8,128)(2,1)S(1)}, u32[]{:S(2)}, u32[]{:S(2)}) collective-permute-start(bf16[64,640]{1,0:T(8,128)(2,1)S(1)} %get-tuple-element.24.refs_0_), channel_id=1, source_target_pairs={{0,4},{1,5},{2,6},{3,7},{4,0},{5,1},{6,2},{7,3},{8,12},{9,13},{10,... | collective-permute-start | bytes 245768 | tf_op jit(solution)/shard_map/ppermute | solution.py:326
  7.3 6.2 %collective-permute-start.1 = (bf16[64,640]{1,0:T(8,128)(2,1)S(1)}, bf16[64,640]{1,0:T(8,128)(2,1)S(1)}, u32[]{:S(2)}, u32[]{:S(2)}) collective-permute-start(bf16[64,640]{1,0:T(8,128)(2,1)S(1)} %get-tuple-element.24.refs_0_), channel_id=1, source_target_pairs={{0,12},{1,13},{2,14},{3,15},{4,8},{5,9},{6,10},{7,11},{8,4},{9,5},... | collective-permute-start | bytes 245768 | tf_op jit(solution)/shard_map/ppermute | solution.py:326
  7.3 10.4 %collective-permute-start = (bf16[64,640]{1,0:T(8,128)(2,1)S(1)}, bf16[64,640]{1,0:T(8,128)(2,1)S(1)}, u32[]{:S(2)}, u32[]{:S(2)}) collective-permute-start(bf16[64,640]{1,0:T(8,128)(2,1)S(1)} %get-tuple-element.24.refs_0_), channel_id=1, source_target_pairs={{0,2},{1,3},{2,0},{3,1},{4,6},{5,7},{6,4},{7,5},{8,10},{9,11},{10,... | collective-permute-start | bytes 245768 | tf_op jit(solution)/shard_map/ppermute | solution.py:326
  9.7 8.0 %collective-permute-start.6 = (bf16[64,640]{1,0:T(8,128)(2,1)S(1)}, bf16[64,640]{1,0:T(8,128)(2,1)S(1)}, u32[]{:S(2)}, u32[]{:S(2)}) collective-permute-start(bf16[64,640]{1,0:T(8,128)(2,1)S(1)} %collective-permute-done.5.refs_3_), channel_id=1, source_target_pairs={{0,2},{1,3},{2,0},{3,1},{4,6},{5,7},{6,4},{7,5},{8,10},{9,11},{10,... | collective-permute-start | bytes 245768 | tf_op jit(solution)/shard_map/ppermute | solution.py:326
  11.9 5.8 %collective-permute-start.4 = (bf16[64,640]{1,0:T(8,128)(2,1)S(1)}, bf16[64,640]{1,0:T(8,128)(2,1)S(1)}, u32[]{:S(2)}, u32[]{:S(2)}) collective-permute-start(bf16[64,640]{1,0:T(8,128)(2,1)S(1)} %collective-permute-done.3.refs_2_), channel_id=1, source_target_pairs={{0,2},{1,3},{2,0},{3,1},{4,6},{5,7},{6,4},{7,5},{8,10},{9,11},{10,... | collective-permute-start | bytes 245768 | tf_op jit(solution)/shard_map/ppermute | solution.py:326
  13.5 4.4 %collective-permute-start.2 = (bf16[64,640]{1,0:T(8,128)(2,1)S(1)}, bf16[64,640]{1,0:T(8,128)(2,1)S(1)}, u32[]{:S(2)}, u32[]{:S(2)}) collective-permute-start(bf16[64,640]{1,0:T(8,128)(2,1)S(1)} %collective-permute-done.1.refs_1_), channel_id=1, source_target_pairs={{0,2},{1,3},{2,0},{3,1},{4,6},{5,7},{6,4},{7,5},{8,10},{9,11},{10,... | collective-permute-start | bytes 245768 | tf_op jit(solution)/shard_map/ppermute | solution.py:326
  15.1 1.2 %collective-permute-start.8 = (bf16[128,128]{1,0:T(8,128)(2,1)S(1)}, bf16[128,128]{1,0:T(8,128)(2,1)S(1)}, u32[]{:S(2)}, u32[]{:S(2)}) collective-permute-start(bf16[128,128]{1,0:T(8,128)(2,1)S(1)} %shard_map.61.refs_4_), channel_id=1, source_target_pairs={{0,1},{1,0},{2,3},{3,2},{4,5},{5,4},{6,7},{7,6},{8,9},{9,8},{10,11... | collective-permute-start | bytes 98312 | tf_op jit(solution)/shard_map/ppermute | solution.py:326
  18.0 1.2 %collective-permute-start.7 = (bf16[128,128]{1,0:T(8,128)(2,1)S(1)}, bf16[128,128]{1,0:T(8,128)(2,1)S(1)}, u32[]{:S(2)}, u32[]{:S(2)}) collective-permute-start(bf16[128,128]{1,0:T(8,128)(2,1)S(1)} %shard_map.60.mine_ref), channel_id=1, source_target_pairs={{0,1},{1,0},{2,3},{3,2},{4,5},{5,4},{6,7},{7,6},{8,9},{9,8},{10,11... | collective-permute-start | bytes 98312 | tf_op jit(solution)/shard_map/ppermute | solution.py:326
  23.1 1.3 %collective-permute-start.9 = (f32[1,1024]{1,0:T(1,128)S(1)}, f32[1,1024]{1,0:T(1,128)S(1)}, u32[]{:S(2)}, u32[]{:S(2)}) collective-permute-start(f32[1,1024]{1,0:T(1,128)S(1)} %get-tuple-element.37.mine_ref), channel_id=1, source_target_pairs={{0,1},{1,0},{2,3},{3,2},{4,5},{5,4},{6,7},{7,6},{8,9},{9,8},{10,11... | collective-permute-start | bytes 12296 | tf_op jit(solution)/shard_map/ppermute | solution.py:326
  26.4 1.2 %collective-permute-start.10 = (f32[1,1024]{1,0:T(1,128)S(1)}, f32[1,1024]{1,0:T(1,128)S(1)}, u32[]{:S(2)}, u32[]{:S(2)}) collective-permute-start(f32[1,1024]{1,0:T(1,128)S(1)} %shard_map.65.mine_ref), channel_id=1, source_target_pairs={{0,1},{1,0},{2,3},{3,2},{4,5},{5,4},{6,7},{7,6},{8,9},{9,8},{10,11... | collective-permute-start | bytes 12296 | tf_op jit(solution)/shard_map/ppermute | solution.py:326
  29.6 1.2 %collective-permute-start.11 = (f32[1,1024]{1,0:T(1,128)S(1)}, f32[1,1024]{1,0:T(1,128)S(1)}, u32[]{:S(2)}, u32[]{:S(2)}) collective-permute-start(f32[1,1024]{1,0:T(1,128)S(1)} %shard_map.66.mine_ref), channel_id=1, source_target_pairs={{0,1},{1,0},{2,3},{3,2},{4,5},{5,4},{6,7},{7,6},{8,9},{9,8},{10,11... | collective-permute-start | bytes 12296 | tf_op jit(solution)/shard_map/ppermute | solution.py:326
  33.1 1.3 %collective-permute-start.12 = (f32[72,128]{1,0:T(8,128)S(1)}, f32[72,128]{1,0:T(8,128)S(1)}, u32[]{:S(2)}, u32[]{:S(2)}) collective-permute-start(f32[72,128]{1,0:T(8,128)S(1)} %get-tuple-element.43.mine_ref), channel_id=1, source_target_pairs={{0,1},{1,0},{2,3},{3,2},{4,5},{5,4},{6,7},{7,6},{8,9},{9,8},{10,11... | collective-permute-start | bytes 110600 | tf_op jit(solution)/shard_map/ppermute | solution.py:326

commit v7 on v6

--- a/solution.py
+++ b/solution.py
@@ -7,6 +7,7 @@
 from jax.sharding import PartitionSpec as P
 
 FEAT = 64
+LOG2E = 1.4426950408889634
 ITERS = 4
 LANES = 128
 BF16 = jnp.bfloat16
@@ -116,7 +117,7 @@
     scores = lax.dot_general(
         img_ref[...], mdl_ref[...], (((0,), (0,)), ((), ())), preferred_element_type=F32
     )
-    tile = jnp.exp(scores * (inv_temp / FEAT)).astype(BF16)
+    tile = jnp.exp2(scores * (inv_temp / FEAT * LOG2E)).astype(BF16)
     kernel_ref[rows, cols] = tile
     turned_ref[cols, rows] = tile.T
 
@@ -125,7 +126,7 @@
     scores = lax.dot_general(
         mdl_ref[...], img_ref[...], (((0,), (0,)), ((), ())), preferred_element_type=F32
     )
-    tile = jnp.exp(scores * (inv_temp / FEAT)).astype(BF16)
+    tile = jnp.exp2(scores * (inv_temp / FEAT * LOG2E)).astype(BF16)
     turned_ref[cols, rows] = tile
     kernel_ref[rows, cols] = tile.T
     wide = tile.astype(F32)
@@ -221,11 +222,9 @@
     lanes = lanes_ref[...]
     high = lanes.astype(BF16)
     rest = (lanes - high.astype(F32)).astype(BF16)
-    ones = jnp.ones((8, LANES), BF16)
-    for part in (high, rest):
-        sums += lax.dot_general(
-            ones, part, (((1,), (1,)), ((), ())), preferred_element_type=F32
-        )
+    both = jnp.concatenate([high, rest], axis=1)
+    ones = jnp.ones((8, 2 * LANES), BF16)
+    sums += lax.dot_general(ones, both, (((1,), (1,)), ((), ())), preferred_element_type=F32)
     return sums[:1]
 
 

time: 35.5 us -> 35.1 us (0.989)
  Pallas kernels: 14.7 us -> 14.3 us
    pallas_call x10, Pallas kernels: 14.7 us -> 14.3 us  [call(): pl.pallas_call(body, out_shape=outs, in_specs=specs or [WHOLE] * len(args...]
where the time goes in v7:
time: 35.1 us; the launch traced here: 34.9 us
  Pallas kernels  14.3 us (41%)
  starting transfers between devices  12.6 us (36%)
  waiting for transfers between devices  7.39 us (21%)
  between operations  0.71 us (2%)
    pallas_call x10, Pallas kernels, call(): pl.pallas_call(body, out_shape=outs, in_specs=specs or [WHOLE] * len(args...  14.3 us
    ppermute x13, starting transfers between devices, swap(): return lax.ppermute(block, 'img', [(i, i ^ distance) for i in range(count)])  12.6 us
    ppermute x13, waiting for transfers between devices, swap(): return lax.ppermute(block, 'img', [(i, i ^ distance) for i in range(count)])  7.39 us
  transfers between devices with their start and end apart: 13, of which 9 were waited for; matrix products, arithmetic and copies ran while one was open for 0% of the time, Pallas kernels for 7%

profile of v7, /device:TPU:0, one launch (start us, length us, event | category | flops | bytes accessed | tf_op | source)
XLA Modules:
  0.0 34.9 jit_solution(11894633613255752869)
XLA Ops:
  0.6 1.0 %shard_map.59 = (bf16[64,640]{1,0:T(8,128)(2,1)S(1)}, f32[8,128]{1,0:T(8,128)S(1)}) custom-call(bf16[64,512]{1,0:T(8,128)(2,1)} %img_hbm.1, bf16[64,64]{1,0:T(8,128)(2,1)} %mdl_hbm.1, f32[4,128]{1,0:T(4,128)} %bitcast.3, f32[8,128]{1,0:T(8,128)} %bitcast.2), custom_call_target="tpu_custom_call" | custom-call | tf_op jit(solution)/shard_map/pallas_call | solution.py:25
  1.6 4.1 %collective-permute-start.5 = (bf16[64,640]{1,0:T(8,128)(2,1)S(1)}, bf16[64,640]{1,0:T(8,128)(2,1)S(1)}, u32[]{:S(2)}, u32[]{:S(2)}) collective-permute-start(bf16[64,640]{1,0:T(8,128)(2,1)S(1)} %get-tuple-element.24.refs_0_), channel_id=1, source_target_pairs={{0,8},{1,9},{2,10},{3,11},{4,12},{5,13},{6,14},{7,15},{8,0},{9,1},... | collective-permute-start | bytes 245768 | tf_op jit(solution)/shard_map/ppermute | solution.py:325
  5.7 1.6 %collective-permute-start.3 = (bf16[64,640]{1,0:T(8,128)(2,1)S(1)}, bf16[64,640]{1,0:T(8,128)(2,1)S(1)}, u32[]{:S(2)}, u32[]{:S(2)}) collective-permute-start(bf16[64,640]{1,0:T(8,128)(2,1)S(1)} %get-tuple-element.24.refs_0_), channel_id=1, source_target_pairs={{0,4},{1,5},{2,6},{3,7},{4,0},{5,1},{6,2},{7,3},{8,12},{9,13},{10,... | collective-permute-start | bytes 245768 | tf_op jit(solution)/shard_map/ppermute | solution.py:325
  7.3 0.0 collective-permute-start.1
  7.3 1.7 %collective-permute-start = (bf16[64,640]{1,0:T(8,128)(2,1)S(1)}, bf16[64,640]{1,0:T(8,128)(2,1)S(1)}, u32[]{:S(2)}, u32[]{:S(2)}) collective-permute-start(bf16[64,640]{1,0:T(8,128)(2,1)S(1)} %get-tuple-element.24.refs_0_), channel_id=1, source_target_pairs={{0,2},{1,3},{2,0},{3,1},{4,6},{5,7},{6,4},{7,5},{8,10},{9,11},{10,... | collective-permute-start | bytes 245768 | tf_op jit(solution)/shard_map/ppermute | solution.py:325
  9.0 0.7 %collective-permute-done.5.refs_3_ = bf16[64,640]{1,0:T(8,128)(2,1)S(1)} collective-permute-done((bf16[64,640]{1,0:T(8,128)(2,1)S(1)}, bf16[64,640]{1,0:T(8,128)(2,1)S(1)}, u32[]{:S(2)}, u32[]{:S(2)}) %collective-permute-start.5) | collective-permute-done | bytes 81952 | tf_op jit(solution)/shard_map/ppermute | solution.py:325
  9.7 2.2 %collective-permute-start.6 = (bf16[64,640]{1,0:T(8,128)(2,1)S(1)}, bf16[64,640]{1,0:T(8,128)(2,1)S(1)}, u32[]{:S(2)}, u32[]{:S(2)}) collective-permute-start(bf16[64,640]{1,0:T(8,128)(2,1)S(1)} %collective-permute-done.5.refs_3_), channel_id=1, source_target_pairs={{0,2},{1,3},{2,0},{3,1},{4,6},{5,7},{6,4},{7,5},{8,10},{9,11},{10,... | collective-permute-start | bytes 245768 | tf_op jit(solution)/shard_map/ppermute | solution.py:325
  11.9 0.0 collective-permute-done.3.refs_2_
  11.9 0.0 collective-permute-start.4
  12.0 1.6 %collective-permute-done.1.refs_1_ = bf16[64,640]{1,0:T(8,128)(2,1)S(1)} collective-permute-done((bf16[64,640]{1,0:T(8,128)(2,1)S(1)}, bf16[64,640]{1,0:T(8,128)(2,1)S(1)}, u32[]{:S(2)}, u32[]{:S(2)}) %collective-permute-start.1) | collective-permute-done | bytes 81952 | tf_op jit(solution)/shard_map/ppermute | solution.py:325
  13.5 1.6 %collective-permute-start.2 = (bf16[64,640]{1,0:T(8,128)(2,1)S(1)}, bf16[64,640]{1,0:T(8,128)(2,1)S(1)}, u32[]{:S(2)}, u32[]{:S(2)}) collective-permute-start(bf16[64,640]{1,0:T(8,128)(2,1)S(1)} %collective-permute-done.1.refs_1_), channel_id=1, source_target_pairs={{0,2},{1,3},{2,0},{3,1},{4,6},{5,7},{6,4},{7,5},{8,10},{9,11},{10,... | collective-permute-start | bytes 245768 | tf_op jit(solution)/shard_map/ppermute | solution.py:325
  15.1 0.0 collective-permute-start.8
  15.1 1.2 %collective-permute-done.8.refs_5_ = bf16[128,128]{1,0:T(8,128)(2,1)S(1)} collective-permute-done((bf16[128,128]{1,0:T(8,128)(2,1)S(1)}, bf16[128,128]{1,0:T(8,128)(2,1)S(1)}, u32[]{:S(2)}, u32[]{:S(2)}) %collective-permute-start.8) | collective-permute-done | bytes 32800 | tf_op jit(solution)/shard_map/ppermute | solution.py:325
  16.3 1.4 %shard_map.62 = (bf16[4096,1024]{1,0:T(8,128)(2,1)S(1)}, bf16[1024,4096]{1,0:T(8,128)(2,1)S(1)}, f32[1024,2048]{1,0:T(8,128)S(1)}, f32[1,2048]{1,0:T(1,128)S(1)}...) custom-call(bf16[64,640]{1,0:T(8,128)(2,1)S(1)} %get-tuple-element.2, ...), custom_call_target="tpu_custom_call" | custom-call | flops 419430400 | bytes 819200 | tf_op jit(solution)/shard_map/pallas_call | solution.py:25
  17.7 0.0 collective-permute-done.refs_0_
  17.7 0.0 collective-permute-done.6.refs_3_
  17.7 0.0 collective-permute-done.4.refs_2_
  17.7 0.3 collective-permute-done.2.refs_1_
  18.0 0.0 collective-permute-start.7
  18.0 1.0 %shard_map.63 = (bf16[4096,1024]{1,0:T(8,128)(2,1)S(1)}, bf16[1024,4096]{1,0:T(8,128)(2,1)S(1)}, bf16[64,2048]{1,0:T(8,128)(2,1)S(1)}, f32[8,2048]{1,0:T(8,128)S(1)}) custom-call(bf16[64,640]{1,0:T(8,128)(2,1)S(1)} %collective-permute-done.refs_0_, bf16[64,640]{1,0:T(8,128)(2,1)S(1)} %collective-permute-done.2.refs_1_, ...), custom_call_target="tpu_custom_call", output_to_operand_aliasing={{0}: (5, {}), {1}: (6, {})} | custom-call | flops 419430400 | bytes 819200 | tf_op jit(solution)/shard_map/pallas_call | solution.py:25
  19.0 0.2 collective-permute-done.7.other_ref
  19.2 3.7 %shard_map.64 = (bf16[4096,1024]{1,0:T(8,128)(2,1)S(1)}, bf16[1024,4096]{1,0:T(8,128)(2,1)S(1)}, f32[1024,2048]{1,0:T(8,128)S(1)}, bf16[64,512]{1,0:T(8,128)(2,1...) custom-call(bf16[128,128]{1,0:T(8,128)(2,1)S(1)} %shard_map.60.mine_, ...), custom_call_target="tpu_custom_call", output_to_operand_aliasing={{0}: (8, {}), {1}: (9, {}), {2}: (10, {})} | custom-call | flops 1677721600 | bytes 3276800 | tf_op jit(solution)/shard_map/pallas_call | solution.py:25
  22.9 0.3 collective-permute-start.9
  23.2 0.8 %collective-permute-done.9.other_ref = f32[1,1024]{1,0:T(1,128)S(1)} collective-permute-done((f32[1,1024]{1,0:T(1,128)S(1)}, f32[1,1024]{1,0:T(1,128)S(1)}, u32[]{:S(2)}, u32[]{:S(2)}) %collective-permute-start.9) | collective-permute-done | bytes 4128 | tf_op jit(solution)/shard_map/ppermute | solution.py:325
  24.0 2.0 %shard_map.65.mine_ref = f32[1,1024]{1,0:T(1,128)S(1)} custom-call(f32[1,1024]{1,0:T(1,128)S(1)} %get-tuple-element.37.mine_ref, f32[1,1024]{1,0:T(1,128)S(1)} %collective-permute-done.9.other_ref, f32[1,512]{1,0:T(1,128)S(1)} %get-tuple-element.38.ce_ref, f32[1,512]{1,0:T(1,128)S(1)} %get-tuple-element.39.co_ref, ...), custom_call_target="tpu_custom_call" | custom-call | tf_op jit(solution)/shard_map/pallas_call | solution.py:25
  26.0 0.3 collective-permute-start.10
  26.4 0.8 %collective-permute-done.10.other_ref = f32[1,1024]{1,0:T(1,128)S(1)} collective-permute-done((f32[1,1024]{1,0:T(1,128)S(1)}, f32[1,1024]{1,0:T(1,128)S(1)}, u32[]{:S(2)}, u32[]{:S(2)}) %collective-permute-start.10) | collective-permute-done | bytes 4128 | tf_op jit(solution)/shard_map/ppermute | solution.py:325
  27.2 2.0 %shard_map.66.mine_ref = f32[1,1024]{1,0:T(1,128)S(1)} custom-call(f32[1,1024]{1,0:T(1,128)S(1)} %shard_map.65.mine_ref, f32[1,1024]{1,0:T(1,128)S(1)} %collective-permute-done.10.other_ref, f32[1,512]{1,0:T(1,128)S(1)} %get-tuple-element.38.ce_ref, f32[1,512]{1,0:T(1,128)S(1)} %get-tuple-element.39.co_ref, ...), custom_call_target="tpu_custom_call" | custom-call | tf_op jit(solution)/shard_map/pallas_call | solution.py:25
  29.2 0.3 collective-permute-start.11
  29.5 0.8 %collective-permute-done.11.other_ref = f32[1,1024]{1,0:T(1,128)S(1)} collective-permute-done((f32[1,1024]{1,0:T(1,128)S(1)}, f32[1,1024]{1,0:T(1,128)S(1)}, u32[]{:S(2)}, u32[]{:S(2)}) %collective-permute-start.11) | collective-permute-done | bytes 4128 | tf_op jit(solution)/shard_map/ppermute | solution.py:325
  30.4 2.3 %shard_map.67 = (f32[72,128]{1,0:T(8,128)S(1)}, f32[1,512]{1,0:T(1,128)S(1)}) custom-call(f32[1,1024]{1,0:T(1,128)S(1)} %shard_map.66.mine_ref, f32[1,1024]{1,0:T(1,128)S(1)} %collective-permute-done.11.other_ref, f32[1,512]{1,0:T(1,128)S(1)} %get-tuple-element.38.ce_ref, f32[1,512]{1,0:T(1,128)S(1)} %get-tuple-element.39.co_ref, ...), custom_call_target="tpu_custom_call" | custom-call | tf_op jit(solution)/shard_map/pallas_call | solution.py:25
  32.7 0.4 %collective-permute-start.12 = (f32[72,128]{1,0:T(8,128)S(1)}, f32[72,128]{1,0:T(8,128)S(1)}, u32[]{:S(2)}, u32[]{:S(2)}) collective-permute-start(f32[72,128]{1,0:T(8,128)S(1)} %get-tuple-element.43.mine_ref), channel_id=1, source_target_pairs={{0,1},{1,0},{2,3},{3,2},{4,5},{5,4},{6,7},{7,6},{8,9},{9,8},{10,11... | collective-permute-start | bytes 110600 | tf_op jit(solution)/shard_map/ppermute | solution.py:325
  33.1 0.9 %collective-permute-done.12.other_ref = f32[72,128]{1,0:T(8,128)S(1)} collective-permute-done((f32[72,128]{1,0:T(8,128)S(1)}, f32[72,128]{1,0:T(8,128)S(1)}, u32[]{:S(2)}, u32[]{:S(2)}) %collective-permute-start.12) | collective-permute-done | bytes 36896 | tf_op jit(solution)/shard_map/ppermute | solution.py:325
  34.0 1.0 %shard_map.68 = (f32[64,512]{1,0:T(8,128)}, f32[64,64]{1,0:T(8,128)}) custom-call(f32[72,128]{1,0:T(8,128)S(1)} %get-tuple-element.43.mine_ref, f32[72,128]{1,0:T(8,128)S(1)} %collective-permute-done.12.other_ref, f32[1,512]{1,0:T(1,128)S(1)} %get-tuple-element.38.ce_ref, f32[1,512]{1,0:T(1,128)S(1)} %get-tuple-element.39.co_ref, ...), custom_call_target="tpu_custom_call" | custom-call | tf_op jit(solution)/shard_map/pallas_call | solution.py:25
  (2 shorter events, 0.0 us)
Async XLA Ops:
  1.6 8.1 %collective-permute-start.5 = (bf16[64,640]{1,0:T(8,128)(2,1)S(1)}, bf16[64,640]{1,0:T(8,128)(2,1)S(1)}, u32[]{:S(2)}, u32[]{:S(2)}) collective-permute-start(bf16[64,640]{1,0:T(8,128)(2,1)S(1)} %get-tuple-element.24.refs_0_), channel_id=1, source_target_pairs={{0,8},{1,9},{2,10},{3,11},{4,12},{5,13},{6,14},{7,15},{8,0},{9,1},... | collective-permute-start | bytes 245768 | tf_op jit(solution)/shard_map/ppermute | solution.py:325
  5.7 6.2 %collective-permute-start.3 = (bf16[64,640]{1,0:T(8,128)(2,1)S(1)}, bf16[64,640]{1,0:T(8,128)(2,1)S(1)}, u32[]{:S(2)}, u32[]{:S(2)}) collective-permute-start(bf16[64,640]{1,0:T(8,128)(2,1)S(1)} %get-tuple-element.24.refs_0_), channel_id=1, source_target_pairs={{0,4},{1,5},{2,6},{3,7},{4,0},{5,1},{6,2},{7,3},{8,12},{9,13},{10,... | collective-permute-start | bytes 245768 | tf_op jit(solution)/shard_map/ppermute | solution.py:325
  7.3 6.2 %collective-permute-start.1 = (bf16[64,640]{1,0:T(8,128)(2,1)S(1)}, bf16[64,640]{1,0:T(8,128)(2,1)S(1)}, u32[]{:S(2)}, u32[]{:S(2)}) collective-permute-start(bf16[64,640]{1,0:T(8,128)(2,1)S(1)} %get-tuple-element.24.refs_0_), channel_id=1, source_target_pairs={{0,12},{1,13},{2,14},{3,15},{4,8},{5,9},{6,10},{7,11},{8,4},{9,5},... | collective-permute-start | bytes 245768 | tf_op jit(solution)/shard_map/ppermute | solution.py:325
  7.3 10.4 %collective-permute-start = (bf16[64,640]{1,0:T(8,128)(2,1)S(1)}, bf16[64,640]{1,0:T(8,128)(2,1)S(1)}, u32[]{:S(2)}, u32[]{:S(2)}) collective-permute-start(bf16[64,640]{1,0:T(8,128)(2,1)S(1)} %get-tuple-element.24.refs_0_), channel_id=1, source_target_pairs={{0,2},{1,3},{2,0},{3,1},{4,6},{5,7},{6,4},{7,5},{8,10},{9,11},{10,... | collective-permute-start | bytes 245768 | tf_op jit(solution)/shard_map/ppermute | solution.py:325
  9.7 8.0 %collective-permute-start.6 = (bf16[64,640]{1,0:T(8,128)(2,1)S(1)}, bf16[64,640]{1,0:T(8,128)(2,1)S(1)}, u32[]{:S(2)}, u32[]{:S(2)}) collective-permute-start(bf16[64,640]{1,0:T(8,128)(2,1)S(1)} %collective-permute-done.5.refs_3_), channel_id=1, source_target_pairs={{0,2},{1,3},{2,0},{3,1},{4,6},{5,7},{6,4},{7,5},{8,10},{9,11},{10,... | collective-permute-start | bytes 245768 | tf_op jit(solution)/shard_map/ppermute | solution.py:325
  11.9 5.8 %collective-permute-start.4 = (bf16[64,640]{1,0:T(8,128)(2,1)S(1)}, bf16[64,640]{1,0:T(8,128)(2,1)S(1)}, u32[]{:S(2)}, u32[]{:S(2)}) collective-permute-start(bf16[64,640]{1,0:T(8,128)(2,1)S(1)} %collective-permute-done.3.refs_2_), channel_id=1, source_target_pairs={{0,2},{1,3},{2,0},{3,1},{4,6},{5,7},{6,4},{7,5},{8,10},{9,11},{10,... | collective-permute-start | bytes 245768 | tf_op jit(solution)/shard_map/ppermute | solution.py:325
  13.5 4.4 %collective-permute-start.2 = (bf16[64,640]{1,0:T(8,128)(2,1)S(1)}, bf16[64,640]{1,0:T(8,128)(2,1)S(1)}, u32[]{:S(2)}, u32[]{:S(2)}) collective-permute-start(bf16[64,640]{1,0:T(8,128)(2,1)S(1)} %collective-permute-done.1.refs_1_), channel_id=1, source_target_pairs={{0,2},{1,3},{2,0},{3,1},{4,6},{5,7},{6,4},{7,5},{8,10},{9,11},{10,... | collective-permute-start | bytes 245768 | tf_op jit(solution)/shard_map/ppermute | solution.py:325
  15.1 1.2 %collective-permute-start.8 = (bf16[128,128]{1,0:T(8,128)(2,1)S(1)}, bf16[128,128]{1,0:T(8,128)(2,1)S(1)}, u32[]{:S(2)}, u32[]{:S(2)}) collective-permute-start(bf16[128,128]{1,0:T(8,128)(2,1)S(1)} %shard_map.61.refs_4_), channel_id=1, source_target_pairs={{0,1},{1,0},{2,3},{3,2},{4,5},{5,4},{6,7},{7,6},{8,9},{9,8},{10,11... | collective-permute-start | bytes 98312 | tf_op jit(solution)/shard_map/ppermute | solution.py:325
  18.0 1.2 %collective-permute-start.7 = (bf16[128,128]{1,0:T(8,128)(2,1)S(1)}, bf16[128,128]{1,0:T(8,128)(2,1)S(1)}, u32[]{:S(2)}, u32[]{:S(2)}) collective-permute-start(bf16[128,128]{1,0:T(8,128)(2,1)S(1)} %shard_map.60.mine_ref), channel_id=1, source_target_pairs={{0,1},{1,0},{2,3},{3,2},{4,5},{5,4},{6,7},{7,6},{8,9},{9,8},{10,11... | collective-permute-start | bytes 98312 | tf_op jit(solution)/shard_map/ppermute | solution.py:325
  22.9 1.2 %collective-permute-start.9 = (f32[1,1024]{1,0:T(1,128)S(1)}, f32[1,1024]{1,0:T(1,128)S(1)}, u32[]{:S(2)}, u32[]{:S(2)}) collective-permute-start(f32[1,1024]{1,0:T(1,128)S(1)} %get-tuple-element.37.mine_ref), channel_id=1, source_target_pairs={{0,1},{1,0},{2,3},{3,2},{4,5},{5,4},{6,7},{7,6},{8,9},{9,8},{10,11... | collective-permute-start | bytes 12296 | tf_op jit(solution)/shard_map/ppermute | solution.py:325
  26.0 1.2 %collective-permute-start.10 = (f32[1,1024]{1,0:T(1,128)S(1)}, f32[1,1024]{1,0:T(1,128)S(1)}, u32[]{:S(2)}, u32[]{:S(2)}) collective-permute-start(f32[1,1024]{1,0:T(1,128)S(1)} %shard_map.65.mine_ref), channel_id=1, source_target_pairs={{0,1},{1,0},{2,3},{3,2},{4,5},{5,4},{6,7},{7,6},{8,9},{9,8},{10,11... | collective-permute-start | bytes 12296 | tf_op jit(solution)/shard_map/ppermute | solution.py:325
  29.2 1.2 %collective-permute-start.11 = (f32[1,1024]{1,0:T(1,128)S(1)}, f32[1,1024]{1,0:T(1,128)S(1)}, u32[]{:S(2)}, u32[]{:S(2)}) collective-permute-start(f32[1,1024]{1,0:T(1,128)S(1)} %shard_map.66.mine_ref), channel_id=1, source_target_pairs={{0,1},{1,0},{2,3},{3,2},{4,5},{5,4},{6,7},{7,6},{8,9},{9,8},{10,11... | collective-permute-start | bytes 12296 | tf_op jit(solution)/shard_map/ppermute | solution.py:325
  32.7 1.3 %collective-permute-start.12 = (f32[72,128]{1,0:T(8,128)S(1)}, f32[72,128]{1,0:T(8,128)S(1)}, u32[]{:S(2)}, u32[]{:S(2)}) collective-permute-start(f32[72,128]{1,0:T(8,128)S(1)} %get-tuple-element.43.mine_ref), channel_id=1, source_target_pairs={{0,1},{1,0},{2,3},{3,2},{4,5},{5,4},{6,7},{7,6},{8,9},{9,8},{10,11... | collective-permute-start | bytes 110600 | tf_op jit(solution)/shard_map/ppermute | solution.py:325
